TPU v7x, 256 devices: a whole 4x4x8 slice. The times are simulated.
256 devices in a mesh: tm: 16 (over y_hi, z), sub: 16 (over x, y_lo, core).
Axes of the slice: x: 4, y: 4 (y_hi: 2, y_lo: 2; y = y_hi * 2 + y_lo), z: 8, core: 2. Of those that a mesh axis runs over, the one named last changes fastest.
Arguments:
- frames: bfloat16 [16384, 1024], P(('tm', 'sub')), may hold values from -16 to 16
- modulation: float32 [8, 1024], replicated, may hold values from -4 to 4
- w_project: bfloat16 [3, 1024, 1024], P(None, None, 'sub'), may hold values from -1 to 1
- w_heads_out: bfloat16 [1024, 1024], P('sub'), may hold values from -0.25 to 0.25
- w_up: bfloat16 [1024, 4096], P(None, 'sub'), may hold values from -0.1875 to 0.1875
- w_down: bfloat16 [4096, 1024], P('sub'), may hold values from -0.125 to 0.125
- w_velocity: bfloat16 [1024, 100], replicated, may hold values from -0.1875 to 0.1875
- noisy_mel: float32 [16384, 100], P('tm'), may hold values from -6 to 6
- w_prelude: bfloat16 [7, 1536, 100], P(None, 'sub'), may hold values from -0.21875 to 0.21875
- w_upsample: bfloat16 [8, 1536, 768], P(None, 'sub'), may hold values from -0.109375 to 0.109375
- snake_alpha: float32 [2, 768], replicated, may hold values from 0.3 to 3
- w_dilated: bfloat16 [3, 768, 768], P(None, 'sub'), may hold values from -0.125 to 0.125
- w_plain: bfloat16 [3, 768, 768], P(None, 'sub'), may hold values from -0.125 to 0.125
Outputs:
- mel_next: float32 [16384, 100], P('tm')
- section_out: bfloat16 [65536, 768], P(('tm', 'sub'))
All inputs are finite; a program needn't handle non-finite values.
Results may differ from a plain program's by a relative error of at most 0.03.
Values may be sent and summed in bfloat16 or wider, within the bound.
No kernel may reach another device: no remote copies, remote signals or barrier semaphores. Data moves between devices by JAX's collectives and lax.ppermute only.
A program may use at most 64 MiB of HBM per device.

v0:
```python
import math

import jax
import jax.numpy as jnp
from jax import lax
from jax.sharding import PartitionSpec as P

HEAD_DIM = 64
BLK = 256


epsilon = 1e-06


def from_behind(block, axis, distance):
    devices = range(lax.axis_size(axis))
    route = [(i - distance, i) for i in devices if i - distance in devices]
    return lax.ppermute(block, axis, route)


def extended_2(cells, sides, width):
    for axis, dim in sides:
        count = lax.axis_size(axis)
        ends = count - 1
        head = lax.slice_in_dim(cells, 0, width, axis=dim)
        tail = lax.slice_in_dim(cells, cells.shape[dim] - width, cells.shape[dim], axis=dim)
        cells = jnp.concatenate(
            [
                lax.ppermute(tail, axis, [(i, (i + 1) % count) for i in range(ends)]),
                cells,
                lax.ppermute(head, axis, [((i + 1) % count, i) for i in range(ends)]),
            ],
            axis=dim,
        )
    return cells


def norm_rows(rows, offset_row, scale_row):
    rows = rows.astype(jnp.float32)
    center = jnp.mean(rows, axis=-1, keepdims=True)
    square = jnp.mean(rows * rows, axis=-1, keepdims=True)
    spread = square - center * center
    return (rows - center) * lax.rsqrt(spread + epsilon) * (1.0 + scale_row) + offset_row


def snake_act(values, alpha_row):
    return values + jnp.square(jnp.sin(alpha_row * values)) / alpha_row


def contract_first(left, right):
    return lax.dot_general(
        left, right, (((0,), (0,)), ((), ())), preferred_element_type=jnp.float32
    )


def phase_terms(prelude_cols, tap_weights, first_frame, span):
    current = lax.dynamic_slice_in_dim(prelude_cols, 1, span, 1)
    earlier = lax.dynamic_slice_in_dim(prelude_cols, first_frame, span, 1)
    later_frames = lax.dynamic_slice_in_dim(prelude_cols, 2, span, 1)

    def tap_product(source, offset):
        return contract_first(source, tap_weights[offset])

    phases = jnp.stack(
        [
            tap_product(current, 2) + tap_product(earlier, 6),
            tap_product(current, 3) + tap_product(earlier, 7),
            tap_product(current, 4) + tap_product(later_frames, 0),
            tap_product(current, 5) + tap_product(later_frames, 1),
        ],
        1,
    )
    return phases.reshape((4 * span, phases.shape[2]))


def block_attention(queries, keys_now, values_now, lookback, is_first):
    frame_count = queries.shape[0]
    head_count = queries.shape[1] // HEAD_DIM
    blocks = frame_count // BLK
    block_shape = (blocks, BLK, head_count, HEAD_DIM)
    edge_shape = (1, BLK, head_count, HEAD_DIM)
    key_blocks = keys_now.reshape(block_shape)
    value_blocks = values_now.reshape(block_shape)
    key_all = jnp.concatenate(
        [jnp.concatenate([lookback[0].reshape(edge_shape), key_blocks[:-1]], 0), key_blocks], 1
    )
    value_all = jnp.concatenate(
        [jnp.concatenate([lookback[1].reshape(edge_shape), value_blocks[:-1]], 0), value_blocks], 1
    )
    scores = jnp.einsum(
        "bqhd,bkhd->bhqk", queries.reshape(block_shape), key_all, preferred_element_type=jnp.float32
    ) / math.sqrt(HEAD_DIM)
    block_ids = lax.broadcasted_iota(jnp.int32, (blocks, 1, 1, 2 * BLK), 0)
    key_ids = lax.broadcasted_iota(jnp.int32, (blocks, 1, 1, 2 * BLK), 3)
    allowed = (block_ids > 0) | (key_ids >= BLK) | jnp.logical_not(is_first)
    scores = jnp.where(allowed, scores, -1e30)
    largest = jnp.max(scores, axis=-1, keepdims=True)
    raised = jnp.exp(scores - largest)
    weights = (raised / jnp.sum(raised, axis=-1, keepdims=True)).astype(jnp.bfloat16)
    attended = jnp.einsum("bhqk,bkhd->bqhd", weights, value_all, preferred_element_type=jnp.float32)
    return attended.reshape((frame_count, head_count * HEAD_DIM)).astype(jnp.bfloat16)


def dilated_conv(extended, row_count, w_dilated):
    empty_sum = jnp.zeros((row_count, w_dilated.shape[2]), jnp.float32)
    running = empty_sum
    weight_rows = lax.all_gather(w_dilated, "sub", axis=1, tiled=True)
    for offset in range(3):
        running = running + jnp.dot(
            extended[3 * offset : 3 * offset + row_count],
            weight_rows[offset],
            preferred_element_type=jnp.float32,
        )
    return running


def plain_conv(extended, row_count, w_plain):
    empty_sum = jnp.zeros((row_count, w_plain.shape[2]), jnp.float32)
    running = empty_sum
    weight_rows = lax.all_gather(w_plain, "sub", axis=1, tiled=True)
    for offset in range(3):
        running = running + jnp.dot(
            extended[offset : offset + row_count],
            weight_rows[offset],
            preferred_element_type=jnp.float32,
        )
    return running


def body(
    frames,
    modulation,
    w_project,
    w_heads_out,
    w_up,
    w_down,
    w_velocity,
    noisy_mel,
    w_prelude,
    w_upsample,
    snake_alpha,
    w_dilated,
    w_plain,
):
    own_rows = frames.shape[0]
    sub_index = lax.axis_index("sub")
    time_index = lax.axis_index("tm")
    gathered = lax.all_gather(frames, "sub", axis=0, tiled=True)
    frame_count = gathered.shape[0]
    first_norm = norm_rows(gathered, modulation[0], modulation[1]).astype(jnp.bfloat16)
    projected = jnp.einsum(
        "td,kde->kte", first_norm, w_project, preferred_element_type=jnp.float32
    ).astype(jnp.bfloat16)
    lookback = from_behind(
        (projected[1, frame_count - BLK :], projected[2, frame_count - BLK :]), "tm", 1
    )
    heads_out = block_attention(projected[0], projected[1], projected[2], lookback, time_index == 0)
    attn = lax.psum_scatter(
        jnp.dot(heads_out, w_heads_out, preferred_element_type=jnp.float32).astype(jnp.bfloat16),
        "sub",
        scatter_dimension=0,
        tiled=True,
    ).astype(jnp.float32)
    mixed_rows = (frames.astype(jnp.float32) + modulation[2] * attn).astype(jnp.bfloat16)
    own_norm = norm_rows(mixed_rows, modulation[3], modulation[4]).astype(jnp.bfloat16)
    second_norm = lax.all_gather(own_norm, "sub", axis=0, tiled=True)
    hidden = jax.nn.gelu(
        jnp.dot(second_norm, w_up, preferred_element_type=jnp.float32), approximate=True
    ).astype(jnp.bfloat16)
    feed = lax.psum_scatter(
        jnp.dot(hidden, w_down, preferred_element_type=jnp.float32).astype(jnp.bfloat16),
        "sub",
        scatter_dimension=0,
        tiled=True,
    ).astype(jnp.float32)
    final_rows = (mixed_rows.astype(jnp.float32) + modulation[5] * feed).astype(jnp.bfloat16)
    final_norm = norm_rows(final_rows, modulation[6], modulation[7]).astype(jnp.bfloat16)
    velocity = jnp.dot(final_norm, w_velocity, preferred_element_type=jnp.float32)
    noisy_own = lax.dynamic_slice_in_dim(noisy_mel, sub_index * own_rows, own_rows, 0)
    mel_own = noisy_own + 0.5 * velocity
    mel_next = lax.all_gather(mel_own, "sub", axis=0, tiled=True)
    mel_low = mel_next.astype(jnp.bfloat16)
    mel_wide = extended_2(mel_low, (("tm", 0),), 4)
    columns = frame_count + 2
    prelude = jnp.zeros((w_prelude.shape[1], columns), jnp.float32)
    for offset in range(7):
        prelude = prelude + lax.dot_general(
            w_prelude[offset],
            mel_wide[offset : offset + columns],
            (((1,), (1,)), ((), ())),
            preferred_element_type=jnp.float32,
        )
    frame_pos = time_index * frame_count - 1 + lax.broadcasted_iota(jnp.int32, (1, columns), 1)
    inside = (frame_pos >= 0) & (frame_pos < lax.axis_size("tm") * frame_count)
    prelude = jnp.where(inside, prelude, 0.0).astype(jnp.bfloat16)
    samples_dev = 4 * own_rows
    up_x = lax.psum_scatter(
        phase_terms(
            prelude, w_upsample, jnp.int32(0) // 4, samples_dev * lax.axis_size("sub") // 4
        ).astype(jnp.bfloat16),
        "sub",
        scatter_dimension=0,
        tiled=True,
    )
    act_one = snake_act(up_x.astype(jnp.float32), snake_alpha[0]).astype(jnp.bfloat16)
    wide_one = extended_2(act_one, ((("tm", "sub"), 0),), 3)
    inner_conv = dilated_conv(wide_one, samples_dev, w_dilated)
    act_two = snake_act(inner_conv, snake_alpha[1]).astype(jnp.bfloat16)
    wide_two = extended_2(act_two, ((("tm", "sub"), 0),), 1)
    outer_conv = plain_conv(wide_two, samples_dev, w_plain)
    section_out = (up_x.astype(jnp.float32) + outer_conv).astype(jnp.bfloat16)
    return (mel_next, section_out)


def solution(mesh):
    in_specs = (
        P(("tm", "sub"), None),
        P(),
        P(None, None, "sub"),
        P("sub", None),
        P(None, "sub"),
        P("sub", None),
        P(),
        P("tm", None),
        P(None, "sub", None),
        P(None, "sub", None),
        P(),
        P(None, "sub", None),
        P(None, "sub", None),
    )
    out_specs = (P("tm", None), P(("tm", "sub"), None))
    return jax.shard_map(body, mesh=mesh, in_specs=in_specs, out_specs=out_specs, check_vma=False)
```

profile of v0, /device:TPU:1, one launch (start us, length us, event | category | flops | bytes accessed | tf_op | source)
XLA Modules:
  0.0 477.0 jit_solution(3565787769455806827)
XLA Ops:
  9.2 41.1 %all-gather.5.cloned.1.call-done = bf16[1024,1024]{1,0:T(8,128)(2,1)} async-done(((bf16[64,1024]{1,0:T(8,128)(2,1)}), bf16[1024,1024]{1,0:T(8,128)(2,1)}) %all-gather.5.cloned.1.call-update) | async-done | bytes 2097168 | tf_op jit(solution)/shard_map/all_gather | solution.py:148
  50.2 2.4 convert_reduce_fusion
  52.7 2.2 fusion.14
  55.0 3.2 collective-permute-start.1
  58.6 3.2 collective-permute-start
  61.8 2.2 fusion.181
  64.0 2.1 fusion.29
  66.3 2.1 convolution_convert_fusion.1
  68.5 64.6 %reduce-scatter.4.cloned.1.call-done = bf16[64,1024]{1,0:T(8,128)(2,1)} async-done(((bf16[1024,1024]{1,0:T(8,128)(2,1)}), bf16[64,1024]{1,0:T(8,128)(2,1)}) %reduce-scatter.4.cloned.1.call-update) | async-done | bytes 131088 | tf_op jit(solution)/shard_map/reduce_scatter | solution.py:158
  135.0 38.8 %all-gather.7.cloned.1.call-done = bf16[1024,1024]{1,0:T(8,128)(2,1)} async-done(((bf16[64,1024]{1,0:T(8,128)(2,1)}), bf16[1024,1024]{1,0:T(8,128)(2,1)}) %all-gather.7.cloned.1.call-update) | async-done | bytes 2097168 | tf_op jit(solution)/shard_map/all_gather | solution.py:166
  173.8 5.2 %convolution_convert_fusion = bf16[1024,1024]{1,0:T(8,128)(2,1)} fusion(bf16[256,1024]{1,0:T(8,128)(2,1)S(1)} %copy-done, bf16[1024,1024]{1,0:T(8,128)(2,1)} %all-gather.7.cloned.1.call-done, bf16[1024,256]{1,0:T(8,128)(2,1)S(1)} %copy-done.11), kind=kOutput, calls=%fused_computation.27 | convolution fusion | flops 1077149696 | bytes 5242880 | tf_op jit(solution)/shard_map/dot_general | solution.py:171
  180.1 62.5 %reduce-scatter.6.cloned.1.call-done = bf16[64,1024]{1,0:T(8,128)(2,1)} async-done(((bf16[1024,1024]{1,0:T(8,128)(2,1)}), bf16[64,1024]{1,0:T(8,128)(2,1)}) %reduce-scatter.6.cloned.1.call-update) | async-done | bytes 131088 | tf_op jit(solution)/shard_map/reduce_scatter | solution.py:170
  244.0 21.4 %all_gather.17 = f32[1024,100]{1,0:T(8,128)S(1)} all-gather(f32[64,100]{1,0:T(8,128)S(1)} %fusion.30), channel_id=1, replica_groups=mesh['tm'=16,'sub'=16] {'sub'}, dimensions={0}, use_global_device_ids=true | all-gather | bytes 435200 | tf_op jit(solution)/shard_map/all_gather | solution.py:181
  266.2 3.2 collective-permute-start.2
  269.5 1.5 collective-permute-start.3
  271.0 2.8 collective-permute-done.3
  283.4 7.5 %copy.33 = bf16[1024,4,768]{2,1,0:T(4,128)(2,1)} copy(bf16[1024,4,768]{2,0,1:T(8,128)(2,1)S(1)} %pad_maximum_fusion) | data formatting | bytes 12582912 | tf_op jit(solution)/shard_map/stack | solution.py:64
  290.9 10.7 %convert_element_type.111 = bf16[4096,768]{1,0:T(8,128)(2,1)} reshape(bf16[1024,4,768]{2,1,0:T(4,128)(2,1)} %copy.33) | data formatting | bytes 12582912 | tf_op jit(solution)/shard_map/convert_element_type | solution.py:200
  304.0 78.0 %reduce-scatter.8.cloned.1.call-done = bf16[256,768]{1,0:T(8,128)(2,1)} async-done(((bf16[4096,768]{1,0:T(8,128)(2,1)}), bf16[256,768]{1,0:T(8,128)(2,1)}) %reduce-scatter.8.cloned.1.call-update) | async-done | bytes 393232 | tf_op jit(solution)/shard_map/reduce_scatter | solution.py:197
  382.1 3.6 fusion.45
  385.7 1.9 collective-permute-start.5
  387.7 3.6 collective-permute-start.4
  391.3 32.0 %all-gather.9.cloned.1.call-done = bf16[3,768,768]{2,1,0:T(8,128)(2,1)} async-done(((bf16[3,48,768]{2,1,0:T(8,128)(2,1)}), bf16[3,768,768]{2,1,0:T(8,128)(2,1)}) %all-gather.9.cloned.1.call-update) | async-done | bytes 3538960 | tf_op jit(solution)/shard_map/all_gather | solution.py:107
  423.3 1.7 fusion.28
  425.0 1.8 fusion.27
  426.8 4.2 add_convert_fusion.4
  431.1 2.2 collective-permute-start.7
  433.3 3.5 collective-permute-start.6
  436.8 27.2 %all-gather.11.cloned.1.call-done = bf16[3,768,768]{2,1,0:T(8,128)(2,1)} async-done(((bf16[3,48,768]{2,1,0:T(8,128)(2,1)}), bf16[3,768,768]{2,1,0:T(8,128)(2,1)}) %all-gather.11.cloned.1.call-update) | async-done | bytes 3538960 | tf_op jit(solution)/shard_map/all_gather | solution.py:120
  464.0 1.7 fusion.26
  465.8 1.8 fusion.25
  467.6 2.5 fusion.24
  (99 shorter events, 19.8 us)
Async XLA Ops:
  7.2 166.6 %copy-start = (bf16[256,1024]{1,0:T(8,128)(2,1)S(1)}, bf16[256,1024]{1,0:T(8,128)(2,1)}, u32[]{:S(2)}) copy-start(bf16[256,1024]{1,0:T(8,128)(2,1)} %param.18) | copy-start | bytes 1572868
  7.2 43.1 %all-gather.5.cloned.1.call-start = ((), (), s32[]{:S(2)}) async-start(), calls=%async_computation.3 | async-start | bytes 2228224 | tf_op jit(solution)/shard_map/all_gather | solution.py:148
  7.9 125.2 %reduce-scatter.4.cloned.1.call-start = ((), (), s32[]{:S(2)}) async-start(), calls=%async_computation.4 | async-start | bytes 2228224 | tf_op jit(solution)/shard_map/reduce_scatter | solution.py:158
  50.2 2.4 copy-start.4
  55.0 6.8 %collective-permute-start.1 = (bf16[256,64]{0,1:T(8,128)(2,1)S(1)}, bf16[256,64]{0,1:T(8,128)(2,1)S(1)}, u32[]{:S(2)}, u32[]{:S(2)}) collective-permute-start(bf16[256,64]{0,1:T(8,128)(2,1)S(1)} %get-tuple-element.21), channel_id=1, source_target_pairs={{0,16},{16,32},{32,48},{48,64},{64,80},{80,96},{96,112},{112,128},... | collective-permute-start | bytes 98312 | tf_op jit(solution)/shard_map/ppermute | solution.py:18
  58.6 5.4 %collective-permute-start = (bf16[256,64]{0,1:T(8,128)(2,1)S(1)}, bf16[256,64]{0,1:T(8,128)(2,1)S(1)}, u32[]{:S(2)}, u32[]{:S(2)}) collective-permute-start(bf16[256,64]{0,1:T(8,128)(2,1)S(1)} %get-tuple-element.20), channel_id=1, source_target_pairs={{0,16},{16,32},{32,48},{48,64},{64,80},{80,96},{96,112},{112,128},... | collective-permute-start | bytes 98312 | tf_op jit(solution)/shard_map/ppermute | solution.py:18
  64.0 2.3 copy-start.9
  66.3 66.8 %copy-start.7 = (bf16[64,1024]{1,0:T(8,128)(2,1)S(1)}, bf16[64,1024]{1,0:T(8,128)(2,1)}, u32[]{:S(2)}) copy-start(bf16[64,1024]{1,0:T(8,128)(2,1)} %param.13) | copy-start | bytes 393220
  66.3 107.5 %copy-start.11 = (bf16[1024,256]{1,0:T(8,128)(2,1)S(1)}, bf16[1024,256]{1,0:T(8,128)(2,1)}, u32[]{:S(2)}) copy-start(bf16[1024,256]{1,0:T(8,128)(2,1)} %param.17) | copy-start | bytes 1572868
  68.4 105.4 %all-gather.7.cloned.1.call-start = ((), (), s32[]{:S(2)}) async-start(), calls=%async_computation.5 | async-start | bytes 2228224 | tf_op jit(solution)/shard_map/all_gather | solution.py:166
  135.0 107.7 %reduce-scatter.6.cloned.1.call-start = ((), (), s32[]{:S(2)}) async-start(), calls=%async_computation.6 | async-start | bytes 2228224 | tf_op jit(solution)/shard_map/reduce_scatter | solution.py:170
  179.0 64.7 %copy-start.12 = (bf16[1024,100]{0,1:T(8,128)(2,1)S(1)}, bf16[1024,100]{0,1:T(8,128)(2,1)}, u32[]{:S(2)}) copy-start(bf16[1024,100]{0,1:T(8,128)(2,1)} %param.19) | copy-start | bytes 614404
  179.0 95.5 %copy-start.8 = (bf16[7,96,100]{2,1,0:T(8,128)(2,1)S(1)}, bf16[7,96,100]{2,1,0:T(8,128)(2,1)}, u32[]{:S(2)}) copy-start(bf16[7,96,100]{2,1,0:T(8,128)(2,1)} %param.21) | copy-start | bytes 403204
  179.0 203.1 %reduce-scatter.8.cloned.1.call-start = ((), (), s32[]{:S(2)}) async-start(), calls=%async_computation.7 | async-start | bytes 6684672 | tf_op jit(solution)/shard_map/reduce_scatter | solution.py:197
  265.4 0.8 copy-start.2
  266.2 4.7 collective-permute-start.2
  269.5 4.3 collective-permute-start.3
  275.7 1.3 copy-start.6
  301.7 1.4 copy-start.10
  301.7 1.4 copy-start.3
  301.7 121.6 %all-gather.9.cloned.1.call-start = ((), (), s32[]{:S(2)}) async-start(), calls=%async_computation.8 | async-start | bytes 3760128 | tf_op jit(solution)/shard_map/all_gather | solution.py:107
  302.3 161.7 %all-gather.11.cloned.1.call-start = ((), (), s32[]{:S(2)}) async-start(), calls=%async_computation.9 | async-start | bytes 3760128 | tf_op jit(solution)/shard_map/all_gather | solution.py:120
  385.7 39.3 %collective-permute-start.5 = (bf16[3,768]{1,0:T(4,128)(2,1)S(1)}, bf16[3,768]{1,0:T(4,128)(2,1)S(1)}, u32[]{:S(2)}, u32[]{:S(2)}) collective-permute-start(bf16[3,768]{1,0:T(4,128)(2,1)S(1)} %get-tuple-element.19), channel_id=1, source_target_pairs={{1,0},{2,1},{3,2},{4,3},{5,4},{6,5},{7,6},{8,7},{9,8},{10,9},{11,1... | collective-permute-start | bytes 13832 | tf_op jit(solution)/shard_map/ppermute | solution.py:31
  387.7 39.1 %collective-permute-start.4 = (bf16[3,768]{1,0:T(4,128)(2,1)S(1)}, bf16[3,768]{1,0:T(4,128)(2,1)S(1)}, u32[]{:S(2)}, u32[]{:S(2)}) collective-permute-start(bf16[3,768]{1,0:T(4,128)(2,1)S(1)} %get-tuple-element.18), channel_id=1, source_target_pairs={{0,1},{1,2},{2,3},{3,4},{4,5},{5,6},{6,7},{7,8},{8,9},{9,10},{10,1... | collective-permute-start | bytes 13832 | tf_op jit(solution)/shard_map/ppermute | solution.py:29
  431.1 34.7 %collective-permute-start.7 = (bf16[1,768]{1,0:T(2,128)(2,1)S(1)}, bf16[1,768]{1,0:T(2,128)(2,1)S(1)}, u32[]{:S(2)}, u32[]{:S(2)}) collective-permute-start(bf16[1,768]{1,0:T(2,128)(2,1)S(1)} %get-tuple-element.17), channel_id=1, source_target_pairs={{1,0},{2,1},{3,2},{4,3},{5,4},{6,5},{7,6},{8,7},{9,8},{10,9},{11,1... | collective-permute-start | bytes 4616 | tf_op jit(solution)/shard_map/ppermute | solution.py:31
  433.3 34.3 %copy-start.5 = (bf16[256,768]{1,0:T(8,128)(2,1)S(1)}, bf16[256,768]{1,0:T(8,128)(2,1)}, u32[]{:S(2)}) copy-start(bf16[256,768]{1,0:T(8,128)(2,1)} %reduce-scatter.8.cloned.1.call-done) | copy-start | bytes 1179652
  433.3 34.3 %collective-permute-start.6 = (bf16[1,768]{1,0:T(2,128)(2,1)S(1)}, bf16[1,768]{1,0:T(2,128)(2,1)S(1)}, u32[]{:S(2)}, u32[]{:S(2)}) collective-permute-start(bf16[1,768]{1,0:T(2,128)(2,1)S(1)} %get-tuple-element.16), channel_id=1, source_target_pairs={{0,1},{1,2},{2,3},{3,4},{4,5},{5,6},{6,7},{7,8},{8,9},{9,10},{10,1... | collective-permute-start | bytes 4616 | tf_op jit(solution)/shard_map/ppermute | solution.py:29
  465.8 4.4 copy-start.1
Sparse Core Ops, SparseCore 0:
  9.8 40.3 all-gather.4
  68.5 64.4 reduce-scatter.3
  135.5 38.2 all-gather.6
  179.1 63.4 reduce-scatter.5
  301.8 80.2 reduce-scatter.7
  383.7 39.4 all-gather.8
  425.1 38.8 all-gather.10
where the time goes:
time: 478 us; the launch traced here: 477 us
  waiting for transfers between devices  349 us (73%)
  matrix products  35.1 us (7%)
  local copies, waits for them, and re-layouts  23.1 us (5%)
  starting transfers between devices  22.8 us (5%)
  blocking collectives  21.4 us (4%)
  between operations  14.7 us (3%)
  other arithmetic  11.1 us (2%)
    reduce_scatter x1, waiting for transfers between devices, body(): lax.psum_scatter(phase_terms(prelude, w_upsample, jnp.int32(0) // 4, samp...  78 us
    reduce_scatter x1, waiting for transfers between devices, body(): lax.psum_scatter(jnp.dot(heads_out, w_heads_out, preferred_element_type=j...  64.6 us
    reduce_scatter x1, waiting for transfers between devices, body(): lax.psum_scatter(jnp.dot(hidden, w_down, preferred_element_type=jnp.float...  62.5 us
    all_gather x1, waiting for transfers between devices, body(): gathered = lax.all_gather(frames, 'sub', axis=0, tiled=True)  41.1 us
    all_gather x1, waiting for transfers between devices, body(): second_norm = lax.all_gather(own_norm, 'sub', axis=0, tiled=True)  38.8 us
    all_gather x1, waiting for transfers between devices, dilated_conv(): weight_rows = lax.all_gather(w_dilated, 'sub', axis=1, tiled=True)  32 us
    all_gather x1, waiting for transfers between devices, plain_conv(): weight_rows = lax.all_gather(w_plain, 'sub', axis=1, tiled=True)  27.2 us
    all_gather x1, blocking collectives, body(): mel_next = lax.all_gather(mel_own, 'sub', axis=0, tiled=True)  21.4 us
  transfers between devices with their start and end apart: 15, of which 8 were waited for; matrix products, arithmetic and copies ran while one was open for 4% of the time, Pallas kernels for 0%

commit v1 on v0

v1 whole, which is shorter than its diff:
```python
import math

import jax
import jax.numpy as jnp
from jax import lax
from jax.experimental import pallas as pl
from jax.experimental.pallas import tpu as pltpu
from jax.sharding import PartitionSpec as P

HEAD_DIM = 64
BLK = 256
MEL_PAD = 128
OFFSETS = 9
HALO = 8

epsilon = 1e-06
bf16 = jnp.bfloat16
f32 = jnp.float32

X_GROUPS = [[4 * x + j for x in range(4)] for j in range(4)]
J_GROUPS = [[4 * x + j for j in range(4)] for x in range(4)]


def norm_rows(rows, offset_row, scale_row):
    rows = rows.astype(f32)
    center = jnp.mean(rows, axis=-1, keepdims=True)
    square = jnp.mean(rows * rows, axis=-1, keepdims=True)
    spread = square - center * center
    return (rows - center) * lax.rsqrt(spread + epsilon) * (1.0 + scale_row) + offset_row


def mm(a, b):
    return jnp.dot(a, b, preferred_element_type=f32)


def mm_t(a, b):
    return lax.dot_general(a, b, (((1,), (1,)), ((), ())), preferred_element_type=f32)


def vmem_specs(n):
    return [pl.BlockSpec(memory_space=pltpu.VMEM)] * n


def attention_kernel(flag_ref, own_ref, back_ref, w_ref, out_ref, heads, w_out):
    first = flag_ref[0] > 0
    for h in range(4):
        c = 256 * h
        k = own_ref[:, c : c + 64]
        v = own_ref[:, c + 64 : c + 128]
        q = own_ref[:, c + 128 : c + 192]
        kb = back_ref[:, 128 * h : 128 * h + 64]
        vb = back_ref[:, 128 * h + 64 : 128 * h + 128]
        scale = 1.0 / math.sqrt(HEAD_DIM)
        s_own = mm_t(q, k) * scale
        s_back = mm_t(q, kb) * scale
        s_back = jnp.where(first, -1e30, s_back)
        top = jnp.maximum(
            jnp.max(s_own, axis=-1, keepdims=True), jnp.max(s_back, axis=-1, keepdims=True)
        )
        e_own = jnp.exp(s_own - top)
        e_back = jnp.exp(s_back - top)
        total = jnp.sum(e_own, axis=-1, keepdims=True) + jnp.sum(e_back, axis=-1, keepdims=True)
        inv = 1.0 / total
        p_own = (e_own * inv).astype(bf16)
        p_back = (e_back * inv).astype(bf16)
        heads[:, 64 * h : 64 * h + 64] = (mm(p_own, v) + mm(p_back, vb)).astype(bf16)
        w_out[64 * h : 64 * h + 64, :] = w_ref[c + 192 : c + 256, :]
    out_ref[...] = mm(heads[...], w_out[...]).astype(bf16)


def attention(flag, own, back, weights):
    return pl.pallas_call(
        attention_kernel,
        out_shape=jax.ShapeDtypeStruct((BLK, 1024), bf16),
        in_specs=[pl.BlockSpec(memory_space=pltpu.SMEM)] + vmem_specs(3),
        out_specs=pl.BlockSpec(memory_space=pltpu.VMEM),
        scratch_shapes=[pltpu.VMEM((BLK, 256), bf16), pltpu.VMEM((256, 1024), bf16)],
        compiler_params=pltpu.CompilerParams(vmem_limit_bytes=24 << 20),
        cost_estimate=pl.CostEstimate(
            flops=5 * 10**8, bytes_accessed=3 << 20, transcendentals=1 << 19
        ),
        name="attention",
    )(flag, own, back, weights)


def mlp_kernel(h_ref, w0, w1, w2, w3, out_ref, acc):
    h = h_ref[...]
    for i, w in enumerate((w0, w1, w2, w3)):
        up = mm(h, w[0:1024, :])
        hid = jax.nn.gelu(up, approximate=True).astype(bf16)
        for k in range(4):
            part = mm(hid, w[1024 + 256 * k : 1280 + 256 * k, :])
            cols = slice(256 * k, 256 * k + 256)
            if i == 0:
                acc[:, cols] = part
            elif i < 3:
                acc[:, cols] += part
            else:
                out_ref[:, cols] = (acc[:, cols] + part).astype(bf16)


def mlp(h, weights):
    return pl.pallas_call(
        mlp_kernel,
        out_shape=jax.ShapeDtypeStruct((256, 1024), bf16),
        in_specs=vmem_specs(5),
        out_specs=pl.BlockSpec(memory_space=pltpu.VMEM),
        scratch_shapes=[pltpu.VMEM((256, 1024), f32)],
        compiler_params=pltpu.CompilerParams(vmem_limit_bytes=24 << 20),
        cost_estimate=pl.CostEstimate(
            flops=11 * 10**8, bytes_accessed=5 << 20, transcendentals=1 << 18
        ),
        name="mlp",
    )(h, *weights)


def snake_act(values, alpha_row):
    return values + jnp.square(jnp.sin(alpha_row * values)) / alpha_row


def shifted(plane, by):
    return pltpu.roll(plane, by % plane.shape[0], 0)


ROWS = 72


def conv_kernel(flag_ref, up_ref, alpha_ref, w_hbm, out_ref, wa, wb, planes, sem):
    copies = []
    for which, (buf, base) in enumerate(((wa, 96), (wb, 240))):
        mine = []
        for s in range(16):
            for tap in range(3):
                mine.append(
                    pltpu.make_async_copy(
                        w_hbm.at[s, pl.ds(base + 48 * tap, 48), :],
                        buf.at[tap, pl.ds(48 * s, 48), :],
                        sem.at[which],
                    )
                )
        copies.append(mine)
    for mine in copies:
        for c in mine:
            c.start()
    first = flag_ref[0] > 0
    last = flag_ref[1] > 0
    row = lax.broadcasted_iota(jnp.int32, (ROWS, 768), 0)
    outside = (first & (row == 0)) | (last & (row == 65))
    for s in range(16):
        block = up_ref[s]
        for p in range(4):
            planes[p, :, 48 * s : 48 * s + 48] = block[:, 48 * p : 48 * p + 48]
    a1 = alpha_ref[0:1, :]
    a2 = alpha_ref[1:2, :]
    ups = []
    acts = []
    for p in range(4):
        u = jnp.where(outside, 0.0, planes[p].astype(f32))
        ups.append(u)
        acts.append(snake_act(u, a1).astype(bf16))
    act = jnp.concatenate(acts, axis=0)
    for c in copies[0]:
        c.wait()
    y = [mm(act, wa[tap]) for tap in range(3)]
    y = [[v[ROWS * p : ROWS * p + ROWS] for p in range(4)] for v in y]
    acts = []
    for p in range(4):
        before = y[0][0] if p == 3 else shifted(y[0][p + 1], 1)
        after = y[2][3] if p == 0 else shifted(y[2][p - 1], -1)
        inner = before + y[1][p] + after
        acts.append(jnp.where(outside, 0.0, snake_act(inner, a2)).astype(bf16))
    act = jnp.concatenate(acts, axis=0)
    for c in copies[1]:
        c.wait()
    y = [mm(act, wb[tap]) for tap in range(3)]
    y = [[v[ROWS * p : ROWS * p + ROWS] for p in range(4)] for v in y]
    for p in range(4):
        before = y[0][p - 1] if p >= 1 else shifted(y[0][3], 1)
        after = y[2][p + 1] if p <= 2 else shifted(y[2][0], -1)
        total = ups[p] + (before + y[1][p] + after)
        out_ref[:, 768 * p : 768 * p + 768] = shifted(total, -1)[0:64].astype(bf16)


def convolutions(flags, up, alpha, weights):
    return pl.pallas_call(
        conv_kernel,
        out_shape=jax.ShapeDtypeStruct((64, 3072), bf16),
        in_specs=[pl.BlockSpec(memory_space=pltpu.SMEM)]
        + vmem_specs(2)
        + [pl.BlockSpec(memory_space=pl.ANY)],
        out_specs=pl.BlockSpec(memory_space=pltpu.VMEM),
        scratch_shapes=[
            pltpu.VMEM((3, 768, 768), bf16),
            pltpu.VMEM((3, 768, 768), bf16),
            pltpu.VMEM((4, ROWS, 768), bf16),
            pltpu.SemaphoreType.DMA((2,)),
        ],
        compiler_params=pltpu.CompilerParams(vmem_limit_bytes=40 << 20),
        cost_estimate=pl.CostEstimate(
            flops=2 * 10**9, bytes_accessed=8 << 20, transcendentals=1 << 19
        ),
        name="convolutions",
    )(flags, up, alpha, weights)


def body(
    frames,
    modulation,
    w_project,
    w_heads_out,
    w_up,
    w_down,
    w_velocity,
    noisy_mel,
    w_prelude,
    w_upsample,
    snake_alpha,
    w_dilated,
    w_plain,
):
    own_rows = frames.shape[0]
    sub_index = lax.axis_index("sub")
    time_index = lax.axis_index("tm")
    n_sub = lax.axis_size("sub")
    n_tm = lax.axis_size("tm")
    n_all = n_sub * n_tm
    both = ("tm", "sub")

    w_t = jnp.swapaxes(w_project, 1, 2)
    w_att = jnp.concatenate([w_t[1], w_t[2], w_t[0], w_heads_out], axis=0)
    w_att = lax.all_gather(w_att, "sub", axis=0, tiled=True, axis_index_groups=X_GROUPS)

    pre = jnp.transpose(w_prelude, (1, 0, 2)).reshape(96, 700)
    pre = jnp.pad(pre, ((0, 0), (0, 68)))
    w_voc = jnp.concatenate([pre, w_dilated.reshape(144, 768), w_plain.reshape(144, 768)], axis=0)
    w_voc, _ = lax.optimization_barrier((w_voc, w_att))
    w_voc = lax.all_gather(w_voc, "sub", axis=0, tiled=False)

    own_w = jnp.concatenate([w_up] + [w_down[:, 256 * k : 256 * k + 256] for k in range(4)], axis=0)
    other_core = lax.ppermute(own_w, "sub", [(i, i ^ 1) for i in range(16)])
    other_y = lax.ppermute(own_w, "sub", [(i, i ^ 2) for i in range(16)])
    other_both = lax.ppermute(other_y, "sub", [(i, i ^ 1) for i in range(16)])

    block = lax.all_gather(frames, "sub", axis=0, tiled=True, axis_index_groups=J_GROUPS)

    order = [2, 3, 4, 5, 6, 7, 0, 1]
    ups = jnp.stack([w_upsample[t] for t in order], axis=1)
    ups = ups.reshape(96, 8, 16, 48).transpose(2, 0, 1, 3).reshape(16 * 96, 384)
    ups = lax.all_to_all(ups, "sub", 0, 0, tiled=True)

    first_norm = norm_rows(block, modulation[0], modulation[1]).astype(bf16)
    projected = mm_t(first_norm, w_att).astype(bf16)
    kv = projected.reshape(256, 4, 256)[:, :, :128].reshape(256, 512)
    back = lax.ppermute(kv, both, [(i, i + 4) for i in range(n_all - 4)])
    is_first = (time_index == 0) & (sub_index < 4)
    partial = attention(is_first.astype(jnp.int32).reshape(1), projected, back, w_att)
    parts = lax.all_to_all(partial, "sub", 0, 0, tiled=True, axis_index_groups=J_GROUPS)
    attn = jnp.sum(parts.reshape(4, own_rows, 1024).astype(f32), axis=0)
    mixed_rows = (frames.astype(f32) + modulation[2] * attn).astype(bf16)
    own_norm = norm_rows(mixed_rows, modulation[3], modulation[4]).astype(bf16)

    second = lax.all_gather(own_norm, "sub", axis=0, tiled=True, axis_index_groups=X_GROUPS)
    partial = mlp(second, (own_w, other_core, other_y, other_both))
    parts = lax.all_to_all(partial, "sub", 0, 0, tiled=True, axis_index_groups=X_GROUPS)
    feed = jnp.sum(parts.reshape(4, own_rows, 1024).astype(f32), axis=0)
    final_rows = (mixed_rows.astype(f32) + modulation[5] * feed).astype(bf16)
    final_norm = norm_rows(final_rows, modulation[6], modulation[7]).astype(bf16)
    velocity = mm(final_norm, w_velocity)
    noisy_own = lax.dynamic_slice_in_dim(noisy_mel, sub_index * own_rows, own_rows, 0)
    mel_own = noisy_own + 0.5 * velocity
    copies = jnp.broadcast_to(mel_own[None], (n_sub,) + mel_own.shape)
    mel_next = lax.all_to_all(copies, "sub", 0, 0).reshape(-1, mel_own.shape[1])

    pre_all = w_voc[:, :96, :].reshape(1536, 768)
    comp = lax.dot_general(pre_all, ups, (((0,), (0,)), ((), ())), preferred_element_type=f32)
    comp = jnp.pad(comp[:700].reshape(7, 100, 384), ((0, 0), (0, MEL_PAD - 100), (0, 0)))
    here, near = comp[:, :, :192], comp[:, :, 192:]
    earlier = lax.broadcasted_iota(jnp.int32, (1, 1, 192), 2) < 96

    def placed(values, start):
        return jnp.pad(values, ((start, OFFSETS - 7 - start), (0, 0), (0, 0)))

    w_here = placed(here, 1)
    w_full = w_here + jnp.where(earlier, placed(near, 0), placed(near, 2))
    w_here = w_here.astype(bf16).reshape(OFFSETS * MEL_PAD, 192)
    w_full = w_full.astype(bf16).reshape(OFFSETS * MEL_PAD, 192)

    mel_low = jnp.pad(mel_next.astype(bf16), ((0, 0), (0, MEL_PAD - 100)))
    count = mel_low.shape[0]
    before = lax.ppermute(mel_low[count - HALO :], "tm", [(i, i + 1) for i in range(n_tm - 1)])
    after = lax.ppermute(mel_low[:HALO], "tm", [(i + 1, i) for i in range(n_tm - 1)])
    mel_ext = jnp.concatenate([before, mel_low, after], axis=0)
    span = count + 2
    cols = jnp.concatenate([mel_ext[3 + k : 3 + k + span] for k in range(OFFSETS)], axis=1)
    up = mm(cols, w_full)
    edge_cols = jnp.concatenate([cols[1:2], cols[count : count + 1]], axis=0)
    edge = mm(edge_cols, w_here)
    row = lax.broadcasted_iota(jnp.int32, (span, 1), 0)
    at_start = (time_index == 0) & (row == 1) & earlier[0]
    at_end = (time_index == n_tm - 1) & (row == count) & jnp.logical_not(earlier[0])
    up = jnp.where(at_start, edge[0:1], jnp.where(at_end, edge[1:2], up)).astype(bf16)
    windows = jnp.stack([up[64 * s : 64 * s + 66] for s in range(16)], axis=0)
    windows = jnp.pad(windows, ((0, 0), (0, ROWS - 66), (0, 0)))
    up_x = lax.all_to_all(windows, "sub", 0, 0, tiled=True)

    here_index = time_index * n_sub + sub_index
    flags = jnp.stack([here_index == 0, here_index == n_all - 1]).astype(jnp.int32)
    out = convolutions(flags, up_x, snake_alpha, w_voc)
    return (mel_next, out.reshape(256, 768))


def solution(mesh):
    in_specs = (
        P(("tm", "sub"), None),
        P(),
        P(None, None, "sub"),
        P("sub", None),
        P(None, "sub"),
        P("sub", None),
        P(),
        P("tm", None),
        P(None, "sub", None),
        P(None, "sub", None),
        P(),
        P(None, "sub", None),
        P(None, "sub", None),
    )
    out_specs = (P("tm", None), P(("tm", "sub"), None))
    return jax.shard_map(body, mesh=mesh, in_specs=in_specs, out_specs=out_specs, check_vma=False)
```

time: 478 us -> 252 us (0.53)
  waiting for transfers between devices: 349 us -> 85.3 us
  blocking collectives: 21.4 us -> 51.3 us
  matrix products: 35.1 us -> 5.54 us
  Pallas kernels: 0 us -> 26.2 us
  starting transfers between devices: 22.8 us -> 31.9 us
  local copies, waits for them, and re-layouts: 23.1 us -> 30.3 us
  other arithmetic: 11.1 us -> 5.59 us
    reduce_scatter x3 -> x0, waiting for transfers between devices: 205 us -> none  [the longest x1 78 us: body(): lax.psum_scatter(phase_terms(prelude, w_upsample, jnp.int32(0) // 4, samp...]
    all_gather x4 -> x2, waiting for transfers between devices: 139 us -> 35.9 us  [the longest x1 35.9 us: body(): lax.all_gather(w_att, 'sub', axis=0, tiled=True, axis_index_groups=X_GROUPS)]
    all_to_all x0 -> x5, waiting for transfers between devices: none -> 35.5 us  [the longest x1 9.23 us: body(): up_x = lax.all_to_all(windows, 'sub', 0, 0, tiled=True)]
    all_gather x1 -> x2, blocking collectives: 21.4 us -> 51.3 us  [the longest x1 41.4 us: body(): lax.all_gather(frames, 'sub', axis=0, tiled=True, axis_index_groups=J_GRO...]
    pallas_call x0 -> x3, Pallas kernels: none -> 26.2 us  [the longest x1 19.1 us: convolutions(): pl.pallas_call(conv_kernel, out_shape=jax.ShapeDtypeStruct((64, 3072), bf...]
    all_to_all x0 -> x5, starting transfers between devices: none -> 26.1 us  [the longest x1 8.78 us: body(): mel_next = lax.all_to_all(copies, 'sub', 0, 0).reshape(-1, mel_own.shape[1])]
    dot_general x25 -> x5, matrix products: 30.8 us -> 5.54 us  [the longest x1 3.07 us: body(): lax.dot_general(pre_all, ups, (((0,), (0,)), ((), ())), preferred_element...]
    ppermute x8 -> x6, starting transfers between devices: 22.3 us -> 5.65 us  [the longest x1 1.47 us: body(): lax.ppermute(mel_low[:HALO], 'tm', [(i + 1, i) for i in range(n_tm - 1)])]
  transfers between devices with their start and end apart: 15 -> 13, of which waited for: 8 -> 8; matrix products, arithmetic and copies ran while one was open for 4% -> 9% of each run, Pallas kernels for 0% -> 3%
where the time goes in v1:
time: 252 us; the launch traced here: 251 us
  waiting for transfers between devices  85.3 us (34%)
  blocking collectives  51.3 us (20%)
  starting transfers between devices  31.9 us (13%)
  local copies, waits for them, and re-layouts  30.3 us (12%)
  Pallas kernels  26.2 us (10%)
  between operations  14.7 us (6%)
  other arithmetic  5.59 us (2%)
  matrix products  5.54 us (2%)
    all_gather x1, blocking collectives, body(): lax.all_gather(frames, 'sub', axis=0, tiled=True, axis_index_groups=J_GRO...  41.4 us
    all_gather x1, waiting for transfers between devices, body(): lax.all_gather(w_att, 'sub', axis=0, tiled=True, axis_index_groups=X_GROUPS)  35.9 us
    pallas_call x1, Pallas kernels, convolutions(): pl.pallas_call(conv_kernel, out_shape=jax.ShapeDtypeStruct((64, 3072), bf...  19.1 us
    unnamed x79, local copies, waits for them, and re-layouts  17.1 us
    ppermute x1, waiting for transfers between devices, body(): back = lax.ppermute(kv, both, [(i, i + 4) for i in range(n_all - 4)])  11.2 us
    all_gather x1, blocking collectives, body(): lax.all_gather(own_norm, 'sub', axis=0, tiled=True, axis_index_groups=X_G...  9.9 us
    all_to_all x1, waiting for transfers between devices, body(): up_x = lax.all_to_all(windows, 'sub', 0, 0, tiled=True)  9.23 us
    all_to_all x1, waiting for transfers between devices, body(): ups = lax.all_to_all(ups, 'sub', 0, 0, tiled=True)  9.13 us
  transfers between devices with their start and end apart: 13, of which 8 were waited for; matrix products, arithmetic and copies ran while one was open for 9% of the time, Pallas kernels for 3%

profile of v1, /device:TPU:1, one launch (start us, length us, event | category | flops | bytes accessed | tf_op | source)
XLA Modules:
  0.0 250.9 jit_solution(11052161283990213973)
XLA Ops:
  8.4 1.7 pad_maximum_fusion
  11.4 35.9 %all-gather.4.cloned.1.call-done.w_ref = bf16[1024,1024]{1,0:T(8,128)(2,1)} async-done(((bf16[256,1024]{1,0:T(8,128)(2,1)}), bf16[1024,1024]{1,0:T(8,128)(2,1)}) %all-gather.4.cloned.1.call-update) | async-done | bytes 2097168 | tf_op jit(solution)/shard_map/all_gather | solution.py:231
  47.5 1.3 collective-permute-start.2
  48.8 41.4 %all_gather.15 = bf16[256,1024]{1,0:T(8,128)(2,1)S(1)} all-gather(bf16[64,1024]{1,0:T(8,128)(2,1)S(1)} %copy-done.13), channel_id=1, replica_groups={{0,1,2,3},{4,5,6,7},{8,9,10,11},{12,13,14,15},{16,17,18,19},{20,21,22,2..., dimensions={0}, use_global_device_ids=true | all-gather | bytes 655360 | tf_op jit(solution)/shard_map/all_gather | solution.py:244
  94.3 1.3 collective-permute-start
  95.8 11.2 %collective-permute-done.back_ref = bf16[256,512]{1,0:T(8,128)(2,1)S(1)} collective-permute-done((bf16[256,512]{1,0:T(8,128)(2,1)}, bf16[256,512]{1,0:T(8,128)(2,1)S(1)}, u32[]{:S(2)}, u32[]{:S(2)}) %collective-permute-start) | collective-permute-done | bytes 262176 | tf_op jit(solution)/shard_map/ppermute | solution.py:254
  107.1 1.6 copy-done.3
  108.7 3.2 %attention.1 = bf16[256,1024]{1,0:T(8,128)(2,1)} custom-call(s32[1]{0:T(128)} %bitcast.1.flag_ref, bf16[256,1024]{1,0:T(8,128)(2,1)S(1)} %convolution_convert_fusion.own_ref, bf16[256,512]{1,0:T(8,128)(2,1)S(1)} %collective-permute-done.back_ref, bf16[1024,1024]{1,0:T(8,128)(2,1)S(1)} %copy-done.3), custom_call_target="tpu_custom_call" | custom-call | flops 500000000 | bytes 3145728 | tf_op jit(solution)/shard_map/attention/pallas_call | solution.py:72
  111.9 4.7 %all-to-all-start = ((bf16[4,64,1024]{2,1,0:T(8,128)(2,1)}), bf16[4,64,1024]{2,1,0:T(8,128)(2,1)S(1)}, u32[]{:S(2)}, u32[]{:S(2)}) async-start(bf16[4,64,1024]{2,1,0:T(8,128)(2,1)} %bitcast.8), calls=%async_computation | async-start | bytes 1048576 | tf_op jit(solution)/shard_map/all_to_all | solution.py:257
  116.6 2.3 fusion.63
  121.6 9.0 %all-to-all-done = bf16[4,64,1024]{2,1,0:T(8,128)(2,1)S(1)} async-done(((bf16[4,64,1024]{2,1,0:T(8,128)(2,1)}), bf16[4,64,1024]{2,1,0:T(8,128)(2,1)S(1)}, u32[]{:S(2)}, u32[]{:S(2)}) %all-to-all-start) | async-done | bytes 524320 | tf_op jit(solution)/shard_map/all_to_all | solution.py:257
  131.9 9.9 %all_gather.17.h_ref = bf16[256,1024]{1,0:T(8,128)(2,1)S(1)} all-gather(bf16[64,1024]{1,0:T(8,128)(2,1)S(1)} %fusion.45), channel_id=1, replica_groups={{0,4,8,12},{1,5,9,13},{2,6,10,14},{3,7,11,15},{16,20,24,28},{17,21,25,2..., dimensions={0}, use_global_device_ids=true | all-gather | bytes 655360 | tf_op jit(solution)/shard_map/all_gather | solution.py:262
  141.8 4.0 %mlp.1 = bf16[256,1024]{1,0:T(8,128)(2,1)} custom-call(bf16[256,1024]{1,0:T(8,128)(2,1)S(1)} %all_gather.17.h_ref, bf16[2048,256]{1,0:T(8,128)(2,1)S(1)} %slice_dynamic-update-slice_fusion.w0, bf16[2048,256]{1,0:T(8,128)(2,1)} %collective-permute-done.1.w1, bf16[2048,256]{1,0:T(8,128)(2,1)S(1)} %collective-permute-done.2.w2, ...), custom_call_target="tpu_custom_call" | custom-call | flops 1100000000 | bytes 5242880 | tf_op jit(solution)/shard_map/mlp/pallas_call | solution.py:103
  145.8 3.6 %all-to-all-start.1 = ((bf16[4,64,1024]{2,1,0:T(8,128)(2,1)}), bf16[4,64,1024]{2,1,0:T(8,128)(2,1)S(1)}, u32[]{:S(2)}, u32[]{:S(2)}) async-start(bf16[4,64,1024]{2,1,0:T(8,128)(2,1)} %bitcast.12), calls=%async_computation.1 | async-start | bytes 1048576 | tf_op jit(solution)/shard_map/all_to_all | solution.py:264
  152.4 3.9 %all-to-all-done.1 = bf16[4,64,1024]{2,1,0:T(8,128)(2,1)S(1)} async-done(((bf16[4,64,1024]{2,1,0:T(8,128)(2,1)}), bf16[4,64,1024]{2,1,0:T(8,128)(2,1)S(1)}, u32[]{:S(2)}, u32[]{:S(2)}) %all-to-all-start.1) | async-done | bytes 524320 | tf_op jit(solution)/shard_map/all_to_all | solution.py:264
  157.7 8.8 %all-to-all-start.2 = ((f32[16,64,100]{2,1,0:T(8,128)}), f32[16,64,100]{2,1,0:T(8,128)S(1)}, u32[]{:S(2)}, u32[]{:S(2)}) async-start(f32[16,64,100]{2,1,0:T(8,128)} %broadcast_in_dim.40), calls=%async_computation.2 | async-start | bytes 1048576 | tf_op jit(solution)/shard_map/all_to_all | solution.py:272
  168.9 1.6 copy.36
  170.5 1.6 copy.37
  172.0 4.2 %all-to-all-done.2 = f32[16,64,100]{2,1,0:T(8,128)S(1)} async-done(((f32[16,64,100]{2,1,0:T(8,128)}), f32[16,64,100]{2,1,0:T(8,128)S(1)}, u32[]{:S(2)}, u32[]{:S(2)}) %all-to-all-start.2) | async-done | bytes 409632 | tf_op jit(solution)/shard_map/all_to_all | solution.py:272
  176.2 4.7 %all-to-all-start.3 = ((bf16[16,96,384]{2,1,0:T(8,128)(2,1)}), bf16[16,96,384]{2,1,0:T(8,128)(2,1)S(1)}, u32[]{:S(2)}, u32[]{:S(2)}) async-start(bf16[16,96,384]{2,1,0:T(8,128)(2,1)} %copy.37), calls=%async_computation.3 | async-start | bytes 2359296 | tf_op jit(solution)/shard_map/all_to_all | solution.py:249
  181.0 1.3 collective-permute-start.4
  182.4 1.5 collective-permute-start.5
  184.3 2.7 %collective-permute-done.5 = bf16[8,128]{1,0:T(8,128)(2,1)S(1)} collective-permute-done((bf16[8,128]{1,0:T(8,128)(2,1)S(1)}, bf16[8,128]{1,0:T(8,128)(2,1)S(1)}, u32[]{:S(2)}, u32[]{:S(2)}) %collective-permute-start.5) | collective-permute-done | bytes 2080 | tf_op jit(solution)/shard_map/ppermute | solution.py:291
  187.5 1.4 copy-done.18
  188.9 9.1 %all-to-all-done.3 = bf16[16,96,384]{2,1,0:T(8,128)(2,1)S(1)} async-done(((bf16[16,96,384]{2,1,0:T(8,128)(2,1)}), bf16[16,96,384]{2,1,0:T(8,128)(2,1)S(1)}, u32[]{:S(2)}, u32[]{:S(2)}) %all-to-all-start.3) | async-done | bytes 1179680 | tf_op jit(solution)/shard_map/all_to_all | solution.py:249
  198.0 3.1 %fusion.4 = f32[768,384]{1,0:T(8,128)S(1)} fusion(bf16[16,96,384]{2,1,0:T(8,128)(2,1)S(1)} %all-to-all-done.3, bf16[16,384,768]{2,1,0:T(8,128)(2,1)} %bitcast.116), kind=kOutput, calls=%fused_computation.10 | convolution fusion | flops 905969664 | bytes 4718592 | tf_op jit(solution)/shard_map/dot_general | solution.py:275
  202.1 1.3 copy-done.19
  203.3 1.3 fusion.1
  205.7 4.3 %all-to-all-start.4 = ((bf16[16,72,192]{2,1,0:T(8,128)(2,1)}), bf16[16,72,192]{2,1,0:T(8,128)(2,1)S(1)}, u32[]{:S(2)}, u32[]{:S(2)}) async-start(bf16[16,72,192]{2,1,0:T(8,128)(2,1)} %pad.34), calls=%async_computation.4 | async-start | bytes 1179648 | tf_op jit(solution)/shard_map/all_to_all | solution.py:304
  211.1 9.2 %all-to-all-done.4.up_ref = bf16[16,72,192]{2,1,0:T(8,128)(2,1)S(1)} async-done(((bf16[16,72,192]{2,1,0:T(8,128)(2,1)}), bf16[16,72,192]{2,1,0:T(8,128)(2,1)S(1)}, u32[]{:S(2)}, u32[]{:S(2)}) %all-to-all-start.4) | async-done | bytes 442400 | tf_op jit(solution)/shard_map/all_to_all | solution.py:304
  220.3 3.7 %copy-done.1 = bf16[6144,768]{1,0:T(8,128)(2,1)S(1)} copy-done((bf16[6144,768]{1,0:T(8,128)(2,1)S(1)}, bf16[6144,768]{1,0:T(8,128)(2,1)}, u32[]{:S(2)}) %copy-start.1) | copy-done | bytes 9437208
  224.0 19.1 %convolutions.1 = bf16[64,3072]{1,0:T(8,128)(2,1)S(1)} custom-call(s32[2]{0:T(128)S(1)} %add_convert_fusion.1.flag_ref, bf16[16,72,192]{2,1,0:T(8,128)(2,1)S(1)} %all-to-all-done.4.up_ref, f32[2,768]{1,0:T(2,128)S(1)} %copy-done.4, bf16[16,384,768]{2,1,0:T(8,128)(2,1)S(1)} %bitcast.117), custom_call_target="tpu_custom_call" | custom-call | flops 2000000000 | bytes 8388608 | tf_op jit(solution)/shard_map/convolutions/pallas_call | solution.py:185
  (134 shorter events, 22.4 us)
Async XLA Ops:
  7.2 142.2 %copy-start = (f32[1024,100]{0,1:T(8,128)S(1)}, f32[1024,100]{0,1:T(8,128)}, u32[]{:S(2)}) copy-start(f32[1024,100]{0,1:T(8,128)} %param.20) | copy-start | bytes 1228804
  7.2 3.0 %copy-start.16 = (bf16[7,96,100]{2,1,0:T(8,128)(2,1)S(1)}, bf16[7,96,100]{2,1,0:T(8,128)(2,1)}, u32[]{:S(2)}) copy-start(bf16[7,96,100]{2,1,0:T(8,128)(2,1)} %param.21) | copy-start | bytes 403204
  7.2 3.3 %copy-start.14 = (bf16[3,48,768]{2,1,0:T(8,128)(2,1)S(1)}, bf16[3,48,768]{2,1,0:T(8,128)(2,1)}, u32[]{:S(2)}) copy-start(bf16[3,48,768]{2,1,0:T(8,128)(2,1)} %param.25) | copy-start | bytes 663556
  7.2 3.3 %copy-start.15 = (bf16[3,48,768]{2,1,0:T(8,128)(2,1)S(1)}, bf16[3,48,768]{2,1,0:T(8,128)(2,1)}, u32[]{:S(2)}) copy-start(bf16[3,48,768]{2,1,0:T(8,128)(2,1)} %param.24) | copy-start | bytes 663556
  7.2 40.0 %all-gather.4.cloned.1.call-start = ((), (), s32[]{:S(2)}) async-start(), calls=%async_computation.5 | async-start | bytes 2621440 | tf_op jit(solution)/shard_map/all_gather | solution.py:231
  10.1 37.1 %copy-start.11 = (bf16[1024,256]{1,0:T(8,128)(2,1)S(1)}, bf16[1024,256]{1,0:T(8,128)(2,1)}, u32[]{:S(2)}) copy-start(bf16[1024,256]{1,0:T(8,128)(2,1)} %param.17) | copy-start | bytes 1572868
  10.2 187.9 %all-gather.6.cloned.1.call-start = ((), (), s32[]{:S(2)}) async-start(), calls=%async_computation.6 | async-start | bytes 10027008 | tf_op jit(solution)/shard_map/all_gather | solution.py:237
  10.3 37.0 %copy-start.12 = (bf16[256,1024]{1,0:T(8,128)(2,1)S(1)}, bf16[256,1024]{1,0:T(8,128)(2,1)}, u32[]{:S(2)}) copy-start(bf16[256,1024]{1,0:T(8,128)(2,1)} %param.18) | copy-start | bytes 1572868
  11.4 37.4 %copy-start.13 = (bf16[64,1024]{1,0:T(8,128)(2,1)S(1)}, bf16[64,1024]{1,0:T(8,128)(2,1)}, u32[]{:S(2)}) copy-start(bf16[64,1024]{1,0:T(8,128)(2,1)} %param.13) | copy-start | bytes 393220
  47.3 43.2 %copy-start.17 = (f32[8,1024]{1,0:T(8,128)S(1)}, f32[8,1024]{1,0:T(8,128)}, u32[]{:S(2)}) copy-start(f32[8,1024]{1,0:T(8,128)} %param.14) | copy-start | bytes 98308
  47.3 43.2 %copy-start.2 = (bf16[1024,1024]{1,0:T(8,128)(2,1)S(1)}, bf16[1024,1024]{1,0:T(8,128)(2,1)}, u32[]{:S(2)}) copy-start(bf16[1024,1024]{1,0:T(8,128)(2,1)} %all-gather.4.cloned.1.call-done.w_ref) | copy-start | bytes 6291460
  47.5 73.4 %collective-permute-start.2 = (bf16[2048,256]{1,0:T(8,128)(2,1)S(1)}, bf16[2048,256]{1,0:T(8,128)(2,1)S(1)}, u32[]{:S(2)}, u32[]{:S(2)}) collective-permute-start(bf16[2048,256]{1,0:T(8,128)(2,1)S(1)} %slice_dynamic-update-slice_fusion.w0), channel_id=1, source_target_pairs={{0,2},{1,3},{2,0},{3,1},{4,6},{5,7},{6,4},{7,5},{8,10},{9,11},{10,... | collective-permute-start | bytes 3145736 | tf_op jit(solution)/shard_map/ppermute | solution.py:241
  94.3 12.8 %collective-permute-start = (bf16[256,512]{1,0:T(8,128)(2,1)}, bf16[256,512]{1,0:T(8,128)(2,1)S(1)}, u32[]{:S(2)}, u32[]{:S(2)}) collective-permute-start(bf16[256,512]{1,0:T(8,128)(2,1)} %bitcast.115), channel_id=1, source_target_pairs={{0,4},{1,5},{2,6},{3,7},{4,8},{5,9},{6,10},{7,11},{8,12},{9,13},{1... | collective-permute-start | bytes 786440 | tf_op jit(solution)/shard_map/ppermute | solution.py:254
  95.6 46.3 %collective-permute-start.1 = (bf16[2048,256]{1,0:T(8,128)(2,1)S(1)}, bf16[2048,256]{1,0:T(8,128)(2,1)}, u32[]{:S(2)}, u32[]{:S(2)}) collective-permute-start(bf16[2048,256]{1,0:T(8,128)(2,1)S(1)} %slice_dynamic-update-slice_fusion.w0), channel_id=1, source_target_pairs={{0,1},{1,0},{2,3},{3,2},{4,5},{5,4},{6,7},{7,6},{8,9},{9,8},{10,11... | collective-permute-start | bytes 3145736 | tf_op jit(solution)/shard_map/ppermute | solution.py:240
  111.9 18.8 %all-to-all-start = ((bf16[4,64,1024]{2,1,0:T(8,128)(2,1)}), bf16[4,64,1024]{2,1,0:T(8,128)(2,1)S(1)}, u32[]{:S(2)}, u32[]{:S(2)}) async-start(bf16[4,64,1024]{2,1,0:T(8,128)(2,1)} %bitcast.8), calls=%async_computation | async-start | bytes 1048576 | tf_op jit(solution)/shard_map/all_to_all | solution.py:257
  120.8 21.0 %collective-permute-start.3 = (bf16[2048,256]{1,0:T(8,128)(2,1)S(1)}, bf16[2048,256]{1,0:T(8,128)(2,1)}, u32[]{:S(2)}, u32[]{:S(2)}) collective-permute-start(bf16[2048,256]{1,0:T(8,128)(2,1)S(1)} %collective-permute-done.2.w2), channel_id=1, source_target_pairs={{0,1},{1,0},{2,3},{3,2},{4,5},{5,4},{6,7},{7,6},{8,9},{9,8},{10,11... | collective-permute-start | bytes 3145736 | tf_op jit(solution)/shard_map/ppermute | solution.py:242
  141.8 7.8 %copy-start.10 = (bf16[1,96,768]{2,1,0:T(8,128)(2,1)S(1)}, bf16[1,96,768]{2,1,0:T(8,128)(2,1)}, u32[]{:S(2)}) copy-start(bf16[1,96,768]{2,1,0:T(8,128)(2,1)} %get-tuple-element.21) | copy-start | bytes 442372
  145.8 4.0 %copy-start.9 = (bf16[1,96,768]{2,1,0:T(8,128)(2,1)S(1)}, bf16[1,96,768]{2,1,0:T(8,128)(2,1)}, u32[]{:S(2)}) copy-start(bf16[1,96,768]{2,1,0:T(8,128)(2,1)} %get-tuple-element.20) | copy-start | bytes 442372
  145.8 4.2 %copy-start.8 = (bf16[1,96,768]{2,1,0:T(8,128)(2,1)S(1)}, bf16[1,96,768]{2,1,0:T(8,128)(2,1)}, u32[]{:S(2)}) copy-start(bf16[1,96,768]{2,1,0:T(8,128)(2,1)} %get-tuple-element.19) | copy-start | bytes 442372
  145.8 4.3 %copy-start.7 = (bf16[1,96,768]{2,1,0:T(8,128)(2,1)S(1)}, bf16[1,96,768]{2,1,0:T(8,128)(2,1)}, u32[]{:S(2)}) copy-start(bf16[1,96,768]{2,1,0:T(8,128)(2,1)} %get-tuple-element.18) | copy-start | bytes 442372
  145.8 10.5 %all-to-all-start.1 = ((bf16[4,64,1024]{2,1,0:T(8,128)(2,1)}), bf16[4,64,1024]{2,1,0:T(8,128)(2,1)S(1)}, u32[]{:S(2)}, u32[]{:S(2)}) async-start(bf16[4,64,1024]{2,1,0:T(8,128)(2,1)} %bitcast.12), calls=%async_computation.1 | async-start | bytes 1048576 | tf_op jit(solution)/shard_map/all_to_all | solution.py:264
  149.9 6.6 %copy-start.20 = (bf16[1024,100]{0,1:T(8,128)(2,1)S(1)}, bf16[1024,100]{0,1:T(8,128)(2,1)}, u32[]{:S(2)}) copy-start(bf16[1024,100]{0,1:T(8,128)(2,1)} %param.19) | copy-start | bytes 614404
  156.4 10.8 %copy-start.6 = (bf16[1,96,768]{2,1,0:T(8,128)(2,1)S(1)}, bf16[1,96,768]{2,1,0:T(8,128)(2,1)}, u32[]{:S(2)}) copy-start(bf16[1,96,768]{2,1,0:T(8,128)(2,1)} %get-tuple-element.17) | copy-start | bytes 442372
  156.5 10.8 %copy-start.5 = (bf16[1,96,768]{2,1,0:T(8,128)(2,1)S(1)}, bf16[1,96,768]{2,1,0:T(8,128)(2,1)}, u32[]{:S(2)}) copy-start(bf16[1,96,768]{2,1,0:T(8,128)(2,1)} %get-tuple-element.16) | copy-start | bytes 442372
  157.7 18.5 %all-to-all-start.2 = ((f32[16,64,100]{2,1,0:T(8,128)}), f32[16,64,100]{2,1,0:T(8,128)S(1)}, u32[]{:S(2)}, u32[]{:S(2)}) async-start(f32[16,64,100]{2,1,0:T(8,128)} %broadcast_in_dim.40), calls=%async_computation.2 | async-start | bytes 1048576 | tf_op jit(solution)/shard_map/all_to_all | solution.py:272
  176.2 21.8 %all-to-all-start.3 = ((bf16[16,96,384]{2,1,0:T(8,128)(2,1)}), bf16[16,96,384]{2,1,0:T(8,128)(2,1)S(1)}, u32[]{:S(2)}, u32[]{:S(2)}) async-start(bf16[16,96,384]{2,1,0:T(8,128)(2,1)} %copy.37), calls=%async_computation.3 | async-start | bytes 2359296 | tf_op jit(solution)/shard_map/all_to_all | solution.py:249
  181.0 2.9 %collective-permute-start.4 = (bf16[8,128]{1,0:T(8,128)(2,1)S(1)}, bf16[8,128]{1,0:T(8,128)(2,1)S(1)}, u32[]{:S(2)}, u32[]{:S(2)}) collective-permute-start(bf16[8,128]{1,0:T(8,128)(2,1)S(1)} %get-tuple-element.30), channel_id=1, source_target_pairs={{0,16},{16,32},{32,48},{48,64},{64,80},{80,96},{96,112},{112,128},... | collective-permute-start | bytes 6152 | tf_op jit(solution)/shard_map/ppermute | solution.py:290
  182.4 4.6 %collective-permute-start.5 = (bf16[8,128]{1,0:T(8,128)(2,1)S(1)}, bf16[8,128]{1,0:T(8,128)(2,1)S(1)}, u32[]{:S(2)}, u32[]{:S(2)}) collective-permute-start(bf16[8,128]{1,0:T(8,128)(2,1)S(1)} %get-tuple-element.29), channel_id=1, source_target_pairs={{16,0},{32,16},{48,32},{64,48},{80,64},{96,80},{112,96},{128,112},... | collective-permute-start | bytes 6152 | tf_op jit(solution)/shard_map/ppermute | solution.py:291
  201.7 1.7 copy-start.19
  204.8 15.5 %copy-start.4 = (f32[2,768]{1,0:T(2,128)S(1)}, f32[2,768]{1,0:T(2,128)}, u32[]{:S(2)}) copy-start(f32[2,768]{1,0:T(2,128)} %alpha_ref.1) | copy-start | bytes 18436
  205.7 14.6 %all-to-all-start.4 = ((bf16[16,72,192]{2,1,0:T(8,128)(2,1)}), bf16[16,72,192]{2,1,0:T(8,128)(2,1)S(1)}, u32[]{:S(2)}, u32[]{:S(2)}) async-start(bf16[16,72,192]{2,1,0:T(8,128)(2,1)} %pad.34), calls=%async_computation.4 | async-start | bytes 1179648 | tf_op jit(solution)/shard_map/all_to_all | solution.py:304
  220.3 3.7 %copy-start.1 = (bf16[6144,768]{1,0:T(8,128)(2,1)S(1)}, bf16[6144,768]{1,0:T(8,128)(2,1)}, u32[]{:S(2)}) copy-start(bf16[6144,768]{1,0:T(8,128)(2,1)} %all-gather.6.cloned.1.call-done) | copy-start | bytes 28311556
  (2 other events, 3.0 us)
Sparse Core Ops, SparseCore 0:
  10.3 36.9 all-gather.3
  49.1 83.6 all-gather.5

commit v2 on v1

v2 whole, which is shorter than its diff:
```python
import math

import jax
import jax.numpy as jnp
from jax import lax
from jax.experimental import pallas as pl
from jax.experimental.pallas import tpu as pltpu
from jax.sharding import PartitionSpec as P


HEAD_DIM = 64
BLK = 256
MEL_PAD = 128
OFFSETS = 9

epsilon = 1e-06
bf16 = jnp.bfloat16
f32 = jnp.float32

X_GROUPS = [[4 * x + j for x in range(4)] for j in range(4)]
J_GROUPS = [[4 * x + j for j in range(4)] for x in range(4)]


def norm_rows(rows, offset_row, scale_row):
    rows = rows.astype(f32)
    center = jnp.mean(rows, axis=-1, keepdims=True)
    square = jnp.mean(rows * rows, axis=-1, keepdims=True)
    spread = square - center * center
    return (rows - center) * lax.rsqrt(spread + epsilon) * (1.0 + scale_row) + offset_row


def mm(a, b):
    return jnp.dot(a, b, preferred_element_type=f32)


def mm_t(a, b):
    return lax.dot_general(a, b, (((1,), (1,)), ((), ())), preferred_element_type=f32)


def vmem_specs(n):
    return [pl.BlockSpec(memory_space=pltpu.VMEM)] * n


def whole(kernel, out_shapes, args, scratch=(), cost=None, smem=0, vmem=24):
    single = not isinstance(out_shapes, (tuple, list))
    return pl.pallas_call(
        kernel,
        out_shape=out_shapes,
        in_specs=[pl.BlockSpec(memory_space=pltpu.SMEM)] * smem + vmem_specs(len(args) - smem),
        out_specs=vmem_specs(1)[0] if single else vmem_specs(len(out_shapes)),
        scratch_shapes=list(scratch),
        compiler_params=pltpu.CompilerParams(vmem_limit_bytes=vmem << 20),
        cost_estimate=cost,
    )(*args)


def cost_of(flops, nbytes, trans=0):
    return pl.CostEstimate(flops=flops, bytes_accessed=nbytes, transcendentals=trans)


def attention_weights_kernel(w_ref, o_ref, out_ref):
    for k in range(3):
        out_ref[64 * k : 64 * k + 64, :] = w_ref[k]
    out_ref[192:256, :] = o_ref[...]


def mlp_weights_kernel(up_ref, down_ref, out_ref):
    out_ref[0:1024, :] = up_ref[...]
    for k in range(4):
        out_ref[1024 + 256 * k : 1280 + 256 * k, :] = down_ref[:, 256 * k : 256 * k + 256]


def vocoder_weights_kernel(pre_ref, dil_ref, plain_ref, out_ref):
    out_ref[0:96, :] = jnp.zeros((96, 768), bf16)
    for k in range(7):
        out_ref[0:96, 100 * k : 100 * k + 100] = pre_ref[k]
    for k in range(3):
        out_ref[96 + 48 * k : 144 + 48 * k, :] = dil_ref[k]
        out_ref[240 + 48 * k : 288 + 48 * k, :] = plain_ref[k]


TAP_ORDER = (2, 3, 4, 5, 6, 7, 0, 1)


def upsample_weights_kernel(w_ref, out_ref):
    for s in range(16):
        for t, tap in enumerate(TAP_ORDER):
            out_ref[s, :, 48 * t : 48 * t + 48] = w_ref[tap, :, 48 * s : 48 * s + 48]


def attention_kernel(
    flag_ref, own_ref, back_ref, mod_ref, w0, w1, w2, w3a, w3b, out_ref, heads, w_out
):
    first = flag_ref[0] > 0
    scale = 1.0 / math.sqrt(HEAD_DIM)
    shift, gain = mod_ref[0:1, :], mod_ref[1:2, :]
    own = norm_rows(own_ref[...], shift, gain).astype(bf16)
    back = norm_rows(back_ref[...], shift, gain).astype(bf16)
    for h, (wa, wb, base) in enumerate(((w0, w0, 128), (w1, w1, 128), (w2, w2, 128), (w3a, w3b, 0))):
        qk = mm_t(own, wa[0:128, :]).astype(bf16)
        q, k = qk[:, 0:64], qk[:, 64:128]
        v = mm_t(own, wb[base : base + 64, :]).astype(bf16)
        kb = mm_t(back, wa[64:128, :]).astype(bf16)
        vb = mm_t(back, wb[base : base + 64, :]).astype(bf16)
        s_own = mm_t(q, k) * scale
        s_back = mm_t(q, kb) * scale
        s_back = jnp.where(first, -1e30, s_back)
        top = jnp.maximum(
            jnp.max(s_own, axis=-1, keepdims=True), jnp.max(s_back, axis=-1, keepdims=True)
        )
        e_own = jnp.exp(s_own - top)
        e_back = jnp.exp(s_back - top)
        total = jnp.sum(e_own, axis=-1, keepdims=True) + jnp.sum(e_back, axis=-1, keepdims=True)
        inv = 1.0 / total
        p_own = (e_own * inv).astype(bf16)
        p_back = (e_back * inv).astype(bf16)
        heads[:, 64 * h : 64 * h + 64] = (mm(p_own, v) + mm(p_back, vb)).astype(bf16)
        w_out[64 * h : 64 * h + 64, :] = wb[base + 64 : base + 128, :]
    out_ref[...] = mm(heads[...], w_out[...]).astype(bf16)


def after_attention_kernel(parts_ref, frames_ref, mod_ref, mixed_ref, norm_ref):
    attn = parts_ref[0].astype(f32)
    for k in range(1, 4):
        attn += parts_ref[k].astype(f32)
    mixed = (frames_ref[...].astype(f32) + mod_ref[2:3, :] * attn).astype(bf16)
    mixed_ref[...] = mixed
    norm_ref[...] = norm_rows(mixed, mod_ref[3:4, :], mod_ref[4:5, :]).astype(bf16)


def mlp_kernel(h_ref, w0, w1, w2, w3, out_ref, acc):
    h = h_ref[...]
    for i, w in enumerate((w0, w1, w2, w3)):
        up = mm(h, w[0:1024, :])
        hid = jax.nn.gelu(up, approximate=True).astype(bf16)
        for k in range(4):
            part = mm(hid, w[1024 + 256 * k : 1280 + 256 * k, :])
            cols = slice(256 * k, 256 * k + 256)
            if i == 0:
                acc[:, cols] = part
            elif i < 3:
                acc[:, cols] += part
            else:
                out_ref[:, cols] = (acc[:, cols] + part).astype(bf16)


def after_mlp_kernel(parts_ref, mixed_ref, mod_ref, wv_ref, noisy_ref, out_ref):
    feed = parts_ref[0].astype(f32)
    for k in range(1, 4):
        feed += parts_ref[k].astype(f32)
    final = (mixed_ref[...].astype(f32) + mod_ref[5:6, :] * feed).astype(bf16)
    normed = norm_rows(final, mod_ref[6:7, :], mod_ref[7:8, :]).astype(bf16)
    mel = noisy_ref[...] + 0.5 * mm(normed, wv_ref[...])
    for s in range(16):
        out_ref[s] = mel


def placed_kernel(comp_ref, full_ref, here_ref):
    earlier = lax.broadcasted_iota(jnp.int32, (100, 192), 1) < 96
    full_ref[...] = jnp.zeros(full_ref.shape, bf16)
    here_ref[...] = jnp.zeros(here_ref.shape, bf16)
    here = [comp_ref[100 * j : 100 * j + 100, 0:192] for j in range(7)]
    near = [comp_ref[100 * j : 100 * j + 100, 192:384] for j in range(7)]
    for d in range(OFFSETS):
        value = jnp.zeros((100, 192), f32)
        if 0 <= d - 1 < 7:
            value = here[d - 1]
            here_ref[MEL_PAD * d : MEL_PAD * d + 100, :] = value.astype(bf16)
        if d < 7:
            value = value + jnp.where(earlier, near[d], 0.0)
        if 0 <= d - 2 < 7:
            value = value + jnp.where(earlier, 0.0, near[d - 2])
        full_ref[MEL_PAD * d : MEL_PAD * d + 100, :] = value.astype(bf16)


EXT = 1056


def upsample_kernel(flag_ref, mel_ref, before_ref, after_ref, full_ref, here_ref, out_ref, ext, up):
    ext[...] = jnp.zeros((EXT, MEL_PAD), f32)
    ext[0:8, 0:100] = before_ref[...]
    for s in range(16):
        ext[8 + 64 * s : 72 + 64 * s, 0:100] = mel_ref[s]
    ext[1032:1040, 0:100] = after_ref[...]
    cols = [ext[3 + k : 3 + k + 1032, :].astype(bf16) for k in range(OFFSETS)]
    up[...] = mm(jnp.concatenate(cols, axis=1), full_ref[...])
    earlier = lax.broadcasted_iota(jnp.int32, (8, 192), 1) < 96
    row = lax.broadcasted_iota(jnp.int32, (8, 192), 0)
    for which, base, r in ((0, 0, 1), (1, 1024, 0)):
        edge_cols = [ext[base + 3 + k : base + 11 + k, :].astype(bf16) for k in range(OFFSETS)]
        edge = mm(jnp.concatenate(edge_cols, axis=1), here_ref[...])
        lanes = earlier if which == 0 else jnp.logical_not(earlier)
        use = (flag_ref[which] > 0) & (row == r) & lanes
        up[base : base + 8, :] = jnp.where(use, edge, up[base : base + 8, :])
    for s in range(16):
        out_ref[s] = up[64 * s : 64 * s + ROWS, :].astype(bf16)


PI_PARTS = (3.140625, 0.000965118408203125, 2.5331974029541016e-06, 1.984187258941006e-09)


def sin_squared(x):
    k = jnp.round(x * (1.0 / math.pi))
    r = x
    for part in PI_PARTS:
        r = r - k * part
    z = r * r
    poly = -2.3889859e-08 * z + 2.7525562e-06
    poly = poly * z - 1.9840874e-04
    poly = poly * z + 8.3333310e-03
    poly = poly * z - 1.6666667e-01
    sine = r + r * (z * poly)
    return sine * sine


def snake_act(values, alpha_row, inverse_row):
    return values + sin_squared(alpha_row * values) * inverse_row


def shifted(plane, by):
    return pltpu.roll(plane, by % plane.shape[0], 0)


ROWS = 72


def conv_kernel(flag_ref, up_ref, alpha_ref, w_ref, out_ref, planes):
    first = flag_ref[0] > 0
    last = flag_ref[1] > 0
    row = lax.broadcasted_iota(jnp.int32, (ROWS, 768), 0)
    outside = (first & (row == 0)) | (last & (row == 65))
    for s in range(16):
        for p in range(4):
            planes[p, :, 48 * s : 48 * s + 48] = up_ref[s, :, 48 * p : 48 * p + 48]
    a1 = alpha_ref[0:1, :]
    a2 = alpha_ref[1:2, :]
    i1 = 1.0 / a1
    i2 = 1.0 / a2

    def weight(base, tap):
        return jnp.concatenate(
            [w_ref[s, base + 48 * tap : base + 48 * tap + 48, :] for s in range(16)], axis=0
        )

    ups = []
    acts = []
    for p in range(4):
        u = jnp.where(outside, 0.0, planes[p].astype(f32))
        ups.append(u)
        acts.append(snake_act(u, a1, i1).astype(bf16))
    act = jnp.concatenate(acts, axis=0)
    y = [mm(act, weight(96, tap)) for tap in range(3)]
    y = [[v[ROWS * p : ROWS * p + ROWS] for p in range(4)] for v in y]
    acts = []
    for p in range(4):
        before = y[0][0] if p == 3 else shifted(y[0][p + 1], 1)
        after = y[2][3] if p == 0 else shifted(y[2][p - 1], -1)
        inner = before + y[1][p] + after
        acts.append(jnp.where(outside, 0.0, snake_act(inner, a2, i2)).astype(bf16))
    act = jnp.concatenate(acts, axis=0)
    y = [mm(act, weight(240, tap)) for tap in range(3)]
    y = [[v[ROWS * p : ROWS * p + ROWS] for p in range(4)] for v in y]
    for p in range(4):
        before = y[0][p - 1] if p >= 1 else shifted(y[0][3], 1)
        after = y[2][p + 1] if p <= 2 else shifted(y[2][0], -1)
        total = ups[p] + (before + y[1][p] + after)
        out_ref[:, 768 * p : 768 * p + 768] = shifted(total, -1)[0:64].astype(bf16)


def gather(value, groups):
    return lax.all_gather(value, "sub", axis=0, tiled=True, axis_index_groups=groups)


def exchange(value, groups=None):
    return lax.all_to_all(value, "sub", 0, 0, tiled=True, axis_index_groups=groups)


def device(y_hi, z, x, y_lo, core):
    return (y_hi * 8 + z) * 16 + x * 4 + y_lo * 2 + core


OTHER_Y = [
    (device(h, z, x, y, c), device(1 - h, z, x, 1 - y, c))
    for h in range(2)
    for z in range(8)
    for x in range(4)
    for y in range(2)
    for c in range(2)
]


def program(
    frames,
    modulation,
    w_project,
    w_heads_out,
    w_up,
    w_down,
    w_velocity,
    noisy_mel,
    w_prelude,
    w_upsample,
    snake_alpha,
    w_dilated,
    w_plain,
):
    own_rows = frames.shape[0]
    sub_index = lax.axis_index("sub")
    time_index = lax.axis_index("tm")
    n_sub = lax.axis_size("sub")
    n_tm = lax.axis_size("tm")
    n_all = n_sub * n_tm
    both = ("tm", "sub")
    shape = jax.ShapeDtypeStruct
    here_index = time_index * n_sub + sub_index

    to_right = [(i, (i + 4) % 16) for i in range(16)]
    to_left = [(i, (i - 4) % 16) for i in range(16)]
    w_own = whole(
        attention_weights_kernel,
        shape((256, 1024), bf16),
        (jnp.swapaxes(w_project, 1, 2), w_heads_out),
        cost=cost_of(0, 1 << 20),
    )
    back_frames = lax.ppermute(frames, both, [(i, i + 4) for i in range(n_all - 4)])
    from_left = lax.ppermute(w_own, "sub", to_right)
    from_right = lax.ppermute(w_own, "sub", to_left)

    w_voc = whole(
        vocoder_weights_kernel,
        shape((384, 768), bf16),
        lax.optimization_barrier((w_prelude, w_dilated, w_plain, w_own))[:3],
        cost=cost_of(0, 2 << 20),
    )
    w_voc = lax.all_gather(w_voc, "sub", axis=0, tiled=False)

    block = gather(frames, J_GROUPS)
    far_a = lax.ppermute(from_left[:128], "sub", to_right)
    far_b = lax.ppermute(from_right[128:], "sub", to_left)
    back = gather(back_frames, J_GROUPS)

    own_mlp = whole(
        mlp_weights_kernel, shape((2048, 256), bf16), (w_up, w_down), cost=cost_of(0, 2 << 20)
    )
    other_core = lax.ppermute(own_mlp, "sub", [(i, i ^ 1) for i in range(16)])
    other_y = lax.ppermute(own_mlp, both, OTHER_Y)
    other_both = lax.ppermute(other_y, "sub", [(i, i ^ 1) for i in range(16)])

    ups = whole(
        upsample_weights_kernel, shape((16, 96, 384), bf16), (w_upsample,), cost=cost_of(0, 3 << 20)
    )

    is_first = (time_index == 0) & (sub_index < 4)
    partial = whole(
        attention_kernel,
        shape((BLK, 1024), bf16),
        (
            is_first.astype(jnp.int32).reshape(1),
            block,
            back,
            modulation,
            w_own,
            from_left,
            from_right,
            far_a,
            far_b,
        ),
        scratch=[pltpu.VMEM((BLK, 256), bf16), pltpu.VMEM((256, 1024), bf16)],
        cost=cost_of(10**9, 4 << 20, 1 << 19),
        smem=1,
    )
    ups = exchange(ups)
    partial, ups = lax.optimization_barrier((partial, ups))
    parts = exchange(partial, J_GROUPS)
    mixed_rows, own_norm = whole(
        after_attention_kernel,
        (shape((own_rows, 1024), bf16), shape((own_rows, 1024), bf16)),
        (parts.reshape(4, own_rows, 1024), frames, modulation),
        cost=cost_of(10**6, 1 << 20),
    )

    second = gather(own_norm, X_GROUPS)
    partial = whole(
        mlp_kernel,
        shape((256, 1024), bf16),
        (second, own_mlp, other_core, other_y, other_both),
        scratch=[pltpu.VMEM((256, 1024), f32)],
        cost=cost_of(11 * 10**8, 5 << 20, 1 << 18),
    )
    parts = exchange(partial, X_GROUPS)
    noisy_own = lax.dynamic_slice_in_dim(noisy_mel, sub_index * own_rows, own_rows, 0)
    copies = whole(
        after_mlp_kernel,
        shape((16, own_rows, 100), f32),
        (parts.reshape(4, own_rows, 1024), mixed_rows, modulation, w_velocity, noisy_own),
        cost=cost_of(10**7, 1 << 20),
    )
    mel_all = exchange(copies)
    mel_next = mel_all.reshape(-1, 100)

    pre_all = w_voc[:, :96, :].reshape(1536, 768)
    comp = lax.dot_general(
        pre_all, ups.reshape(1536, 384), (((0,), (0,)), ((), ())), preferred_element_type=f32
    )
    w_full, w_here = whole(
        placed_kernel,
        (shape((OFFSETS * MEL_PAD, 192), bf16), shape((OFFSETS * MEL_PAD, 192), bf16)),
        (comp,),
        cost=cost_of(10**6, 2 << 20),
    )

    before = lax.ppermute(mel_all[15, 56:], "tm", [(i, i + 1) for i in range(n_tm - 1)])
    after = lax.ppermute(mel_all[0, :8], "tm", [(i + 1, i) for i in range(n_tm - 1)])
    windows = whole(
        upsample_kernel,
        shape((16, ROWS, 192), bf16),
        (
            jnp.stack([time_index == 0, time_index == n_tm - 1]).astype(jnp.int32),
            mel_all,
            before,
            after,
            w_full,
            w_here,
        ),
        scratch=[pltpu.VMEM((EXT, MEL_PAD), f32), pltpu.VMEM((1032, 192), f32)],
        cost=cost_of(5 * 10**8, 2 << 20),
        smem=1,
    )
    up_x = exchange(windows)

    flags = jnp.stack([here_index == 0, here_index == n_all - 1]).astype(jnp.int32)
    out = whole(
        conv_kernel,
        shape((64, 3072), bf16),
        (flags, up_x, snake_alpha, w_voc),
        scratch=[pltpu.VMEM((4, ROWS, 768), bf16)],
        cost=cost_of(2 * 10**9, 8 << 20, 1 << 18),
        smem=1,
        vmem=32,
    )
    return (mel_next, out.reshape(256, 768))


def solution(mesh):
    in_specs = (
        P(("tm", "sub"), None),
        P(),
        P(None, None, "sub"),
        P("sub", None),
        P(None, "sub"),
        P("sub", None),
        P(),
        P("tm", None),
        P(None, "sub", None),
        P(None, "sub", None),
        P(),
        P(None, "sub", None),
        P(None, "sub", None),
    )
    out_specs = (P("tm", None), P(("tm", "sub"), None))
    return jax.shard_map(program, mesh=mesh, in_specs=in_specs, out_specs=out_specs, check_vma=False)
```

time: 252 us -> 211 us (0.84)
  the two profiles are of different devices: /device:TPU:1 before, /device:TPU:16 now
where the time goes in v2:
time: 211 us; the launch traced here: 210 us
  waiting for transfers between devices  67.7 us (32%)
  blocking collectives  44.9 us (21%)
  starting transfers between devices  42.1 us (20%)
  Pallas kernels  21.4 us (10%)
  local copies, waits for them, and re-layouts  16 us (8%)
  between operations  14.3 us (7%)
  matrix products  3.39 us (2%)
    ppermute x1, waiting for transfers between devices, program(): from_left = lax.ppermute(w_own, 'sub', to_right)  38.8 us
    all_gather x3, blocking collectives, gather(): lax.all_gather(value, 'sub', axis=0, tiled=True, axis_index_groups=groups)  33.7 us
    all_to_all x4, waiting for transfers between devices, exchange(): lax.all_to_all(value, 'sub', 0, 0, tiled=True, axis_index_groups=groups)  28.8 us
    pallas_call x11, Pallas kernels, whole(): pl.pallas_call(kernel, out_shape=out_shapes, in_specs=[pl.BlockSpec(memor...  21.4 us
    all_to_all x4, starting transfers between devices, exchange(): lax.all_to_all(value, 'sub', 0, 0, tiled=True, axis_index_groups=groups)  16.2 us
    unnamed x43, local copies, waits for them, and re-layouts  14.2 us
    all_to_all x1, blocking collectives, exchange(): lax.all_to_all(value, 'sub', 0, 0, tiled=True, axis_index_groups=groups)  11.2 us
    ppermute x1, starting transfers between devices, program(): lax.ppermute(mel_all[0, :8], 'tm', [(i + 1, i) for i in range(n_tm - 1)])  9.79 us
  transfers between devices with their start and end apart: 15, of which 4 were waited for; matrix products, arithmetic and copies ran while one was open for 3% of the time, Pallas kernels for 6%

profile of v2, /device:TPU:16, one launch (start us, length us, event | category | flops | bytes accessed | tf_op | source)
XLA Modules:
  0.0 209.9 jit_solution(10274626569373854651)
XLA Ops:
  7.2 1.0 copy-done.10
  9.2 1.0 copy-done.14
  14.4 2.5 %shard_map.142 = bf16[16,96,384]{2,1,0:T(8,128)(2,1)} custom-call(bf16[8,96,768]{2,1,0:T(8,128)(2,1)S(1)} %copy-done.2), custom_call_target="tpu_custom_call" | custom-call | bytes 3145728 | tf_op jit(solution)/shard_map/pallas_call | solution.py:46
  16.9 5.3 %all-to-all-start = ((bf16[16,96,384]{2,1,0:T(8,128)(2,1)}), bf16[16,96,384]{2,1,0:T(8,128)(2,1)}, u32[]{:S(2)}, u32[]{:S(2)}) async-start(bf16[16,96,384]{2,1,0:T(8,128)(2,1)} %shard_map.142), calls=%async_computation | async-start | bytes 2359296 | tf_op jit(solution)/shard_map/all_to_all | solution.py:275
  22.2 2.0 collective-permute-start.1
  24.1 1.4 collective-permute-start.2
  25.5 2.6 %collective-permute-start = (bf16[64,1024]{1,0:T(8,128)(2,1)S(1)}, bf16[64,1024]{1,0:T(8,128)(2,1)}, u32[]{:S(2)}, u32[]{:S(2)}) collective-permute-start(bf16[64,1024]{1,0:T(8,128)(2,1)S(1)} %copy-done.7), channel_id=1, source_target_pairs={{0,4},{1,5},{2,6},{3,7},{4,8},{5,9},{6,10},{7,11},{8,12},{9,13},{1... | collective-permute-start | bytes 393224 | tf_op jit(solution)/shard_map/ppermute | solution.py:325
  28.1 38.8 %collective-permute-done.1.w1 = bf16[256,1024]{1,0:T(8,128)(2,1)S(1)} collective-permute-done((bf16[256,1024]{1,0:T(8,128)(2,1)S(1)}, bf16[256,1024]{1,0:T(8,128)(2,1)S(1)}, u32[]{:S(2)}, u32[]{:S(2)}) %collective-permute-start.1) | collective-permute-done | bytes 524320 | tf_op jit(solution)/shard_map/ppermute | solution.py:326
  66.9 2.6 %collective-permute-start.3 = (bf16[128,1024]{1,0:T(8,128)(2,1)S(1)}, bf16[128,1024]{1,0:T(8,128)(2,1)S(1)}, u32[]{:S(2)}, u32[]{:S(2)}) collective-permute-start(bf16[128,1024]{1,0:T(8,128)(2,1)S(1)} %slice.20), channel_id=1, source_target_pairs={{0,4},{1,5},{2,6},{3,7},{4,8},{5,9},{6,10},{7,11},{8,12},{9,13},{1... | collective-permute-start | bytes 786440 | tf_op jit(solution)/shard_map/ppermute | solution.py:338
  70.2 2.5 %collective-permute-start.4 = (bf16[128,1024]{1,0:T(8,128)(2,1)}, bf16[128,1024]{1,0:T(8,128)(2,1)S(1)}, u32[]{:S(2)}, u32[]{:S(2)}) collective-permute-start(bf16[128,1024]{1,0:T(8,128)(2,1)} %slice.21), channel_id=1, source_target_pairs={{0,12},{1,13},{2,14},{3,15},{4,0},{5,1},{6,2},{7,3},{8,4},{9,5},{1... | collective-permute-start | bytes 786440 | tf_op jit(solution)/shard_map/ppermute | solution.py:339
  72.7 10.2 %all_gather.15.own_ref = bf16[256,1024]{1,0:T(8,128)(2,1)S(1)} all-gather(bf16[64,1024]{1,0:T(8,128)(2,1)S(1)} %copy-done.7), channel_id=1, replica_groups={{0,1,2,3},{4,5,6,7},{8,9,10,11},{12,13,14,15},{16,17,18,19},{20,21,22,2..., dimensions={0}, use_global_device_ids=true | all-gather | bytes 655360 | tf_op jit(solution)/shard_map/all_gather | solution.py:271
  82.9 10.1 %all_gather.16.back_ref = bf16[256,1024]{1,0:T(8,128)(2,1)S(1)} all-gather(bf16[64,1024]{1,0:T(8,128)(2,1)} %collective-permute-done), channel_id=1, replica_groups={{0,1,2,3},{4,5,6,7},{8,9,10,11},{12,13,14,15},{16,17,18,19},{20,21,22,2..., dimensions={0}, use_global_device_ids=true | all-gather | bytes 655360 | tf_op jit(solution)/shard_map/all_gather | solution.py:271
  93.7 1.1 copy-done.4
  94.8 1.1 copy-done.6
  96.8 4.9 %shard_map.141 = bf16[256,1024]{1,0:T(8,128)(2,1)S(1)} custom-call(s32[1]{0:T(128)} %bitcast.flag_ref, bf16[256,1024]{1,0:T(8,128)(2,1)S(1)} %all_gather.15.own_ref, bf16[256,1024]{1,0:T(8,128)(2,1)S(1)} %all_gather.16.back_ref, f32[8,1024]{1,0:T(8,128)S(1)} %copy-done.11, bf16[256,1024]{1,0:T(8,128)(2,1)S(1)} %shard_map.140.w0, ...), custom_call_target="tpu_custom_call" | custom-call | flops 1000000000 | bytes 4194304 | tf_op jit(solution)/shard_map/pallas_call | solution.py:46
  101.7 11.2 %all_to_all.33.parts_ref = bf16[4,64,1024]{2,1,0:T(8,128)(2,1)S(1)} all-to-all(bf16[4,64,1024]{2,1,0:T(8,128)(2,1)S(1)} %bitcast.20), channel_id=1, replica_groups={{0,1,2,3},{4,5,6,7},{8,9,10,11},{12,13,14,15},{16,17,18,19},{20,21,22,2..., dimensions={0} | all-to-all | bytes 1048576 | tf_op jit(solution)/shard_map/all_to_all | solution.py:275
  113.1 13.5 %all_gather.17.h_ref = bf16[256,1024]{1,0:T(8,128)(2,1)S(1)} all-gather(bf16[64,1024]{1,0:T(8,128)(2,1)S(1)} %get-tuple-element.12), channel_id=1, replica_groups={{0,4,8,12},{1,5,9,13},{2,6,10,14},{3,7,11,15},{16,20,24,28},{17,21,25,2..., dimensions={0}, use_global_device_ids=true | all-gather | bytes 655360 | tf_op jit(solution)/shard_map/all_gather | solution.py:271
  126.6 4.2 %shard_map.145 = bf16[256,1024]{1,0:T(8,128)(2,1)} custom-call(bf16[256,1024]{1,0:T(8,128)(2,1)S(1)} %all_gather.17.h_ref, bf16[2048,256]{1,0:T(8,128)(2,1)S(1)} %shard_map.144.w0, bf16[2048,256]{1,0:T(8,128)(2,1)} %collective-permute-done.5.w1, bf16[2048,256]{1,0:T(8,128)(2,1)} %collective-permute-done.6.w2, bf16[2048,256]{1,0:T(8,128)(2,1)} %collective-permute-done.7.w3), custom_call_target="tpu_custom_call" | custom-call | flops 1100000000 | bytes 5242880 | tf_op jit(solution)/shard_map/pallas_call | solution.py:46
  130.9 3.6 %all-to-all-start.2 = ((bf16[4,64,1024]{2,1,0:T(8,128)(2,1)}), bf16[4,64,1024]{2,1,0:T(8,128)(2,1)S(1)}, u32[]{:S(2)}, u32[]{:S(2)}) async-start(bf16[4,64,1024]{2,1,0:T(8,128)(2,1)} %bitcast.3), calls=%async_computation.2 | async-start | bytes 1048576 | tf_op jit(solution)/shard_map/all_to_all | solution.py:275
  134.8 7.7 %all-to-all-done.2.parts_ref = bf16[4,64,1024]{2,1,0:T(8,128)(2,1)S(1)} async-done(((bf16[4,64,1024]{2,1,0:T(8,128)(2,1)}), bf16[4,64,1024]{2,1,0:T(8,128)(2,1)S(1)}, u32[]{:S(2)}, u32[]{:S(2)}) %all-to-all-start.2) | async-done | bytes 524320 | tf_op jit(solution)/shard_map/all_to_all | solution.py:275
  142.5 1.2 shard_map.146
  143.7 3.6 %all-to-all-start.3 = ((f32[16,64,100]{2,1,0:T(8,128)}), f32[16,64,100]{2,1,0:T(8,128)S(1)}, u32[]{:S(2)}, u32[]{:S(2)}) async-start(f32[16,64,100]{2,1,0:T(8,128)} %shard_map.146), calls=%async_computation.3 | async-start | bytes 1048576 | tf_op jit(solution)/shard_map/all_to_all | solution.py:275
  147.3 10.7 %all-to-all-done.3.mel_ref = f32[16,64,100]{2,1,0:T(8,128)S(1)} async-done(((f32[16,64,100]{2,1,0:T(8,128)}), f32[16,64,100]{2,1,0:T(8,128)S(1)}, u32[]{:S(2)}, u32[]{:S(2)}) %all-to-all-start.3) | async-done | bytes 409632 | tf_op jit(solution)/shard_map/all_to_all | solution.py:275
  158.1 4.6 %collective-permute-start.8 = (f32[8,100]{1,0:T(8,128)S(1)}, f32[8,100]{1,0:T(8,128)S(1)}, u32[]{:S(2)}, u32[]{:S(2)}) collective-permute-start(f32[8,100]{1,0:T(8,128)S(1)} %get-tuple-element.23), channel_id=1, source_target_pairs={{0,16},{16,32},{32,48},{48,64},{64,80},{80,96},{96,112},{112,128},... | collective-permute-start | bytes 9608 | tf_op jit(solution)/shard_map/ppermute | solution.py:412
  162.7 9.8 %collective-permute-start.9 = (f32[8,100]{1,0:T(8,128)S(1)}, f32[8,100]{1,0:T(8,128)S(1)}, u32[]{:S(2)}, u32[]{:S(2)}) collective-permute-start(f32[8,100]{1,0:T(8,128)S(1)} %get-tuple-element.22), channel_id=1, source_target_pairs={{16,0},{32,16},{48,32},{64,48},{80,64},{96,80},{112,96},{128,112},... | collective-permute-start | bytes 9608 | tf_op jit(solution)/shard_map/ppermute | solution.py:413
  172.5 3.4 %fusion.2.comp_ref = f32[768,384]{1,0:T(8,128)S(1)} fusion(bf16[16,96,384]{2,1,0:T(8,128)(2,1)} %all-to-all-done, bf16[16,384,768]{2,1,0:T(8,128)(2,1)} %bitcast.17), kind=kOutput, calls=%fused_computation.2 | convolution fusion | flops 905969664 | bytes 4718592 | tf_op jit(solution)/shard_map/dot_general | solution.py:402
  176.2 2.5 %shard_map.149 = bf16[16,72,192]{2,1,0:T(8,128)(2,1)} custom-call(s32[2]{0:T(128)S(1)} %add_convert_fusion.1.flag_ref, f32[16,64,100]{2,1,0:T(8,128)S(1)} %all-to-all-done.3.mel_ref, f32[8,100]{1,0:T(8,128)S(1)} %collective-permute-done.8.before_ref, f32[8,100]{1,0:T(8,128)S(1)} %collective-permute-done.9.after_ref, ...), custom_call_target="tpu_custom_call" | custom-call | flops 500000000 | bytes 2097152 | tf_op jit(solution)/shard_map/pallas_call | solution.py:46
  178.7 3.7 %all-to-all-start.4 = ((bf16[16,72,192]{2,1,0:T(8,128)(2,1)}), bf16[16,72,192]{2,1,0:T(8,128)(2,1)S(1)}, u32[]{:S(2)}, u32[]{:S(2)}) async-start(bf16[16,72,192]{2,1,0:T(8,128)(2,1)} %shard_map.149), calls=%async_computation.4 | async-start | bytes 1179648 | tf_op jit(solution)/shard_map/all_to_all | solution.py:275
  183.5 10.4 %all-to-all-done.4.up_ref = bf16[16,72,192]{2,1,0:T(8,128)(2,1)S(1)} async-done(((bf16[16,72,192]{2,1,0:T(8,128)(2,1)}), bf16[16,72,192]{2,1,0:T(8,128)(2,1)S(1)}, u32[]{:S(2)}, u32[]{:S(2)}) %all-to-all-start.4) | async-done | bytes 442400 | tf_op jit(solution)/shard_map/all_to_all | solution.py:275
  194.0 3.7 %copy-done.1 = bf16[6144,768]{1,0:T(8,128)(2,1)S(1)} copy-done((bf16[6144,768]{1,0:T(8,128)(2,1)S(1)}, bf16[6144,768]{1,0:T(8,128)(2,1)}, u32[]{:S(2)}) %copy-start.1) | copy-done | bytes 9437208
  197.6 4.5 %shard_map.150 = bf16[64,3072]{1,0:T(8,128)(2,1)S(1)} custom-call(s32[2]{0:T(128)S(1)} %add_convert_fusion.flag_ref, bf16[16,72,192]{2,1,0:T(8,128)(2,1)S(1)} %all-to-all-done.4.up_ref, f32[2,768]{1,0:T(2,128)S(1)} %copy-done.18, bf16[16,384,768]{2,1,0:T(8,128)(2,1)S(1)} %bitcast.18), custom_call_target="tpu_custom_call" | custom-call | flops 2000000000 | bytes 8388608 | tf_op jit(solution)/shard_map/pallas_call | solution.py:46
  202.1 1.0 reshape.28
  (65 shorter events, 9.6 us)
Async XLA Ops:
  7.2 127.3 %copy-start = (f32[1024,100]{0,1:T(8,128)S(1)}, f32[1024,100]{0,1:T(8,128)}, u32[]{:S(2)}) copy-start(f32[1024,100]{0,1:T(8,128)} %param.20) | copy-start | bytes 1228804
  7.2 165.3 %all-gather.3.cloned.1.call-start = ((), (), s32[]{:S(2)}) async-start(), calls=%async_computation.5 | async-start | bytes 10027008 | tf_op jit(solution)/shard_map/all_gather | solution.py:335
  7.2 1.0 copy-start.10
  9.2 3.9 %copy-start.8 = (bf16[1024,256]{1,0:T(8,128)(2,1)S(1)}, bf16[1024,256]{1,0:T(8,128)(2,1)}, u32[]{:S(2)}) copy-start(bf16[1024,256]{1,0:T(8,128)(2,1)} %up_ref.1) | copy-start | bytes 1572868
  9.2 3.9 %copy-start.9 = (bf16[256,1024]{1,0:T(8,128)(2,1)S(1)}, bf16[256,1024]{1,0:T(8,128)(2,1)}, u32[]{:S(2)}) copy-start(bf16[256,1024]{1,0:T(8,128)(2,1)} %down_ref.1) | copy-start | bytes 1572868
  9.2 1.0 copy-start.14
  10.2 0.9 copy-start.15
  13.1 1.3 copy-start.2
  13.2 59.5 %collective-permute-start.6 = (bf16[2048,256]{1,0:T(8,128)(2,1)S(1)}, bf16[2048,256]{1,0:T(8,128)(2,1)}, u32[]{:S(2)}, u32[]{:S(2)}) collective-permute-start(bf16[2048,256]{1,0:T(8,128)(2,1)S(1)} %shard_map.144.w0), channel_id=1, source_target_pairs={{0,130},{1,131},{2,128},{3,129},{4,134},{5,135},{6,132},{7,133},{8... | collective-permute-start | bytes 3145736 | tf_op jit(solution)/shard_map/ppermute | solution.py:346
  16.9 8.6 %copy-start.7 = (bf16[64,1024]{1,0:T(8,128)(2,1)S(1)}, bf16[64,1024]{1,0:T(8,128)(2,1)}, u32[]{:S(2)}) copy-start(bf16[64,1024]{1,0:T(8,128)(2,1)} %frames_ref.1) | copy-start | bytes 393220
  16.9 84.8 %all-to-all-start = ((bf16[16,96,384]{2,1,0:T(8,128)(2,1)}), bf16[16,96,384]{2,1,0:T(8,128)(2,1)}, u32[]{:S(2)}, u32[]{:S(2)}) async-start(bf16[16,96,384]{2,1,0:T(8,128)(2,1)} %shard_map.142), calls=%async_computation | async-start | bytes 2359296 | tf_op jit(solution)/shard_map/all_to_all | solution.py:275
  22.2 71.5 %copy-start.11 = (f32[8,1024]{1,0:T(8,128)S(1)}, f32[8,1024]{1,0:T(8,128)}, u32[]{:S(2)}) copy-start(f32[8,1024]{1,0:T(8,128)} %mod_ref.5) | copy-start | bytes 98308
  22.2 44.7 %collective-permute-start.1 = (bf16[256,1024]{1,0:T(8,128)(2,1)S(1)}, bf16[256,1024]{1,0:T(8,128)(2,1)S(1)}, u32[]{:S(2)}, u32[]{:S(2)}) collective-permute-start(bf16[256,1024]{1,0:T(8,128)(2,1)S(1)} %shard_map.140.w0), channel_id=1, source_target_pairs={{0,4},{1,5},{2,6},{3,7},{4,8},{5,9},{6,10},{7,11},{8,12},{9,13},{1... | collective-permute-start | bytes 1572872 | tf_op jit(solution)/shard_map/ppermute | solution.py:326
  24.1 45.3 %collective-permute-start.2 = (bf16[256,1024]{1,0:T(8,128)(2,1)S(1)}, bf16[256,1024]{1,0:T(8,128)(2,1)S(1)}, u32[]{:S(2)}, u32[]{:S(2)}) collective-permute-start(bf16[256,1024]{1,0:T(8,128)(2,1)S(1)} %shard_map.140.w0), channel_id=1, source_target_pairs={{0,12},{1,13},{2,14},{3,15},{4,0},{5,1},{6,2},{7,3},{8,4},{9,5},{1... | collective-permute-start | bytes 1572872 | tf_op jit(solution)/shard_map/ppermute | solution.py:327
  25.5 101.1 %collective-permute-start.5 = (bf16[2048,256]{1,0:T(8,128)(2,1)S(1)}, bf16[2048,256]{1,0:T(8,128)(2,1)}, u32[]{:S(2)}, u32[]{:S(2)}) collective-permute-start(bf16[2048,256]{1,0:T(8,128)(2,1)S(1)} %shard_map.144.w0), channel_id=1, source_target_pairs={{0,1},{1,0},{2,3},{3,2},{4,5},{5,4},{6,7},{7,6},{8,9},{9,8},{10,11... | collective-permute-start | bytes 3145736 | tf_op jit(solution)/shard_map/ppermute | solution.py:345
  25.5 57.4 %collective-permute-start = (bf16[64,1024]{1,0:T(8,128)(2,1)S(1)}, bf16[64,1024]{1,0:T(8,128)(2,1)}, u32[]{:S(2)}, u32[]{:S(2)}) collective-permute-start(bf16[64,1024]{1,0:T(8,128)(2,1)S(1)} %copy-done.7), channel_id=1, source_target_pairs={{0,4},{1,5},{2,6},{3,7},{4,8},{5,9},{6,10},{7,11},{8,12},{9,13},{1... | collective-permute-start | bytes 393224 | tf_op jit(solution)/shard_map/ppermute | solution.py:325
  66.9 5.9 %copy-start.3 = (bf16[256,1024]{1,0:T(8,128)(2,1)}, bf16[256,1024]{1,0:T(8,128)(2,1)S(1)}, u32[]{:S(2)}) copy-start(bf16[256,1024]{1,0:T(8,128)(2,1)S(1)} %collective-permute-done.1.w1) | copy-start | bytes 1572868
  66.9 26.1 %collective-permute-start.3 = (bf16[128,1024]{1,0:T(8,128)(2,1)S(1)}, bf16[128,1024]{1,0:T(8,128)(2,1)S(1)}, u32[]{:S(2)}, u32[]{:S(2)}) collective-permute-start(bf16[128,1024]{1,0:T(8,128)(2,1)S(1)} %slice.20), channel_id=1, source_target_pairs={{0,4},{1,5},{2,6},{3,7},{4,8},{5,9},{6,10},{7,11},{8,12},{9,13},{1... | collective-permute-start | bytes 786440 | tf_op jit(solution)/shard_map/ppermute | solution.py:338
  69.4 3.3 %copy-start.5 = (bf16[256,1024]{1,0:T(8,128)(2,1)}, bf16[256,1024]{1,0:T(8,128)(2,1)S(1)}, u32[]{:S(2)}) copy-start(bf16[256,1024]{1,0:T(8,128)(2,1)S(1)} %collective-permute-done.2.w2) | copy-start | bytes 1572868
  70.2 22.8 %collective-permute-start.4 = (bf16[128,1024]{1,0:T(8,128)(2,1)}, bf16[128,1024]{1,0:T(8,128)(2,1)S(1)}, u32[]{:S(2)}, u32[]{:S(2)}) collective-permute-start(bf16[128,1024]{1,0:T(8,128)(2,1)} %slice.21), channel_id=1, source_target_pairs={{0,12},{1,13},{2,14},{3,15},{4,0},{5,1},{6,2},{7,3},{8,4},{9,5},{1... | collective-permute-start | bytes 786440 | tf_op jit(solution)/shard_map/ppermute | solution.py:339
  72.7 53.9 %collective-permute-start.7 = (bf16[2048,256]{1,0:T(8,128)(2,1)}, bf16[2048,256]{1,0:T(8,128)(2,1)}, u32[]{:S(2)}, u32[]{:S(2)}) collective-permute-start(bf16[2048,256]{1,0:T(8,128)(2,1)} %collective-permute-done.6.w2), channel_id=1, source_target_pairs={{0,1},{1,0},{2,3},{3,2},{4,5},{5,4},{6,7},{7,6},{8,9},{9,8},{10,11... | collective-permute-start | bytes 3145736 | tf_op jit(solution)/shard_map/ppermute | solution.py:347
  93.7 1.1 copy-start.4
  94.8 1.1 copy-start.6
  95.8 0.9 copy-start.13
  130.8 3.8 %copy-start.19 = (bf16[1024,100]{0,1:T(8,128)(2,1)S(1)}, bf16[1024,100]{0,1:T(8,128)(2,1)}, u32[]{:S(2)}) copy-start(bf16[1024,100]{0,1:T(8,128)(2,1)} %param.19) | copy-start | bytes 614404
  130.9 11.7 %all-to-all-start.2 = ((bf16[4,64,1024]{2,1,0:T(8,128)(2,1)}), bf16[4,64,1024]{2,1,0:T(8,128)(2,1)S(1)}, u32[]{:S(2)}, u32[]{:S(2)}) async-start(bf16[4,64,1024]{2,1,0:T(8,128)(2,1)} %bitcast.3), calls=%async_computation.2 | async-start | bytes 1048576 | tf_op jit(solution)/shard_map/all_to_all | solution.py:275
  143.7 14.4 %all-to-all-start.3 = ((f32[16,64,100]{2,1,0:T(8,128)}), f32[16,64,100]{2,1,0:T(8,128)S(1)}, u32[]{:S(2)}, u32[]{:S(2)}) async-start(f32[16,64,100]{2,1,0:T(8,128)} %shard_map.146), calls=%async_computation.3 | async-start | bytes 1048576 | tf_op jit(solution)/shard_map/all_to_all | solution.py:275
  158.1 18.2 %collective-permute-start.8 = (f32[8,100]{1,0:T(8,128)S(1)}, f32[8,100]{1,0:T(8,128)S(1)}, u32[]{:S(2)}, u32[]{:S(2)}) collective-permute-start(f32[8,100]{1,0:T(8,128)S(1)} %get-tuple-element.23), channel_id=1, source_target_pairs={{0,16},{16,32},{32,48},{48,64},{64,80},{80,96},{96,112},{112,128},... | collective-permute-start | bytes 9608 | tf_op jit(solution)/shard_map/ppermute | solution.py:412
  162.7 13.6 %collective-permute-start.9 = (f32[8,100]{1,0:T(8,128)S(1)}, f32[8,100]{1,0:T(8,128)S(1)}, u32[]{:S(2)}, u32[]{:S(2)}) collective-permute-start(f32[8,100]{1,0:T(8,128)S(1)} %get-tuple-element.22), channel_id=1, source_target_pairs={{16,0},{32,16},{48,32},{64,48},{80,64},{96,80},{112,96},{128,112},... | collective-permute-start | bytes 9608 | tf_op jit(solution)/shard_map/ppermute | solution.py:413
  178.7 15.2 %copy-start.18 = (f32[2,768]{1,0:T(2,128)S(1)}, f32[2,768]{1,0:T(2,128)}, u32[]{:S(2)}) copy-start(f32[2,768]{1,0:T(2,128)} %alpha_ref.1) | copy-start | bytes 18436
  178.7 15.2 %all-to-all-start.4 = ((bf16[16,72,192]{2,1,0:T(8,128)(2,1)}), bf16[16,72,192]{2,1,0:T(8,128)(2,1)S(1)}, u32[]{:S(2)}, u32[]{:S(2)}) async-start(bf16[16,72,192]{2,1,0:T(8,128)(2,1)} %shard_map.149), calls=%async_computation.4 | async-start | bytes 1179648 | tf_op jit(solution)/shard_map/all_to_all | solution.py:275
  194.0 3.7 %copy-start.1 = (bf16[6144,768]{1,0:T(8,128)(2,1)S(1)}, bf16[6144,768]{1,0:T(8,128)(2,1)}, u32[]{:S(2)}) copy-start(bf16[6144,768]{1,0:T(8,128)(2,1)} %all-gather.3.cloned.1.call-done) | copy-start | bytes 28311556
  (3 other events, 2.5 us)
Sparse Core Ops, SparseCore 0:
  13.2 87.4 all-gather.2

commit v3 on v2

--- a/solution.py
+++ b/solution.py
@@ -58,10 +58,11 @@
     return pl.CostEstimate(flops=flops, bytes_accessed=nbytes, transcendentals=trans)
 
 
-def attention_weights_kernel(w_ref, o_ref, out_ref):
-    for k in range(3):
-        out_ref[64 * k : 64 * k + 64, :] = w_ref[k]
-    out_ref[192:256, :] = o_ref[...]
+def attention_weights_kernel(w_ref, o_ref, a_ref, b_ref):
+    a_ref[0:64, :] = w_ref[0]
+    a_ref[64:128, :] = w_ref[1]
+    b_ref[0:64, :] = w_ref[2]
+    b_ref[64:128, :] = o_ref[...]
 
 
 def mlp_weights_kernel(up_ref, down_ref, out_ref):
@@ -89,19 +90,19 @@
 
 
 def attention_kernel(
-    flag_ref, own_ref, back_ref, mod_ref, w0, w1, w2, w3a, w3b, out_ref, heads, w_out
+    flag_ref, own_ref, back_ref, mod_ref, a0, b0, a1, b1, a2, b2, a3, b3, out_ref, heads, w_out
 ):
     first = flag_ref[0] > 0
     scale = 1.0 / math.sqrt(HEAD_DIM)
     shift, gain = mod_ref[0:1, :], mod_ref[1:2, :]
     own = norm_rows(own_ref[...], shift, gain).astype(bf16)
     back = norm_rows(back_ref[...], shift, gain).astype(bf16)
-    for h, (wa, wb, base) in enumerate(((w0, w0, 128), (w1, w1, 128), (w2, w2, 128), (w3a, w3b, 0))):
+    for h, (wa, wb) in enumerate(((a0, b0), (a1, b1), (a2, b2), (a3, b3))):
         qk = mm_t(own, wa[0:128, :]).astype(bf16)
         q, k = qk[:, 0:64], qk[:, 64:128]
-        v = mm_t(own, wb[base : base + 64, :]).astype(bf16)
+        v = mm_t(own, wb[0:64, :]).astype(bf16)
         kb = mm_t(back, wa[64:128, :]).astype(bf16)
-        vb = mm_t(back, wb[base : base + 64, :]).astype(bf16)
+        vb = mm_t(back, wb[0:64, :]).astype(bf16)
         s_own = mm_t(q, k) * scale
         s_back = mm_t(q, kb) * scale
         s_back = jnp.where(first, -1e30, s_back)
@@ -115,7 +116,7 @@
         p_own = (e_own * inv).astype(bf16)
         p_back = (e_back * inv).astype(bf16)
         heads[:, 64 * h : 64 * h + 64] = (mm(p_own, v) + mm(p_back, vb)).astype(bf16)
-        w_out[64 * h : 64 * h + 64, :] = wb[base + 64 : base + 128, :]
+        w_out[64 * h : 64 * h + 64, :] = wb[64:128, :]
     out_ref[...] = mm(heads[...], w_out[...]).astype(bf16)
 
 
@@ -224,7 +225,17 @@
 ROWS = 72
 
 
-def conv_kernel(flag_ref, up_ref, alpha_ref, w_ref, out_ref, planes):
+def conv_kernel(flag_ref, up_ref, alpha_ref, w_hbm, out_ref, planes, w_ref, sem):
+    copies = [
+        pltpu.make_async_copy(
+            w_hbm.at[:, pl.ds(96 + 144 * k, 144), :],
+            w_ref.at[:, pl.ds(144 * k, 144), :],
+            sem.at[k],
+        )
+        for k in range(2)
+    ]
+    for c in copies:
+        c.start()
     first = flag_ref[0] > 0
     last = flag_ref[1] > 0
     row = lax.broadcasted_iota(jnp.int32, (ROWS, 768), 0)
@@ -249,7 +260,8 @@
         ups.append(u)
         acts.append(snake_act(u, a1, i1).astype(bf16))
     act = jnp.concatenate(acts, axis=0)
-    y = [mm(act, weight(96, tap)) for tap in range(3)]
+    copies[0].wait()
+    y = [mm(act, weight(0, tap)) for tap in range(3)]
     y = [[v[ROWS * p : ROWS * p + ROWS] for p in range(4)] for v in y]
     acts = []
     for p in range(4):
@@ -258,7 +270,8 @@
         inner = before + y[1][p] + after
         acts.append(jnp.where(outside, 0.0, snake_act(inner, a2, i2)).astype(bf16))
     act = jnp.concatenate(acts, axis=0)
-    y = [mm(act, weight(240, tap)) for tap in range(3)]
+    copies[1].wait()
+    y = [mm(act, weight(144, tap)) for tap in range(3)]
     y = [[v[ROWS * p : ROWS * p + ROWS] for p in range(4)] for v in y]
     for p in range(4):
         before = y[0][p - 1] if p >= 1 else shifted(y[0][3], 1)
@@ -271,8 +284,8 @@
     return lax.all_gather(value, "sub", axis=0, tiled=True, axis_index_groups=groups)
 
 
-def exchange(value, groups=None):
-    return lax.all_to_all(value, "sub", 0, 0, tiled=True, axis_index_groups=groups)
+def exchange(value, groups=None, axis="sub"):
+    return lax.all_to_all(value, axis, 0, 0, tiled=True, axis_index_groups=groups)
 
 
 def device(y_hi, z, x, y_lo, core):
@@ -286,6 +299,11 @@
     for x in range(4)
     for y in range(2)
     for c in range(2)
+]
+OTHER_GROUPS = [
+    [device(y ^ side, z, x, y, c) for x in range(4) for y in range(2) for c in range(2)]
+    for side in range(2)
+    for z in range(8)
 ]
 
 
@@ -316,27 +334,29 @@
 
     to_right = [(i, (i + 4) % 16) for i in range(16)]
     to_left = [(i, (i - 4) % 16) for i in range(16)]
-    w_own = whole(
+    own_a, own_b = whole(
         attention_weights_kernel,
-        shape((256, 1024), bf16),
+        (shape((128, 1024), bf16), shape((128, 1024), bf16)),
         (jnp.swapaxes(w_project, 1, 2), w_heads_out),
         cost=cost_of(0, 1 << 20),
     )
     back_frames = lax.ppermute(frames, both, [(i, i + 4) for i in range(n_all - 4)])
-    from_left = lax.ppermute(w_own, "sub", to_right)
-    from_right = lax.ppermute(w_own, "sub", to_left)
+    left_a = lax.ppermute(own_a, "sub", to_right)
+    right_b = lax.ppermute(own_b, "sub", to_left)
+    left_b = lax.ppermute(own_b, "sub", to_right)
+    right_a = lax.ppermute(own_a, "sub", to_left)
+    far_a = lax.ppermute(left_a, "sub", to_right)
+    far_b = lax.ppermute(right_b, "sub", to_left)
 
     w_voc = whole(
         vocoder_weights_kernel,
         shape((384, 768), bf16),
-        lax.optimization_barrier((w_prelude, w_dilated, w_plain, w_own))[:3],
+        lax.optimization_barrier((w_prelude, w_dilated, w_plain, own_a))[:3],
         cost=cost_of(0, 2 << 20),
     )
     w_voc = lax.all_gather(w_voc, "sub", axis=0, tiled=False)
 
     block = gather(frames, J_GROUPS)
-    far_a = lax.ppermute(from_left[:128], "sub", to_right)
-    far_b = lax.ppermute(from_right[128:], "sub", to_left)
     back = gather(back_frames, J_GROUPS)
 
     own_mlp = whole(
@@ -359,9 +379,12 @@
             block,
             back,
             modulation,
-            w_own,
-            from_left,
-            from_right,
+            own_a,
+            own_b,
+            left_a,
+            left_b,
+            right_a,
+            right_b,
             far_a,
             far_b,
         ),
@@ -369,7 +392,7 @@
         cost=cost_of(10**9, 4 << 20, 1 << 19),
         smem=1,
     )
-    ups = exchange(ups)
+    ups = exchange(ups, OTHER_GROUPS, both)
     partial, ups = lax.optimization_barrier((partial, ups))
     parts = exchange(partial, J_GROUPS)
     mixed_rows, own_norm = whole(
@@ -429,15 +452,22 @@
     up_x = exchange(windows)
 
     flags = jnp.stack([here_index == 0, here_index == n_all - 1]).astype(jnp.int32)
-    out = whole(
+    out = pl.pallas_call(
         conv_kernel,
-        shape((64, 3072), bf16),
-        (flags, up_x, snake_alpha, w_voc),
-        scratch=[pltpu.VMEM((4, ROWS, 768), bf16)],
-        cost=cost_of(2 * 10**9, 8 << 20, 1 << 18),
-        smem=1,
-        vmem=32,
-    )
+        out_shape=shape((64, 3072), bf16),
+        in_specs=[pl.BlockSpec(memory_space=pltpu.SMEM)]
+        + vmem_specs(2)
+        + [pl.BlockSpec(memory_space=pltpu.MemorySpace.HBM)],
+        out_specs=pl.BlockSpec(memory_space=pltpu.VMEM),
+        scratch_shapes=[
+            pltpu.VMEM((4, ROWS, 768), bf16),
+            pltpu.VMEM((16, 288, 768), bf16),
+            pltpu.SemaphoreType.DMA((2,)),
+        ],
+        compiler_params=pltpu.CompilerParams(vmem_limit_bytes=54 << 20),
+        cost_estimate=cost_of(2 * 10**9, 8 << 20, 1 << 18),
+        name="convolutions",
+    )(flags, up_x, snake_alpha, w_voc)
     return (mel_next, out.reshape(256, 768))
 
 

time: 211 us -> 208 us (0.986)
  local copies, waits for them, and re-layouts: 16 us -> 11.5 us
  blocking collectives: 44.9 us -> 48.8 us
  waiting for transfers between devices: 67.7 us -> 63.9 us
  Pallas kernels: 21.4 us -> 25.2 us
  starting transfers between devices: 42.1 us -> 39.3 us
    ppermute x4 -> x6, waiting for transfers between devices: 38.8 us -> 4.52 us  [the longest x1 4.51 us: program(): right_a = lax.ppermute(own_a, 'sub', to_left)]
    ppermute x1, waiting for transfers between devices: 0.01 us -> 31.3 us  [program(): lax.ppermute(frames, both, [(i, i + 4) for i in range(n_all - 4)])]
    pallas_call x0 -> x1, Pallas kernels: none -> 7.17 us  [program(): pl.pallas_call(conv_kernel, out_shape=shape((64, 3072), bf16), in_specs=[...]
    unnamed x43 -> x39, local copies, waits for them, and re-layouts: 14.2 us -> 9.45 us
    all_gather x3, blocking collectives: 33.7 us -> 37.4 us  [gather(): lax.all_gather(value, 'sub', axis=0, tiled=True, axis_index_groups=groups)]
    pallas_call x11 -> x10, Pallas kernels: 21.4 us -> 18.1 us  [whole(): pl.pallas_call(kernel, out_shape=out_shapes, in_specs=[pl.BlockSpec(memor...]
    ppermute x1, starting transfers between devices: 9.79 us -> 7.6 us  [program(): lax.ppermute(mel_all[0, :8], 'tm', [(i + 1, i) for i in range(n_tm - 1)])]
    ppermute x4 -> x6, starting transfers between devices: 8.36 us -> 9.56 us  [the longest x1 2.48 us: program(): left_b = lax.ppermute(own_b, 'sub', to_right)]
  transfers between devices with their start and end apart: 15 -> 17, of which waited for: 4 -> 5; matrix products, arithmetic and copies ran while one was open for 3% -> 3% of each run, Pallas kernels for 6% -> 7%
where the time goes in v3:
time: 208 us; the launch traced here: 207 us
  waiting for transfers between devices  63.9 us (31%)
  blocking collectives  48.8 us (23%)
  starting transfers between devices  39.3 us (19%)
  Pallas kernels  25.2 us (12%)
  between operations  14.3 us (7%)
  local copies, waits for them, and re-layouts  11.5 us (6%)
  matrix products  3.39 us (2%)
    all_gather x3, blocking collectives, gather(): lax.all_gather(value, 'sub', axis=0, tiled=True, axis_index_groups=groups)  37.4 us
    ppermute x1, waiting for transfers between devices, program(): lax.ppermute(frames, both, [(i, i + 4) for i in range(n_all - 4)])  31.3 us
    all_to_all x4, waiting for transfers between devices, exchange(): lax.all_to_all(value, axis, 0, 0, tiled=True, axis_index_groups=groups)  28 us
    pallas_call x10, Pallas kernels, whole(): pl.pallas_call(kernel, out_shape=out_shapes, in_specs=[pl.BlockSpec(memor...  18.1 us
    all_to_all x4, starting transfers between devices, exchange(): lax.all_to_all(value, axis, 0, 0, tiled=True, axis_index_groups=groups)  15.9 us
    all_to_all x1, blocking collectives, exchange(): lax.all_to_all(value, axis, 0, 0, tiled=True, axis_index_groups=groups)  11.4 us
    unnamed x39, local copies, waits for them, and re-layouts  9.45 us
    ppermute x1, starting transfers between devices, program(): lax.ppermute(mel_all[0, :8], 'tm', [(i + 1, i) for i in range(n_tm - 1)])  7.6 us
  transfers between devices with their start and end apart: 17, of which 5 were waited for; matrix products, arithmetic and copies ran while one was open for 3% of the time, Pallas kernels for 7%

profile of v3, /device:TPU:16, one launch (start us, length us, event | category | flops | bytes accessed | tf_op | source)
XLA Modules:
  0.0 207.2 jit_solution(17469454692279604868)
XLA Ops:
  7.3 1.1 copy-done.5
  12.1 1.0 shard_map.147
  14.4 2.5 %shard_map.142 = bf16[16,96,384]{2,1,0:T(8,128)(2,1)} custom-call(bf16[8,96,768]{2,1,0:T(8,128)(2,1)S(1)} %copy-done.1), custom_call_target="tpu_custom_call" | custom-call | bytes 3145728 | tf_op jit(solution)/shard_map/pallas_call | solution.py:46
  16.8 4.9 %all-to-all-start = ((bf16[16,96,384]{2,1,0:T(8,128)(2,1)}), bf16[16,96,384]{2,1,0:T(8,128)(2,1)}, u32[]{:S(2)}, u32[]{:S(2)}) async-start(bf16[16,96,384]{2,1,0:T(8,128)(2,1)} %shard_map.142), calls=%async_computation | async-start | bytes 2359296 | tf_op jit(solution)/shard_map/all_to_all | solution.py:288
  21.8 2.0 collective-permute-start.1
  23.8 1.4 collective-permute-start.4
  25.1 1.9 collective-permute-start.3
  27.0 2.0 collective-permute-start
  29.1 31.3 %collective-permute-done = bf16[64,1024]{1,0:T(8,128)(2,1)S(1)} collective-permute-done((bf16[64,1024]{1,0:T(8,128)(2,1)S(1)}, bf16[64,1024]{1,0:T(8,128)(2,1)S(1)}, u32[]{:S(2)}, u32[]{:S(2)}) %collective-permute-start) | collective-permute-done | bytes 131104 | tf_op jit(solution)/shard_map/ppermute | solution.py:343
  60.3 2.5 %collective-permute-start.2 = (bf16[128,1024]{1,0:T(8,128)(2,1)S(1)}, bf16[128,1024]{1,0:T(8,128)(2,1)}, u32[]{:S(2)}, u32[]{:S(2)}) collective-permute-start(bf16[128,1024]{1,0:T(8,128)(2,1)S(1)} %get-tuple-element.14.b0), channel_id=1, source_target_pairs={{0,4},{1,5},{2,6},{3,7},{4,8},{5,9},{6,10},{7,11},{8,12},{9,13},{1... | collective-permute-start | bytes 786440 | tf_op jit(solution)/shard_map/ppermute | solution.py:346
  62.8 1.1 collective-permute-start.5
  64.0 4.5 %collective-permute-done.3.a2 = bf16[128,1024]{1,0:T(8,128)(2,1)S(1)} collective-permute-done((bf16[128,1024]{1,0:T(8,128)(2,1)S(1)}, bf16[128,1024]{1,0:T(8,128)(2,1)S(1)}, u32[]{:S(2)}, u32[]{:S(2)}) %collective-permute-start.3) | collective-permute-done | bytes 262176 | tf_op jit(solution)/shard_map/ppermute | solution.py:347
  69.3 13.6 %all_gather.15.own_ref = bf16[256,1024]{1,0:T(8,128)(2,1)S(1)} all-gather(bf16[64,1024]{1,0:T(8,128)(2,1)S(1)} %copy-done.2), channel_id=1, replica_groups={{0,1,2,3},{4,5,6,7},{8,9,10,11},{12,13,14,15},{16,17,18,19},{20,21,22,2..., dimensions={0}, use_global_device_ids=true | all-gather | bytes 655360 | tf_op jit(solution)/shard_map/all_gather | solution.py:284
  82.8 10.4 %all_gather.16.back_ref = bf16[256,1024]{1,0:T(8,128)(2,1)S(1)} all-gather(bf16[64,1024]{1,0:T(8,128)(2,1)} %copy-done.17), channel_id=1, replica_groups={{0,1,2,3},{4,5,6,7},{8,9,10,11},{12,13,14,15},{16,17,18,19},{20,21,22,2..., dimensions={0}, use_global_device_ids=true | all-gather | bytes 655360 | tf_op jit(solution)/shard_map/all_gather | solution.py:284
  95.1 6.0 %shard_map.141 = bf16[256,1024]{1,0:T(8,128)(2,1)S(1)} custom-call(s32[1]{0:T(128)} %bitcast.flag_ref, bf16[256,1024]{1,0:T(8,128)(2,1)S(1)} %all_gather.15.own_ref, bf16[256,1024]{1,0:T(8,128)(2,1)S(1)} %all_gather.16.back_ref, f32[8,1024]{1,0:T(8,128)S(1)} %copy-done.6, bf16[128,1024]{1,0:T(8,128)(2,1)S(1)} %get-tuple-element.13.a0, ...), custom_call_target="tpu_custom_call" | custom-call | flops 1000000000 | bytes 4194304 | tf_op jit(solution)/shard_map/pallas_call | solution.py:46
  101.2 11.4 %all_to_all.33.parts_ref = bf16[4,64,1024]{2,1,0:T(8,128)(2,1)S(1)} all-to-all(bf16[4,64,1024]{2,1,0:T(8,128)(2,1)S(1)} %bitcast.18), channel_id=1, replica_groups={{0,1,2,3},{4,5,6,7},{8,9,10,11},{12,13,14,15},{16,17,18,19},{20,21,22,2..., dimensions={0} | all-to-all | bytes 1048576 | tf_op jit(solution)/shard_map/all_to_all | solution.py:288
  112.8 13.4 %all_gather.17.h_ref = bf16[256,1024]{1,0:T(8,128)(2,1)S(1)} all-gather(bf16[64,1024]{1,0:T(8,128)(2,1)S(1)} %get-tuple-element.16), channel_id=1, replica_groups={{0,4,8,12},{1,5,9,13},{2,6,10,14},{3,7,11,15},{16,20,24,28},{17,21,25,2..., dimensions={0}, use_global_device_ids=true | all-gather | bytes 655360 | tf_op jit(solution)/shard_map/all_gather | solution.py:284
  126.3 4.2 %shard_map.145 = bf16[256,1024]{1,0:T(8,128)(2,1)} custom-call(bf16[256,1024]{1,0:T(8,128)(2,1)S(1)} %all_gather.17.h_ref, bf16[2048,256]{1,0:T(8,128)(2,1)S(1)} %shard_map.144.w0, bf16[2048,256]{1,0:T(8,128)(2,1)} %collective-permute-done.7.w1, bf16[2048,256]{1,0:T(8,128)(2,1)} %collective-permute-done.8.w2, bf16[2048,256]{1,0:T(8,128)(2,1)} %collective-permute-done.9.w3), custom_call_target="tpu_custom_call" | custom-call | flops 1100000000 | bytes 5242880 | tf_op jit(solution)/shard_map/pallas_call | solution.py:46
  130.5 3.6 %all-to-all-start.2 = ((bf16[4,64,1024]{2,1,0:T(8,128)(2,1)}), bf16[4,64,1024]{2,1,0:T(8,128)(2,1)S(1)}, u32[]{:S(2)}, u32[]{:S(2)}) async-start(bf16[4,64,1024]{2,1,0:T(8,128)(2,1)} %bitcast.3), calls=%async_computation.2 | async-start | bytes 1048576 | tf_op jit(solution)/shard_map/all_to_all | solution.py:288
  134.5 7.7 %all-to-all-done.2.parts_ref = bf16[4,64,1024]{2,1,0:T(8,128)(2,1)S(1)} async-done(((bf16[4,64,1024]{2,1,0:T(8,128)(2,1)}), bf16[4,64,1024]{2,1,0:T(8,128)(2,1)S(1)}, u32[]{:S(2)}, u32[]{:S(2)}) %all-to-all-start.2) | async-done | bytes 524320 | tf_op jit(solution)/shard_map/all_to_all | solution.py:288
  142.2 1.2 shard_map.146
  143.3 3.6 %all-to-all-start.3 = ((f32[16,64,100]{2,1,0:T(8,128)}), f32[16,64,100]{2,1,0:T(8,128)S(1)}, u32[]{:S(2)}, u32[]{:S(2)}) async-start(f32[16,64,100]{2,1,0:T(8,128)} %shard_map.146), calls=%async_computation.3 | async-start | bytes 1048576 | tf_op jit(solution)/shard_map/all_to_all | solution.py:288
  147.0 10.7 %all-to-all-done.3.mel_ref = f32[16,64,100]{2,1,0:T(8,128)S(1)} async-done(((f32[16,64,100]{2,1,0:T(8,128)}), f32[16,64,100]{2,1,0:T(8,128)S(1)}, u32[]{:S(2)}, u32[]{:S(2)}) %all-to-all-start.3) | async-done | bytes 409632 | tf_op jit(solution)/shard_map/all_to_all | solution.py:288
  157.7 3.6 %collective-permute-start.10 = (f32[8,100]{1,0:T(8,128)S(1)}, f32[8,100]{1,0:T(8,128)S(1)}, u32[]{:S(2)}, u32[]{:S(2)}) collective-permute-start(f32[8,100]{1,0:T(8,128)S(1)} %get-tuple-element.27), channel_id=1, source_target_pairs={{0,16},{16,32},{32,48},{48,64},{64,80},{80,96},{96,112},{112,128},... | collective-permute-start | bytes 9608 | tf_op jit(solution)/shard_map/ppermute | solution.py:435
  161.3 7.6 %collective-permute-start.11 = (f32[8,100]{1,0:T(8,128)S(1)}, f32[8,100]{1,0:T(8,128)S(1)}, u32[]{:S(2)}, u32[]{:S(2)}) collective-permute-start(f32[8,100]{1,0:T(8,128)S(1)} %get-tuple-element.26), channel_id=1, source_target_pairs={{16,0},{32,16},{48,32},{64,48},{80,64},{96,80},{112,96},{128,112},... | collective-permute-start | bytes 9608 | tf_op jit(solution)/shard_map/ppermute | solution.py:436
  169.0 3.4 %fusion.2.comp_ref = f32[768,384]{1,0:T(8,128)S(1)} fusion(bf16[16,96,384]{2,1,0:T(8,128)(2,1)} %all-to-all-done, bf16[16,384,768]{2,1,0:T(8,128)(2,1)} %bitcast.20), kind=kOutput, calls=%fused_computation.2 | convolution fusion | flops 905969664 | bytes 4718592 | tf_op jit(solution)/shard_map/dot_general | solution.py:425
  172.7 2.5 %shard_map.149 = bf16[16,72,192]{2,1,0:T(8,128)(2,1)} custom-call(s32[2]{0:T(128)S(1)} %add_convert_fusion.1.flag_ref, f32[16,64,100]{2,1,0:T(8,128)S(1)} %all-to-all-done.3.mel_ref, f32[8,100]{1,0:T(8,128)S(1)} %collective-permute-done.10.before_ref, f32[8,100]{1,0:T(8,128)S(1)} %collective-permute-done.11.after_ref, ...), custom_call_target="tpu_custom_call" | custom-call | flops 500000000 | bytes 2097152 | tf_op jit(solution)/shard_map/pallas_call | solution.py:46
  175.2 3.8 %all-to-all-start.4 = ((bf16[16,72,192]{2,1,0:T(8,128)(2,1)}), bf16[16,72,192]{2,1,0:T(8,128)(2,1)S(1)}, u32[]{:S(2)}, u32[]{:S(2)}) async-start(bf16[16,72,192]{2,1,0:T(8,128)(2,1)} %shard_map.149), calls=%async_computation.4 | async-start | bytes 1179648 | tf_op jit(solution)/shard_map/all_to_all | solution.py:288
  179.7 1.0 copy.17
  180.7 9.6 %all-to-all-done.4.up_ref = bf16[16,72,192]{2,1,0:T(8,128)(2,1)S(1)} async-done(((bf16[16,72,192]{2,1,0:T(8,128)(2,1)}), bf16[16,72,192]{2,1,0:T(8,128)(2,1)S(1)}, u32[]{:S(2)}, u32[]{:S(2)}) %all-to-all-start.4) | async-done | bytes 442400 | tf_op jit(solution)/shard_map/all_to_all | solution.py:288
  191.2 7.2 %convolutions.1 = bf16[64,3072]{1,0:T(8,128)(2,1)} custom-call(s32[2]{0:T(128)} %add_convert_fusion.flag_ref, bf16[16,72,192]{2,1,0:T(8,128)(2,1)} %copy-done.15, f32[2,768]{1,0:T(2,128)} %alpha_ref.1, bf16[16,384,768]{2,1,0:T(8,128)(2,1)} %bitcast.21), custom_call_target="tpu_custom_call" | custom-call | flops 2000000000 | bytes 8388608 | tf_op jit(solution)/shard_map/convolutions/pallas_call | solution.py:455
  198.3 2.0 reshape.28
  (63 shorter events, 10.3 us)
Async XLA Ops:
  7.2 126.9 %copy-start = (f32[1024,100]{0,1:T(8,128)S(1)}, f32[1024,100]{0,1:T(8,128)}, u32[]{:S(2)}) copy-start(f32[1024,100]{0,1:T(8,128)} %param.20) | copy-start | bytes 1228804
  7.2 5.9 %copy-start.3 = (bf16[1024,256]{1,0:T(8,128)(2,1)S(1)}, bf16[1024,256]{1,0:T(8,128)(2,1)}, u32[]{:S(2)}) copy-start(bf16[1024,256]{1,0:T(8,128)(2,1)} %up_ref.1) | copy-start | bytes 1572868
  7.2 5.9 %copy-start.4 = (bf16[256,1024]{1,0:T(8,128)(2,1)S(1)}, bf16[256,1024]{1,0:T(8,128)(2,1)}, u32[]{:S(2)}) copy-start(bf16[256,1024]{1,0:T(8,128)(2,1)} %down_ref.1) | copy-start | bytes 1572868
  7.2 161.8 %all-gather.3.cloned.1.call-start = ((), (), s32[]{:S(2)}) async-start(), calls=%async_computation.5 | async-start | bytes 10027008 | tf_op jit(solution)/shard_map/all_gather | solution.py:357
  7.2 1.1 copy-start.5
  9.3 0.9 copy-start.11
  10.2 0.9 copy-start.12
  13.1 1.3 copy-start.1
  13.2 56.1 %collective-permute-start.8 = (bf16[2048,256]{1,0:T(8,128)(2,1)S(1)}, bf16[2048,256]{1,0:T(8,128)(2,1)}, u32[]{:S(2)}, u32[]{:S(2)}) collective-permute-start(bf16[2048,256]{1,0:T(8,128)(2,1)S(1)} %shard_map.144.w0), channel_id=1, source_target_pairs={{0,130},{1,131},{2,128},{3,129},{4,134},{5,135},{6,132},{7,133},{8... | collective-permute-start | bytes 3145736 | tf_op jit(solution)/shard_map/ppermute | solution.py:366
  16.8 10.2 %copy-start.2 = (bf16[64,1024]{1,0:T(8,128)(2,1)S(1)}, bf16[64,1024]{1,0:T(8,128)(2,1)}, u32[]{:S(2)}) copy-start(bf16[64,1024]{1,0:T(8,128)(2,1)} %frames_ref.1) | copy-start | bytes 393220
  16.8 84.3 %all-to-all-start = ((bf16[16,96,384]{2,1,0:T(8,128)(2,1)}), bf16[16,96,384]{2,1,0:T(8,128)(2,1)}, u32[]{:S(2)}, u32[]{:S(2)}) async-start(bf16[16,96,384]{2,1,0:T(8,128)(2,1)} %shard_map.142), calls=%async_computation | async-start | bytes 2359296 | tf_op jit(solution)/shard_map/all_to_all | solution.py:288
  21.8 71.4 %copy-start.6 = (f32[8,1024]{1,0:T(8,128)S(1)}, f32[8,1024]{1,0:T(8,128)}, u32[]{:S(2)}) copy-start(f32[8,1024]{1,0:T(8,128)} %mod_ref.5) | copy-start | bytes 98308
  21.8 41.0 %collective-permute-start.1 = (bf16[128,1024]{1,0:T(8,128)(2,1)S(1)}, bf16[128,1024]{1,0:T(8,128)(2,1)S(1)}, u32[]{:S(2)}, u32[]{:S(2)}) collective-permute-start(bf16[128,1024]{1,0:T(8,128)(2,1)S(1)} %get-tuple-element.13.a0), channel_id=1, source_target_pairs={{0,4},{1,5},{2,6},{3,7},{4,8},{5,9},{6,10},{7,11},{8,12},{9,13},{1... | collective-permute-start | bytes 786440 | tf_op jit(solution)/shard_map/ppermute | solution.py:344
  23.8 39.1 %collective-permute-start.4 = (bf16[128,1024]{1,0:T(8,128)(2,1)S(1)}, bf16[128,1024]{1,0:T(8,128)(2,1)S(1)}, u32[]{:S(2)}, u32[]{:S(2)}) collective-permute-start(bf16[128,1024]{1,0:T(8,128)(2,1)S(1)} %get-tuple-element.14.b0), channel_id=1, source_target_pairs={{0,12},{1,13},{2,14},{3,15},{4,0},{5,1},{6,2},{7,3},{8,4},{9,5},{1... | collective-permute-start | bytes 786440 | tf_op jit(solution)/shard_map/ppermute | solution.py:345
  25.1 43.4 %collective-permute-start.3 = (bf16[128,1024]{1,0:T(8,128)(2,1)S(1)}, bf16[128,1024]{1,0:T(8,128)(2,1)S(1)}, u32[]{:S(2)}, u32[]{:S(2)}) collective-permute-start(bf16[128,1024]{1,0:T(8,128)(2,1)S(1)} %get-tuple-element.13.a0), channel_id=1, source_target_pairs={{0,12},{1,13},{2,14},{3,15},{4,0},{5,1},{6,2},{7,3},{8,4},{9,5},{1... | collective-permute-start | bytes 786440 | tf_op jit(solution)/shard_map/ppermute | solution.py:347
  27.0 33.3 %collective-permute-start = (bf16[64,1024]{1,0:T(8,128)(2,1)S(1)}, bf16[64,1024]{1,0:T(8,128)(2,1)S(1)}, u32[]{:S(2)}, u32[]{:S(2)}) collective-permute-start(bf16[64,1024]{1,0:T(8,128)(2,1)S(1)} %copy-done.2), channel_id=1, source_target_pairs={{0,4},{1,5},{2,6},{3,7},{4,8},{5,9},{6,10},{7,11},{8,12},{9,13},{1... | collective-permute-start | bytes 393224 | tf_op jit(solution)/shard_map/ppermute | solution.py:343
  60.3 8.9 %copy-start.17 = (bf16[64,1024]{1,0:T(8,128)(2,1)}, bf16[64,1024]{1,0:T(8,128)(2,1)S(1)}, u32[]{:S(2)}) copy-start(bf16[64,1024]{1,0:T(8,128)(2,1)S(1)} %collective-permute-done) | copy-start | bytes 393220
  60.3 32.9 %collective-permute-start.2 = (bf16[128,1024]{1,0:T(8,128)(2,1)S(1)}, bf16[128,1024]{1,0:T(8,128)(2,1)}, u32[]{:S(2)}, u32[]{:S(2)}) collective-permute-start(bf16[128,1024]{1,0:T(8,128)(2,1)S(1)} %get-tuple-element.14.b0), channel_id=1, source_target_pairs={{0,4},{1,5},{2,6},{3,7},{4,8},{5,9},{6,10},{7,11},{8,12},{9,13},{1... | collective-permute-start | bytes 786440 | tf_op jit(solution)/shard_map/ppermute | solution.py:346
  62.8 63.4 %collective-permute-start.7 = (bf16[2048,256]{1,0:T(8,128)(2,1)S(1)}, bf16[2048,256]{1,0:T(8,128)(2,1)}, u32[]{:S(2)}, u32[]{:S(2)}) collective-permute-start(bf16[2048,256]{1,0:T(8,128)(2,1)S(1)} %shard_map.144.w0), channel_id=1, source_target_pairs={{0,1},{1,0},{2,3},{3,2},{4,5},{5,4},{6,7},{7,6},{8,9},{9,8},{10,11... | collective-permute-start | bytes 3145736 | tf_op jit(solution)/shard_map/ppermute | solution.py:365
  62.8 30.4 %copy-start.7 = (bf16[128,1024]{1,0:T(8,128)(2,1)}, bf16[128,1024]{1,0:T(8,128)(2,1)S(1)}, u32[]{:S(2)}) copy-start(bf16[128,1024]{1,0:T(8,128)(2,1)S(1)} %collective-permute-done.4.b2) | copy-start | bytes 786436
  62.8 30.4 %collective-permute-start.5 = (bf16[128,1024]{1,0:T(8,128)(2,1)S(1)}, bf16[128,1024]{1,0:T(8,128)(2,1)}, u32[]{:S(2)}, u32[]{:S(2)}) collective-permute-start(bf16[128,1024]{1,0:T(8,128)(2,1)S(1)} %collective-permute-done.1.a1), channel_id=1, source_target_pairs={{0,4},{1,5},{2,6},{3,7},{4,8},{5,9},{6,10},{7,11},{8,12},{9,13},{1... | collective-permute-start | bytes 786440 | tf_op jit(solution)/shard_map/ppermute | solution.py:348
  68.5 24.7 %copy-start.9 = (bf16[128,1024]{1,0:T(8,128)(2,1)}, bf16[128,1024]{1,0:T(8,128)(2,1)S(1)}, u32[]{:S(2)}) copy-start(bf16[128,1024]{1,0:T(8,128)(2,1)S(1)} %collective-permute-done.3.a2) | copy-start | bytes 786436
  68.5 24.7 %collective-permute-start.6 = (bf16[128,1024]{1,0:T(8,128)(2,1)S(1)}, bf16[128,1024]{1,0:T(8,128)(2,1)}, u32[]{:S(2)}, u32[]{:S(2)}) collective-permute-start(bf16[128,1024]{1,0:T(8,128)(2,1)S(1)} %collective-permute-done.4.b2), channel_id=1, source_target_pairs={{0,12},{1,13},{2,14},{3,15},{4,0},{5,1},{6,2},{7,3},{8,4},{9,5},{1... | collective-permute-start | bytes 786440 | tf_op jit(solution)/shard_map/ppermute | solution.py:349
  69.2 57.0 %collective-permute-start.9 = (bf16[2048,256]{1,0:T(8,128)(2,1)}, bf16[2048,256]{1,0:T(8,128)(2,1)}, u32[]{:S(2)}, u32[]{:S(2)}) collective-permute-start(bf16[2048,256]{1,0:T(8,128)(2,1)} %collective-permute-done.8.w2), channel_id=1, source_target_pairs={{0,1},{1,0},{2,3},{3,2},{4,5},{5,4},{6,7},{7,6},{8,9},{9,8},{10,11... | collective-permute-start | bytes 3145736 | tf_op jit(solution)/shard_map/ppermute | solution.py:367
  93.2 1.0 copy-start.8
  94.2 0.9 copy-start.10
  130.5 3.8 %copy-start.16 = (bf16[1024,100]{0,1:T(8,128)(2,1)S(1)}, bf16[1024,100]{0,1:T(8,128)(2,1)}, u32[]{:S(2)}) copy-start(bf16[1024,100]{0,1:T(8,128)(2,1)} %param.19) | copy-start | bytes 614404
  130.5 11.7 %all-to-all-start.2 = ((bf16[4,64,1024]{2,1,0:T(8,128)(2,1)}), bf16[4,64,1024]{2,1,0:T(8,128)(2,1)S(1)}, u32[]{:S(2)}, u32[]{:S(2)}) async-start(bf16[4,64,1024]{2,1,0:T(8,128)(2,1)} %bitcast.3), calls=%async_computation.2 | async-start | bytes 1048576 | tf_op jit(solution)/shard_map/all_to_all | solution.py:288
  143.3 14.4 %all-to-all-start.3 = ((f32[16,64,100]{2,1,0:T(8,128)}), f32[16,64,100]{2,1,0:T(8,128)S(1)}, u32[]{:S(2)}, u32[]{:S(2)}) async-start(f32[16,64,100]{2,1,0:T(8,128)} %shard_map.146), calls=%async_computation.3 | async-start | bytes 1048576 | tf_op jit(solution)/shard_map/all_to_all | solution.py:288
  157.7 15.0 %collective-permute-start.10 = (f32[8,100]{1,0:T(8,128)S(1)}, f32[8,100]{1,0:T(8,128)S(1)}, u32[]{:S(2)}, u32[]{:S(2)}) collective-permute-start(f32[8,100]{1,0:T(8,128)S(1)} %get-tuple-element.27), channel_id=1, source_target_pairs={{0,16},{16,32},{32,48},{48,64},{64,80},{80,96},{96,112},{112,128},... | collective-permute-start | bytes 9608 | tf_op jit(solution)/shard_map/ppermute | solution.py:435
  161.3 11.4 %collective-permute-start.11 = (f32[8,100]{1,0:T(8,128)S(1)}, f32[8,100]{1,0:T(8,128)S(1)}, u32[]{:S(2)}, u32[]{:S(2)}) collective-permute-start(f32[8,100]{1,0:T(8,128)S(1)} %get-tuple-element.26), channel_id=1, source_target_pairs={{16,0},{32,16},{48,32},{64,48},{80,64},{96,80},{112,96},{128,112},... | collective-permute-start | bytes 9608 | tf_op jit(solution)/shard_map/ppermute | solution.py:436
  175.2 15.1 %all-to-all-start.4 = ((bf16[16,72,192]{2,1,0:T(8,128)(2,1)}), bf16[16,72,192]{2,1,0:T(8,128)(2,1)S(1)}, u32[]{:S(2)}, u32[]{:S(2)}) async-start(bf16[16,72,192]{2,1,0:T(8,128)(2,1)} %shard_map.149), calls=%async_computation.4 | async-start | bytes 1179648 | tf_op jit(solution)/shard_map/all_to_all | solution.py:288
  (3 other events, 2.7 us)
Sparse Core Ops, SparseCore 0:
  13.2 88.6 all-gather.2

commit v4 on v3

--- a/solution.py
+++ b/solution.py
@@ -17,7 +17,6 @@
 bf16 = jnp.bfloat16
 f32 = jnp.float32
 
-X_GROUPS = [[4 * x + j for x in range(4)] for j in range(4)]
 J_GROUPS = [[4 * x + j for j in range(4)] for x in range(4)]
 
 
@@ -58,11 +57,17 @@
     return pl.CostEstimate(flops=flops, bytes_accessed=nbytes, transcendentals=trans)
 
 
-def attention_weights_kernel(w_ref, o_ref, a_ref, b_ref):
+def first_weights_kernel(w_ref, o_ref, pre_ref, dil_ref, plain_ref, a_ref, b_ref, voc_ref):
     a_ref[0:64, :] = w_ref[0]
     a_ref[64:128, :] = w_ref[1]
     b_ref[0:64, :] = w_ref[2]
     b_ref[64:128, :] = o_ref[...]
+    voc_ref[0:96, :] = jnp.zeros((96, 768), bf16)
+    for k in range(7):
+        voc_ref[0:96, 100 * k : 100 * k + 100] = pre_ref[k]
+    for k in range(3):
+        voc_ref[96 + 48 * k : 144 + 48 * k, :] = dil_ref[k]
+        voc_ref[240 + 48 * k : 288 + 48 * k, :] = plain_ref[k]
 
 
 def mlp_weights_kernel(up_ref, down_ref, out_ref):
@@ -71,15 +76,6 @@
         out_ref[1024 + 256 * k : 1280 + 256 * k, :] = down_ref[:, 256 * k : 256 * k + 256]
 
 
-def vocoder_weights_kernel(pre_ref, dil_ref, plain_ref, out_ref):
-    out_ref[0:96, :] = jnp.zeros((96, 768), bf16)
-    for k in range(7):
-        out_ref[0:96, 100 * k : 100 * k + 100] = pre_ref[k]
-    for k in range(3):
-        out_ref[96 + 48 * k : 144 + 48 * k, :] = dil_ref[k]
-        out_ref[240 + 48 * k : 288 + 48 * k, :] = plain_ref[k]
-
-
 TAP_ORDER = (2, 3, 4, 5, 6, 7, 0, 1)
 
 
@@ -90,7 +86,7 @@
 
 
 def attention_kernel(
-    flag_ref, own_ref, back_ref, mod_ref, a0, b0, a1, b1, a2, b2, a3, b3, out_ref, heads, w_out
+    flag_ref, own_ref, back_ref, mod_ref, a0, b0, a1, b1, a2, b2, a3, b3, o0, o1, o2, o3, heads, w_out, total_out
 ):
     first = flag_ref[0] > 0
     scale = 1.0 / math.sqrt(HEAD_DIM)
@@ -117,20 +113,25 @@
         p_back = (e_back * inv).astype(bf16)
         heads[:, 64 * h : 64 * h + 64] = (mm(p_own, v) + mm(p_back, vb)).astype(bf16)
         w_out[64 * h : 64 * h + 64, :] = wb[64:128, :]
-    out_ref[...] = mm(heads[...], w_out[...]).astype(bf16)
-
-
-def after_attention_kernel(parts_ref, frames_ref, mod_ref, mixed_ref, norm_ref):
-    attn = parts_ref[0].astype(f32)
-    for k in range(1, 4):
-        attn += parts_ref[k].astype(f32)
+    total_out[...] = mm(heads[...], w_out[...]).astype(bf16)
+    for k, out in enumerate((o0, o1, o2, o3)):
+        start = pl.multiple_of(64 * (flag_ref[1] ^ k), 64)
+        out[...] = total_out[pl.ds(start, 64), :]
+
+
+def sum_of(p0, p1, p2, p3):
+    return (p0[...].astype(f32) + p1[...].astype(f32)) + (p2[...].astype(f32) + p3[...].astype(f32))
+
+
+def after_attention_kernel(p0, p1, p2, p3, frames_ref, mod_ref, mixed_ref, norm_ref):
+    attn = sum_of(p0, p1, p2, p3)
     mixed = (frames_ref[...].astype(f32) + mod_ref[2:3, :] * attn).astype(bf16)
     mixed_ref[...] = mixed
     norm_ref[...] = norm_rows(mixed, mod_ref[3:4, :], mod_ref[4:5, :]).astype(bf16)
 
 
-def mlp_kernel(h_ref, w0, w1, w2, w3, out_ref, acc):
-    h = h_ref[...]
+def mlp_kernel(h0, h1, h2, h3, w0, w1, w2, w3, o0, o1, o2, o3, acc):
+    h = jnp.concatenate([h0[...], h1[...], h2[...], h3[...]], axis=0)
     for i, w in enumerate((w0, w1, w2, w3)):
         up = mm(h, w[0:1024, :])
         hid = jax.nn.gelu(up, approximate=True).astype(bf16)
@@ -142,13 +143,13 @@
             elif i < 3:
                 acc[:, cols] += part
             else:
-                out_ref[:, cols] = (acc[:, cols] + part).astype(bf16)
-
-
-def after_mlp_kernel(parts_ref, mixed_ref, mod_ref, wv_ref, noisy_ref, out_ref):
-    feed = parts_ref[0].astype(f32)
-    for k in range(1, 4):
-        feed += parts_ref[k].astype(f32)
+                value = (acc[:, cols] + part).astype(bf16)
+                for n, out in enumerate((o0, o1, o2, o3)):
+                    out[:, cols] = value[64 * n : 64 * n + 64]
+
+
+def after_mlp_kernel(p0, p1, p2, p3, mixed_ref, mod_ref, wv_ref, noisy_ref, out_ref):
+    feed = sum_of(p0, p1, p2, p3)
     final = (mixed_ref[...].astype(f32) + mod_ref[5:6, :] * feed).astype(bf16)
     normed = norm_rows(final, mod_ref[6:7, :], mod_ref[7:8, :]).astype(bf16)
     mel = noisy_ref[...] + 0.5 * mm(normed, wv_ref[...])
@@ -225,17 +226,13 @@
 ROWS = 72
 
 
-def conv_kernel(flag_ref, up_ref, alpha_ref, w_hbm, out_ref, planes, w_ref, sem):
-    copies = [
-        pltpu.make_async_copy(
-            w_hbm.at[:, pl.ds(96 + 144 * k, 144), :],
-            w_ref.at[:, pl.ds(144 * k, 144), :],
-            sem.at[k],
-        )
-        for k in range(2)
-    ]
-    for c in copies:
-        c.start()
+def conv_weights_kernel(w_hbm, out_ref, sem):
+    copy = pltpu.make_async_copy(w_hbm.at[:, pl.ds(96, 288), :], out_ref, sem)
+    copy.start()
+    copy.wait()
+
+
+def conv_kernel(flag_ref, up_ref, alpha_ref, w_ref, out_ref, planes):
     first = flag_ref[0] > 0
     last = flag_ref[1] > 0
     row = lax.broadcasted_iota(jnp.int32, (ROWS, 768), 0)
@@ -260,7 +257,6 @@
         ups.append(u)
         acts.append(snake_act(u, a1, i1).astype(bf16))
     act = jnp.concatenate(acts, axis=0)
-    copies[0].wait()
     y = [mm(act, weight(0, tap)) for tap in range(3)]
     y = [[v[ROWS * p : ROWS * p + ROWS] for p in range(4)] for v in y]
     acts = []
@@ -270,7 +266,6 @@
         inner = before + y[1][p] + after
         acts.append(jnp.where(outside, 0.0, snake_act(inner, a2, i2)).astype(bf16))
     act = jnp.concatenate(acts, axis=0)
-    copies[1].wait()
     y = [mm(act, weight(144, tap)) for tap in range(3)]
     y = [[v[ROWS * p : ROWS * p + ROWS] for p in range(4)] for v in y]
     for p in range(4):
@@ -334,11 +329,11 @@
 
     to_right = [(i, (i + 4) % 16) for i in range(16)]
     to_left = [(i, (i - 4) % 16) for i in range(16)]
-    own_a, own_b = whole(
-        attention_weights_kernel,
-        (shape((128, 1024), bf16), shape((128, 1024), bf16)),
-        (jnp.swapaxes(w_project, 1, 2), w_heads_out),
-        cost=cost_of(0, 1 << 20),
+    own_a, own_b, w_voc = whole(
+        first_weights_kernel,
+        (shape((128, 1024), bf16), shape((128, 1024), bf16), shape((384, 768), bf16)),
+        (jnp.swapaxes(w_project, 1, 2), w_heads_out, w_prelude, w_dilated, w_plain),
+        cost=cost_of(0, 3 << 20),
     )
     back_frames = lax.ppermute(frames, both, [(i, i + 4) for i in range(n_all - 4)])
     left_a = lax.ppermute(own_a, "sub", to_right)
@@ -348,12 +343,6 @@
     far_a = lax.ppermute(left_a, "sub", to_right)
     far_b = lax.ppermute(right_b, "sub", to_left)
 
-    w_voc = whole(
-        vocoder_weights_kernel,
-        shape((384, 768), bf16),
-        lax.optimization_barrier((w_prelude, w_dilated, w_plain, own_a))[:3],
-        cost=cost_of(0, 2 << 20),
-    )
     w_voc = lax.all_gather(w_voc, "sub", axis=0, tiled=False)
 
     block = gather(frames, J_GROUPS)
@@ -371,11 +360,12 @@
     )
 
     is_first = (time_index == 0) & (sub_index < 4)
+    quarter = shape((own_rows, 1024), bf16)
     partial = whole(
         attention_kernel,
-        shape((BLK, 1024), bf16),
+        (quarter,) * 4,
         (
-            is_first.astype(jnp.int32).reshape(1),
+            jnp.stack([is_first.astype(jnp.int32), lax.rem(sub_index, 4)]),
             block,
             back,
             modulation,
@@ -388,34 +378,47 @@
             far_a,
             far_b,
         ),
-        scratch=[pltpu.VMEM((BLK, 256), bf16), pltpu.VMEM((256, 1024), bf16)],
+        scratch=[pltpu.VMEM((BLK, 256), bf16)] + [pltpu.VMEM((256, 1024), bf16)] * 2,
         cost=cost_of(10**9, 4 << 20, 1 << 19),
         smem=1,
     )
     ups = exchange(ups, OTHER_GROUPS, both)
-    partial, ups = lax.optimization_barrier((partial, ups))
-    parts = exchange(partial, J_GROUPS)
+    parts = [partial[0]] + [
+        lax.ppermute(partial[k], "sub", [(i, i ^ k) for i in range(16)]) for k in (1, 2, 3)
+    ]
     mixed_rows, own_norm = whole(
         after_attention_kernel,
-        (shape((own_rows, 1024), bf16), shape((own_rows, 1024), bf16)),
-        (parts.reshape(4, own_rows, 1024), frames, modulation),
+        (quarter, quarter),
+        (*parts, frames, modulation),
         cost=cost_of(10**6, 1 << 20),
     )
 
-    second = gather(own_norm, X_GROUPS)
+    own_norm, ups = lax.optimization_barrier((own_norm, ups))
+    across = [(i, (i + 8) % 16) for i in range(16)]
+    second = [
+        own_norm,
+        lax.ppermute(own_norm, "sub", across),
+        lax.ppermute(own_norm, "sub", to_right),
+        lax.ppermute(own_norm, "sub", to_left),
+    ]
     partial = whole(
         mlp_kernel,
-        shape((256, 1024), bf16),
-        (second, own_mlp, other_core, other_y, other_both),
+        (quarter,) * 4,
+        (*second, own_mlp, other_core, other_y, other_both),
         scratch=[pltpu.VMEM((256, 1024), f32)],
         cost=cost_of(11 * 10**8, 5 << 20, 1 << 18),
     )
-    parts = exchange(partial, X_GROUPS)
+    parts = [
+        partial[0],
+        lax.ppermute(partial[1], "sub", across),
+        lax.ppermute(partial[2], "sub", to_left),
+        lax.ppermute(partial[3], "sub", to_right),
+    ]
     noisy_own = lax.dynamic_slice_in_dim(noisy_mel, sub_index * own_rows, own_rows, 0)
     copies = whole(
         after_mlp_kernel,
         shape((16, own_rows, 100), f32),
-        (parts.reshape(4, own_rows, 1024), mixed_rows, modulation, w_velocity, noisy_own),
+        (*parts, mixed_rows, modulation, w_velocity, noisy_own),
         cost=cost_of(10**7, 1 << 20),
     )
     mel_all = exchange(copies)
@@ -452,22 +455,25 @@
     up_x = exchange(windows)
 
     flags = jnp.stack([here_index == 0, here_index == n_all - 1]).astype(jnp.int32)
-    out = pl.pallas_call(
+    w_conv = pl.pallas_call(
+        conv_weights_kernel,
+        out_shape=shape((16, 288, 768), bf16),
+        in_specs=[pl.BlockSpec(memory_space=pl.ANY)],
+        out_specs=pl.BlockSpec(memory_space=pltpu.VMEM),
+        scratch_shapes=[pltpu.SemaphoreType.DMA],
+        compiler_params=pltpu.CompilerParams(vmem_limit_bytes=16 << 20),
+        cost_estimate=cost_of(0, 14 << 20),
+        name="conv_weights",
+    )(w_voc)
+    out = whole(
         conv_kernel,
-        out_shape=shape((64, 3072), bf16),
-        in_specs=[pl.BlockSpec(memory_space=pltpu.SMEM)]
-        + vmem_specs(2)
-        + [pl.BlockSpec(memory_space=pltpu.MemorySpace.HBM)],
-        out_specs=pl.BlockSpec(memory_space=pltpu.VMEM),
-        scratch_shapes=[
-            pltpu.VMEM((4, ROWS, 768), bf16),
-            pltpu.VMEM((16, 288, 768), bf16),
-            pltpu.SemaphoreType.DMA((2,)),
-        ],
-        compiler_params=pltpu.CompilerParams(vmem_limit_bytes=54 << 20),
-        cost_estimate=cost_of(2 * 10**9, 8 << 20, 1 << 18),
-        name="convolutions",
-    )(flags, up_x, snake_alpha, w_voc)
+        shape((64, 3072), bf16),
+        (flags, up_x, snake_alpha, w_conv),
+        scratch=[pltpu.VMEM((4, ROWS, 768), bf16)],
+        cost=cost_of(2 * 10**9, 8 << 20, 1 << 18),
+        smem=1,
+        vmem=32,
+    )
     return (mel_next, out.reshape(256, 768))
 
 

time: 208 us -> 196 us (0.942)
  blocking collectives: 48.8 us -> 23.8 us
  starting transfers between devices: 39.3 us -> 47.7 us
  local copies, waits for them, and re-layouts: 11.5 us -> 17.9 us
  Pallas kernels: 25.2 us -> 21.9 us
  waiting for transfers between devices: 63.9 us -> 66.3 us
    ppermute x1, waiting for transfers between devices: 31.3 us -> 0.01 us  [program(): lax.ppermute(frames, both, [(i, i + 4) for i in range(n_all - 4)])]
    ppermute x1, waiting for transfers between devices: 0.01 us -> 25.8 us  [program(): other_y = lax.ppermute(own_mlp, both, OTHER_Y)]
    ppermute x0 -> x9, waiting for transfers between devices: none -> 16.7 us  [the longest x3 6.57 us: program(): lax.ppermute(partial[k], 'sub', [(i, i ^ k) for i in range(16)])]
    all_to_all x4 -> x3, waiting for transfers between devices: 28 us -> 14.2 us  [exchange(): lax.all_to_all(value, axis, 0, 0, tiled=True, axis_index_groups=groups)]
    all_gather x3 -> x2, blocking collectives: 37.4 us -> 23.8 us  [gather(): lax.all_gather(value, 'sub', axis=0, tiled=True, axis_index_groups=groups)]
    ppermute x0 -> x9, starting transfers between devices: none -> 12 us  [the longest x1 3.23 us: program(): lax.ppermute(own_norm, 'sub', to_left)]
    all_to_all x1 -> x0, blocking collectives: 11.4 us -> none  [exchange(): lax.all_to_all(value, axis, 0, 0, tiled=True, axis_index_groups=groups)]
    unnamed x39 -> x37, local copies, waits for them, and re-layouts: 9.45 us -> 16.9 us
  transfers between devices with their start and end apart: 17 -> 25, of which waited for: 5 -> 11; matrix products, arithmetic and copies ran while one was open for 3% -> 3% of each run, Pallas kernels for 7% -> 7%
where the time goes in v4:
time: 196 us; the launch traced here: 195 us
  waiting for transfers between devices  66.3 us (34%)
  starting transfers between devices  47.7 us (24%)
  blocking collectives  23.8 us (12%)
  Pallas kernels  21.9 us (11%)
  local copies, waits for them, and re-layouts  17.9 us (9%)
  between operations  14.3 us (7%)
  matrix products  3.39 us (2%)
    ppermute x1, waiting for transfers between devices, program(): other_y = lax.ppermute(own_mlp, both, OTHER_Y)  25.8 us
    all_gather x2, blocking collectives, gather(): lax.all_gather(value, 'sub', axis=0, tiled=True, axis_index_groups=groups)  23.8 us
    pallas_call x10, Pallas kernels, whole(): pl.pallas_call(kernel, out_shape=out_shapes, in_specs=[pl.BlockSpec(memor...  21.4 us
    unnamed x37, local copies, waits for them, and re-layouts  16.9 us
    all_to_all x3, waiting for transfers between devices, exchange(): lax.all_to_all(value, axis, 0, 0, tiled=True, axis_index_groups=groups)  14.2 us
    all_to_all x3, starting transfers between devices, exchange(): lax.all_to_all(value, axis, 0, 0, tiled=True, axis_index_groups=groups)  12.4 us
    ppermute x1, starting transfers between devices, program(): lax.ppermute(mel_all[0, :8], 'tm', [(i + 1, i) for i in range(n_tm - 1)])  8.51 us
    ppermute x1, waiting for transfers between devices, program(): left_b = lax.ppermute(own_b, 'sub', to_right)  7.14 us
  transfers between devices with their start and end apart: 25, of which 11 were waited for; matrix products, arithmetic and copies ran while one was open for 3% of the time, Pallas kernels for 7%

profile of v4, /device:TPU:16, one launch (start us, length us, event | category | flops | bytes accessed | tf_op | source)
XLA Modules:
  0.0 195.5 jit_solution(13739079077907552394)
XLA Ops:
  14.3 2.5 %shard_map.143 = bf16[16,96,384]{2,1,0:T(8,128)(2,1)} custom-call(bf16[8,96,768]{2,1,0:T(8,128)(2,1)S(1)} %copy-done.4), custom_call_target="tpu_custom_call" | custom-call | bytes 3145728 | tf_op jit(solution)/shard_map/pallas_call | solution.py:45
  16.8 4.9 %all-to-all-start = ((bf16[16,96,384]{2,1,0:T(8,128)(2,1)}), bf16[16,96,384]{2,1,0:T(8,128)(2,1)}, u32[]{:S(2)}, u32[]{:S(2)}) async-start(bf16[16,96,384]{2,1,0:T(8,128)(2,1)} %shard_map.143), calls=%async_computation | async-start | bytes 2359296 | tf_op jit(solution)/shard_map/all_to_all | solution.py:283
  21.8 3.8 %collective-permute-start = (bf16[64,1024]{1,0:T(8,128)(2,1)S(1)}, bf16[64,1024]{1,0:T(8,128)(2,1)S(1)}, u32[]{:S(2)}, u32[]{:S(2)}) collective-permute-start(bf16[64,1024]{1,0:T(8,128)(2,1)S(1)} %copy-done.5), channel_id=1, source_target_pairs={{0,4},{1,5},{2,6},{3,7},{4,8},{5,9},{6,10},{7,11},{8,12},{9,13},{1... | collective-permute-start | bytes 393224 | tf_op jit(solution)/shard_map/ppermute | solution.py:338
  25.7 25.8 %collective-permute-done.14.w2 = bf16[2048,256]{1,0:T(8,128)(2,1)S(1)} collective-permute-done((bf16[2048,256]{1,0:T(8,128)(2,1)S(1)}, bf16[2048,256]{1,0:T(8,128)(2,1)S(1)}, u32[]{:S(2)}, u32[]{:S(2)}) %collective-permute-start.14) | collective-permute-done | bytes 1048608 | tf_op jit(solution)/shard_map/ppermute | solution.py:355
  52.4 3.1 %collective-permute-start.4 = (bf16[128,1024]{1,0:T(8,128)(2,1)S(1)}, bf16[128,1024]{1,0:T(8,128)(2,1)}, u32[]{:S(2)}, u32[]{:S(2)}) collective-permute-start(bf16[128,1024]{1,0:T(8,128)(2,1)S(1)} %get-tuple-element.20.b0), channel_id=1, source_target_pairs={{0,12},{1,13},{2,14},{3,15},{4,0},{5,1},{6,2},{7,3},{8,4},{9,5},{1... | collective-permute-start | bytes 786440 | tf_op jit(solution)/shard_map/ppermute | solution.py:340
  55.5 12.2 %all_gather.12.own_ref = bf16[256,1024]{1,0:T(8,128)(2,1)S(1)} all-gather(bf16[64,1024]{1,0:T(8,128)(2,1)S(1)} %copy-done.5), channel_id=1, replica_groups={{0,1,2,3},{4,5,6,7},{8,9,10,11},{12,13,14,15},{16,17,18,19},{20,21,22,2..., dimensions={0}, use_global_device_ids=true | all-gather | bytes 655360 | tf_op jit(solution)/shard_map/all_gather | solution.py:279
  68.0 7.1 %collective-permute-done.2.b1 = bf16[128,1024]{1,0:T(8,128)(2,1)} collective-permute-done((bf16[128,1024]{1,0:T(8,128)(2,1)S(1)}, bf16[128,1024]{1,0:T(8,128)(2,1)}, u32[]{:S(2)}, u32[]{:S(2)}) %collective-permute-start.2) | collective-permute-done | bytes 262176 | tf_op jit(solution)/shard_map/ppermute | solution.py:341
  75.1 2.6 %collective-permute-start.5 = (bf16[128,1024]{1,0:T(8,128)(2,1)S(1)}, bf16[128,1024]{1,0:T(8,128)(2,1)S(1)}, u32[]{:S(2)}, u32[]{:S(2)}) collective-permute-start(bf16[128,1024]{1,0:T(8,128)(2,1)S(1)} %collective-permute-done.1.a1), channel_id=1, source_target_pairs={{0,4},{1,5},{2,6},{3,7},{4,8},{5,9},{6,10},{7,11},{8,12},{9,13},{1... | collective-permute-start | bytes 786440 | tf_op jit(solution)/shard_map/ppermute | solution.py:343
  78.4 11.6 %all_gather.13.back_ref = bf16[256,1024]{1,0:T(8,128)(2,1)S(1)} all-gather(bf16[64,1024]{1,0:T(8,128)(2,1)} %copy-done.16), channel_id=1, replica_groups={{0,1,2,3},{4,5,6,7},{8,9,10,11},{12,13,14,15},{16,17,18,19},{20,21,22,2..., dimensions={0}, use_global_device_ids=true | all-gather | bytes 655360 | tf_op jit(solution)/shard_map/all_gather | solution.py:279
  90.0 2.4 %collective-permute-done.6.b3 = bf16[128,1024]{1,0:T(8,128)(2,1)S(1)} collective-permute-done((bf16[128,1024]{1,0:T(8,128)(2,1)}, bf16[128,1024]{1,0:T(8,128)(2,1)S(1)}, u32[]{:S(2)}, u32[]{:S(2)}) %collective-permute-start.6) | collective-permute-done | bytes 262176 | tf_op jit(solution)/shard_map/ppermute | solution.py:344
  92.4 6.0 %shard_map.141 = (bf16[64,1024]{1,0:T(8,128)(2,1)S(1)}, bf16[64,1024]{1,0:T(8,128)(2,1)S(1)}, bf16[64,1024]{1,0:T(8,128)(2,1)S(1)}, bf16[64,1024]{1,0:T(8,128)(2,1)S(1)}) custom-call(s32[2]{0:T(128)S(1)} %pad_add_fusion.flag_ref, bf16[256,1024]{1,0:T(8,128)(2,1)S(1)} %all_gather.12.own_ref, bf16[256,1024]{1,0:T(8,128)(2,1)S(1)} %all_gather.13.back_ref, ...), custom_call_target="tpu_custom_call" | custom-call | flops 1000000000 | bytes 4194304 | tf_op jit(solution)/shard_map/pallas_call | solution.py:45
  98.5 2.6 %collective-permute-start.8 = (bf16[64,1024]{1,0:T(8,128)(2,1)S(1)}, bf16[64,1024]{1,0:T(8,128)(2,1)S(1)}, u32[]{:S(2)}, u32[]{:S(2)}) collective-permute-start(bf16[64,1024]{1,0:T(8,128)(2,1)S(1)} %get-tuple-element.23), channel_id=1, source_target_pairs={{0,2},{1,3},{2,0},{3,1},{4,6},{5,7},{6,4},{7,5},{8,10},{9,11},{10,... | collective-permute-start | bytes 393224 | tf_op jit(solution)/shard_map/ppermute | solution.py:387
  101.0 4.3 %collective-permute-done.8.p2 = bf16[64,1024]{1,0:T(8,128)(2,1)S(1)} collective-permute-done((bf16[64,1024]{1,0:T(8,128)(2,1)S(1)}, bf16[64,1024]{1,0:T(8,128)(2,1)S(1)}, u32[]{:S(2)}, u32[]{:S(2)}) %collective-permute-start.8) | collective-permute-done | bytes 131104 | tf_op jit(solution)/shard_map/ppermute | solution.py:387
  105.4 2.2 %collective-permute-done.9.p3 = bf16[64,1024]{1,0:T(8,128)(2,1)S(1)} collective-permute-done((bf16[64,1024]{1,0:T(8,128)(2,1)S(1)}, bf16[64,1024]{1,0:T(8,128)(2,1)S(1)}, u32[]{:S(2)}, u32[]{:S(2)}) %collective-permute-start.9) | collective-permute-done | bytes 131104 | tf_op jit(solution)/shard_map/ppermute | solution.py:387
  107.9 2.2 %collective-permute-start.10 = (bf16[64,1024]{1,0:T(8,128)(2,1)S(1)}, bf16[64,1024]{1,0:T(8,128)(2,1)S(1)}, u32[]{:S(2)}, u32[]{:S(2)}) collective-permute-start(bf16[64,1024]{1,0:T(8,128)(2,1)S(1)} %get-tuple-element.26.h0), channel_id=1, source_target_pairs={{0,8},{1,9},{2,10},{3,11},{4,12},{5,13},{6,14},{7,15},{8,0},{9,1},... | collective-permute-start | bytes 393224 | tf_op jit(solution)/shard_map/ppermute | solution.py:400
  110.1 3.2 %collective-permute-start.12 = (bf16[64,1024]{1,0:T(8,128)(2,1)S(1)}, bf16[64,1024]{1,0:T(8,128)(2,1)S(1)}, u32[]{:S(2)}, u32[]{:S(2)}) collective-permute-start(bf16[64,1024]{1,0:T(8,128)(2,1)S(1)} %get-tuple-element.26.h0), channel_id=1, source_target_pairs={{0,12},{1,13},{2,14},{3,15},{4,0},{5,1},{6,2},{7,3},{8,4},{9,5},{1... | collective-permute-start | bytes 393224 | tf_op jit(solution)/shard_map/ppermute | solution.py:402
  113.3 2.5 %collective-permute-done.10.h1 = bf16[64,1024]{1,0:T(8,128)(2,1)S(1)} collective-permute-done((bf16[64,1024]{1,0:T(8,128)(2,1)S(1)}, bf16[64,1024]{1,0:T(8,128)(2,1)S(1)}, u32[]{:S(2)}, u32[]{:S(2)}) %collective-permute-start.10) | collective-permute-done | bytes 131104 | tf_op jit(solution)/shard_map/ppermute | solution.py:400
  115.8 2.0 %collective-permute-done.11.h2 = bf16[64,1024]{1,0:T(8,128)(2,1)S(1)} collective-permute-done((bf16[64,1024]{1,0:T(8,128)(2,1)S(1)}, bf16[64,1024]{1,0:T(8,128)(2,1)S(1)}, u32[]{:S(2)}, u32[]{:S(2)}) %collective-permute-start.11) | collective-permute-done | bytes 131104 | tf_op jit(solution)/shard_map/ppermute | solution.py:401
  117.8 3.1 %shard_map.145 = (bf16[64,1024]{1,0:T(8,128)(2,1)S(1)}, bf16[64,1024]{1,0:T(8,128)(2,1)S(1)}, bf16[64,1024]{1,0:T(8,128)(2,1)S(1)}, bf16[64,1024]{1,0:T(8,128)(2,1)S(1)}) custom-call(bf16[64,1024]{1,0:T(8,128)(2,1)S(1)} %get-tuple-element.26.h0, bf16[64,1024]{1,0:T(8,128)(2,1)S(1)} %collective-permute-done.10.h1, ...), custom_call_target="tpu_custom_call" | custom-call | flops 1100000000 | bytes 5242880 | tf_op jit(solution)/shard_map/pallas_call | solution.py:45
  125.2 3.7 %collective-permute-done.16.p1 = bf16[64,1024]{1,0:T(8,128)(2,1)S(1)} collective-permute-done((bf16[64,1024]{1,0:T(8,128)(2,1)S(1)}, bf16[64,1024]{1,0:T(8,128)(2,1)S(1)}, u32[]{:S(2)}, u32[]{:S(2)}) %collective-permute-start.16) | collective-permute-done | bytes 131104 | tf_op jit(solution)/shard_map/ppermute | solution.py:413
  132.0 3.9 %all-to-all-start.1 = ((f32[16,64,100]{2,1,0:T(8,128)}), f32[16,64,100]{2,1,0:T(8,128)S(1)}, u32[]{:S(2)}, u32[]{:S(2)}) async-start(f32[16,64,100]{2,1,0:T(8,128)} %shard_map.146), calls=%async_computation.1 | async-start | bytes 1048576 | tf_op jit(solution)/shard_map/all_to_all | solution.py:283
  136.0 10.7 %all-to-all-done.1.mel_ref = f32[16,64,100]{2,1,0:T(8,128)S(1)} async-done(((f32[16,64,100]{2,1,0:T(8,128)}), f32[16,64,100]{2,1,0:T(8,128)S(1)}, u32[]{:S(2)}, u32[]{:S(2)}) %all-to-all-start.1) | async-done | bytes 409632 | tf_op jit(solution)/shard_map/all_to_all | solution.py:283
  146.7 3.6 %collective-permute-start.19 = (f32[8,100]{1,0:T(8,128)S(1)}, f32[8,100]{1,0:T(8,128)S(1)}, u32[]{:S(2)}, u32[]{:S(2)}) collective-permute-start(f32[8,100]{1,0:T(8,128)S(1)} %get-tuple-element.39), channel_id=1, source_target_pairs={{0,16},{16,32},{32,48},{48,64},{64,80},{80,96},{96,112},{112,128},... | collective-permute-start | bytes 9608 | tf_op jit(solution)/shard_map/ppermute | solution.py:438
  150.3 8.5 %collective-permute-start.20 = (f32[8,100]{1,0:T(8,128)S(1)}, f32[8,100]{1,0:T(8,128)S(1)}, u32[]{:S(2)}, u32[]{:S(2)}) collective-permute-start(f32[8,100]{1,0:T(8,128)S(1)} %get-tuple-element.38), channel_id=1, source_target_pairs={{16,0},{32,16},{48,32},{64,48},{80,64},{96,80},{112,96},{128,112},... | collective-permute-start | bytes 9608 | tf_op jit(solution)/shard_map/ppermute | solution.py:439
  158.8 3.4 %fusion.2.comp_ref = f32[768,384]{1,0:T(8,128)S(1)} fusion(bf16[16,96,384]{2,1,0:T(8,128)(2,1)} %all-to-all-done, bf16[16,384,768]{2,1,0:T(8,128)(2,1)} %bitcast.16), kind=kOutput, calls=%fused_computation.2 | convolution fusion | flops 905969664 | bytes 4718592 | tf_op jit(solution)/shard_map/dot_general | solution.py:428
  162.6 2.5 %shard_map.148 = bf16[16,72,192]{2,1,0:T(8,128)(2,1)} custom-call(s32[2]{0:T(128)S(1)} %add_convert_fusion.1.flag_ref, f32[16,64,100]{2,1,0:T(8,128)S(1)} %all-to-all-done.1.mel_ref, f32[8,100]{1,0:T(8,128)S(1)} %collective-permute-done.19.before_ref, f32[8,100]{1,0:T(8,128)S(1)} %collective-permute-done.20.after_ref, ...), custom_call_target="tpu_custom_call" | custom-call | flops 500000000 | bytes 2097152 | tf_op jit(solution)/shard_map/pallas_call | solution.py:45
  165.1 3.6 %all-to-all-start.2 = ((bf16[16,72,192]{2,1,0:T(8,128)(2,1)}), bf16[16,72,192]{2,1,0:T(8,128)(2,1)S(1)}, u32[]{:S(2)}, u32[]{:S(2)}) async-start(bf16[16,72,192]{2,1,0:T(8,128)(2,1)} %shard_map.148), calls=%async_computation.2 | async-start | bytes 1179648 | tf_op jit(solution)/shard_map/all_to_all | solution.py:283
  169.7 3.7 %copy-done.3 = bf16[6144,768]{1,0:T(8,128)(2,1)S(1)} copy-done((bf16[6144,768]{1,0:T(8,128)(2,1)S(1)}, bf16[6144,768]{1,0:T(8,128)(2,1)}, u32[]{:S(2)}) %copy-start.3) | copy-done | bytes 9437208
  173.9 2.8 %copy-done.1 = bf16[16,288,768]{2,1,0:T(8,128)(2,1)} copy-done((bf16[16,288,768]{2,1,0:T(8,128)(2,1)}, bf16[16,288,768]{2,1,0:T(8,128)(2,1)S(1)}, u32[]{:S(2)}) %copy-start.1) | copy-done | bytes 7077912
  176.7 3.4 %all-to-all-done.2.up_ref = bf16[16,72,192]{2,1,0:T(8,128)(2,1)S(1)} async-done(((bf16[16,72,192]{2,1,0:T(8,128)(2,1)}), bf16[16,72,192]{2,1,0:T(8,128)(2,1)S(1)}, u32[]{:S(2)}, u32[]{:S(2)}) %all-to-all-start.2) | async-done | bytes 442400 | tf_op jit(solution)/shard_map/all_to_all | solution.py:283
  180.2 3.0 %copy-done.2 = bf16[16,288,768]{2,1,0:T(8,128)(2,1)S(1)} copy-done((bf16[16,288,768]{2,1,0:T(8,128)(2,1)S(1)}, bf16[16,288,768]{2,1,0:T(8,128)(2,1)}, u32[]{:S(2)}) %copy-start.2) | copy-done | bytes 7077912
  183.2 4.5 %shard_map.149 = bf16[64,3072]{1,0:T(8,128)(2,1)S(1)} custom-call(s32[2]{0:T(128)S(1)} %add_convert_fusion.flag_ref, bf16[16,72,192]{2,1,0:T(8,128)(2,1)S(1)} %all-to-all-done.2.up_ref, f32[2,768]{1,0:T(2,128)S(1)} %copy-done.14, bf16[16,288,768]{2,1,0:T(8,128)(2,1)S(1)} %copy-done.2), custom_call_target="tpu_custom_call" | custom-call | flops 2000000000 | bytes 8388608 | tf_op jit(solution)/shard_map/pallas_call | solution.py:45
  (76 shorter events, 19.7 us)
Async XLA Ops:
  7.2 117.8 %copy-start = (f32[1024,100]{0,1:T(8,128)S(1)}, f32[1024,100]{0,1:T(8,128)}, u32[]{:S(2)}) copy-start(f32[1024,100]{0,1:T(8,128)} %param.20) | copy-start | bytes 1228804
  7.2 5.9 %copy-start.6 = (bf16[1024,256]{1,0:T(8,128)(2,1)S(1)}, bf16[1024,256]{1,0:T(8,128)(2,1)}, u32[]{:S(2)}) copy-start(bf16[1024,256]{1,0:T(8,128)(2,1)} %up_ref.1) | copy-start | bytes 1572868
  7.2 5.9 %copy-start.7 = (bf16[256,1024]{1,0:T(8,128)(2,1)S(1)}, bf16[256,1024]{1,0:T(8,128)(2,1)}, u32[]{:S(2)}) copy-start(bf16[256,1024]{1,0:T(8,128)(2,1)} %down_ref.1) | copy-start | bytes 1572868
  7.2 151.6 %all-gather.3.cloned.1.call-start = ((), (), s32[]{:S(2)}) async-start(), calls=%async_computation.3 | async-start | bytes 10027008 | tf_op jit(solution)/shard_map/all_gather | solution.py:346
  13.2 38.4 %collective-permute-start.14 = (bf16[2048,256]{1,0:T(8,128)(2,1)S(1)}, bf16[2048,256]{1,0:T(8,128)(2,1)S(1)}, u32[]{:S(2)}, u32[]{:S(2)}) collective-permute-start(bf16[2048,256]{1,0:T(8,128)(2,1)S(1)} %shard_map.144.w0), channel_id=1, source_target_pairs={{0,130},{1,131},{2,128},{3,129},{4,134},{5,135},{6,132},{7,133},{8... | collective-permute-start | bytes 3145736 | tf_op jit(solution)/shard_map/ppermute | solution.py:355
  16.8 5.0 %copy-start.5 = (bf16[64,1024]{1,0:T(8,128)(2,1)S(1)}, bf16[64,1024]{1,0:T(8,128)(2,1)}, u32[]{:S(2)}) copy-start(bf16[64,1024]{1,0:T(8,128)(2,1)} %frames_ref.1) | copy-start | bytes 393220
  16.8 91.0 %all-to-all-start = ((bf16[16,96,384]{2,1,0:T(8,128)(2,1)}), bf16[16,96,384]{2,1,0:T(8,128)(2,1)}, u32[]{:S(2)}, u32[]{:S(2)}) async-start(bf16[16,96,384]{2,1,0:T(8,128)(2,1)} %shard_map.143), calls=%async_computation | async-start | bytes 2359296 | tf_op jit(solution)/shard_map/all_to_all | solution.py:283
  21.8 70.6 %copy-start.13 = (f32[8,1024]{1,0:T(8,128)S(1)}, f32[8,1024]{1,0:T(8,128)}, u32[]{:S(2)}) copy-start(f32[8,1024]{1,0:T(8,128)} %mod_ref.5) | copy-start | bytes 98308
  21.8 29.9 %collective-permute-start = (bf16[64,1024]{1,0:T(8,128)(2,1)S(1)}, bf16[64,1024]{1,0:T(8,128)(2,1)S(1)}, u32[]{:S(2)}, u32[]{:S(2)}) collective-permute-start(bf16[64,1024]{1,0:T(8,128)(2,1)S(1)} %copy-done.5), channel_id=1, source_target_pairs={{0,4},{1,5},{2,6},{3,7},{4,8},{5,9},{6,10},{7,11},{8,12},{9,13},{1... | collective-permute-start | bytes 393224 | tf_op jit(solution)/shard_map/ppermute | solution.py:338
  25.6 87.7 %collective-permute-start.13 = (bf16[2048,256]{1,0:T(8,128)(2,1)S(1)}, bf16[2048,256]{1,0:T(8,128)(2,1)}, u32[]{:S(2)}, u32[]{:S(2)}) collective-permute-start(bf16[2048,256]{1,0:T(8,128)(2,1)S(1)} %shard_map.144.w0), channel_id=1, source_target_pairs={{0,1},{1,0},{2,3},{3,2},{4,5},{5,4},{6,7},{7,6},{8,9},{9,8},{10,11... | collective-permute-start | bytes 3145736 | tf_op jit(solution)/shard_map/ppermute | solution.py:354
  51.6 66.2 %collective-permute-start.15 = (bf16[2048,256]{1,0:T(8,128)(2,1)S(1)}, bf16[2048,256]{1,0:T(8,128)(2,1)}, u32[]{:S(2)}, u32[]{:S(2)}) collective-permute-start(bf16[2048,256]{1,0:T(8,128)(2,1)S(1)} %collective-permute-done.14.w2), channel_id=1, source_target_pairs={{0,1},{1,0},{2,3},{3,2},{4,5},{5,4},{6,7},{7,6},{8,9},{9,8},{10,11... | collective-permute-start | bytes 3145736 | tf_op jit(solution)/shard_map/ppermute | solution.py:356
  51.6 16.1 %collective-permute-start.1 = (bf16[128,1024]{1,0:T(8,128)(2,1)S(1)}, bf16[128,1024]{1,0:T(8,128)(2,1)S(1)}, u32[]{:S(2)}, u32[]{:S(2)}) collective-permute-start(bf16[128,1024]{1,0:T(8,128)(2,1)S(1)} %get-tuple-element.19.a0), channel_id=1, source_target_pairs={{0,4},{1,5},{2,6},{3,7},{4,8},{5,9},{6,10},{7,11},{8,12},{9,13},{1... | collective-permute-start | bytes 786440 | tf_op jit(solution)/shard_map/ppermute | solution.py:339
  51.6 23.5 %collective-permute-start.2 = (bf16[128,1024]{1,0:T(8,128)(2,1)S(1)}, bf16[128,1024]{1,0:T(8,128)(2,1)}, u32[]{:S(2)}, u32[]{:S(2)}) collective-permute-start(bf16[128,1024]{1,0:T(8,128)(2,1)S(1)} %get-tuple-element.20.b0), channel_id=1, source_target_pairs={{0,4},{1,5},{2,6},{3,7},{4,8},{5,9},{6,10},{7,11},{8,12},{9,13},{1... | collective-permute-start | bytes 786440 | tf_op jit(solution)/shard_map/ppermute | solution.py:341
  52.4 25.3 %collective-permute-start.4 = (bf16[128,1024]{1,0:T(8,128)(2,1)S(1)}, bf16[128,1024]{1,0:T(8,128)(2,1)}, u32[]{:S(2)}, u32[]{:S(2)}) collective-permute-start(bf16[128,1024]{1,0:T(8,128)(2,1)S(1)} %get-tuple-element.20.b0), channel_id=1, source_target_pairs={{0,12},{1,13},{2,14},{3,15},{4,0},{5,1},{6,2},{7,3},{8,4},{9,5},{1... | collective-permute-start | bytes 786440 | tf_op jit(solution)/shard_map/ppermute | solution.py:340
  67.7 22.3 %collective-permute-start.3 = (bf16[128,1024]{1,0:T(8,128)(2,1)S(1)}, bf16[128,1024]{1,0:T(8,128)(2,1)S(1)}, u32[]{:S(2)}, u32[]{:S(2)}) collective-permute-start(bf16[128,1024]{1,0:T(8,128)(2,1)S(1)} %get-tuple-element.19.a0), channel_id=1, source_target_pairs={{0,12},{1,13},{2,14},{3,15},{4,0},{5,1},{6,2},{7,3},{8,4},{9,5},{1... | collective-permute-start | bytes 786440 | tf_op jit(solution)/shard_map/ppermute | solution.py:342
  75.1 14.9 %collective-permute-start.5 = (bf16[128,1024]{1,0:T(8,128)(2,1)S(1)}, bf16[128,1024]{1,0:T(8,128)(2,1)S(1)}, u32[]{:S(2)}, u32[]{:S(2)}) collective-permute-start(bf16[128,1024]{1,0:T(8,128)(2,1)S(1)} %collective-permute-done.1.a1), channel_id=1, source_target_pairs={{0,4},{1,5},{2,6},{3,7},{4,8},{5,9},{6,10},{7,11},{8,12},{9,13},{1... | collective-permute-start | bytes 786440 | tf_op jit(solution)/shard_map/ppermute | solution.py:343
  77.7 14.7 %collective-permute-start.6 = (bf16[128,1024]{1,0:T(8,128)(2,1)}, bf16[128,1024]{1,0:T(8,128)(2,1)S(1)}, u32[]{:S(2)}, u32[]{:S(2)}) collective-permute-start(bf16[128,1024]{1,0:T(8,128)(2,1)} %collective-permute-done.4.b2), channel_id=1, source_target_pairs={{0,12},{1,13},{2,14},{3,15},{4,0},{5,1},{6,2},{7,3},{8,4},{9,5},{1... | collective-permute-start | bytes 786440 | tf_op jit(solution)/shard_map/ppermute | solution.py:344
  98.4 2.7 %collective-permute-start.7 = (bf16[64,1024]{1,0:T(8,128)(2,1)S(1)}, bf16[64,1024]{1,0:T(8,128)(2,1)S(1)}, u32[]{:S(2)}, u32[]{:S(2)}) collective-permute-start(bf16[64,1024]{1,0:T(8,128)(2,1)S(1)} %get-tuple-element.22), channel_id=1, source_target_pairs={{0,1},{1,0},{2,3},{3,2},{4,5},{5,4},{6,7},{7,6},{8,9},{9,8},{10,11... | collective-permute-start | bytes 393224 | tf_op jit(solution)/shard_map/ppermute | solution.py:387
  98.5 6.9 %collective-permute-start.8 = (bf16[64,1024]{1,0:T(8,128)(2,1)S(1)}, bf16[64,1024]{1,0:T(8,128)(2,1)S(1)}, u32[]{:S(2)}, u32[]{:S(2)}) collective-permute-start(bf16[64,1024]{1,0:T(8,128)(2,1)S(1)} %get-tuple-element.23), channel_id=1, source_target_pairs={{0,2},{1,3},{2,0},{3,1},{4,6},{5,7},{6,4},{7,5},{8,10},{9,11},{10,... | collective-permute-start | bytes 393224 | tf_op jit(solution)/shard_map/ppermute | solution.py:387
  101.0 6.6 %collective-permute-start.9 = (bf16[64,1024]{1,0:T(8,128)(2,1)S(1)}, bf16[64,1024]{1,0:T(8,128)(2,1)S(1)}, u32[]{:S(2)}, u32[]{:S(2)}) collective-permute-start(bf16[64,1024]{1,0:T(8,128)(2,1)S(1)} %get-tuple-element.24), channel_id=1, source_target_pairs={{0,3},{1,2},{2,1},{3,0},{4,7},{5,6},{6,5},{7,4},{8,11},{9,10},{10,... | collective-permute-start | bytes 393224 | tf_op jit(solution)/shard_map/ppermute | solution.py:387
  107.9 16.9 %copy-start.15 = (bf16[1024,100]{0,1:T(8,128)(2,1)S(1)}, bf16[1024,100]{0,1:T(8,128)(2,1)}, u32[]{:S(2)}) copy-start(bf16[1024,100]{0,1:T(8,128)(2,1)} %param.19) | copy-start | bytes 614404
  107.9 8.0 %collective-permute-start.10 = (bf16[64,1024]{1,0:T(8,128)(2,1)S(1)}, bf16[64,1024]{1,0:T(8,128)(2,1)S(1)}, u32[]{:S(2)}, u32[]{:S(2)}) collective-permute-start(bf16[64,1024]{1,0:T(8,128)(2,1)S(1)} %get-tuple-element.26.h0), channel_id=1, source_target_pairs={{0,8},{1,9},{2,10},{3,11},{4,12},{5,13},{6,14},{7,15},{8,0},{9,1},... | collective-permute-start | bytes 393224 | tf_op jit(solution)/shard_map/ppermute | solution.py:400
  110.1 7.7 %collective-permute-start.11 = (bf16[64,1024]{1,0:T(8,128)(2,1)S(1)}, bf16[64,1024]{1,0:T(8,128)(2,1)S(1)}, u32[]{:S(2)}, u32[]{:S(2)}) collective-permute-start(bf16[64,1024]{1,0:T(8,128)(2,1)S(1)} %get-tuple-element.26.h0), channel_id=1, source_target_pairs={{0,4},{1,5},{2,6},{3,7},{4,8},{5,9},{6,10},{7,11},{8,12},{9,13},{1... | collective-permute-start | bytes 393224 | tf_op jit(solution)/shard_map/ppermute | solution.py:401
  110.1 7.7 %collective-permute-start.12 = (bf16[64,1024]{1,0:T(8,128)(2,1)S(1)}, bf16[64,1024]{1,0:T(8,128)(2,1)S(1)}, u32[]{:S(2)}, u32[]{:S(2)}) collective-permute-start(bf16[64,1024]{1,0:T(8,128)(2,1)S(1)} %get-tuple-element.26.h0), channel_id=1, source_target_pairs={{0,12},{1,13},{2,14},{3,15},{4,0},{5,1},{6,2},{7,3},{8,4},{9,5},{1... | collective-permute-start | bytes 393224 | tf_op jit(solution)/shard_map/ppermute | solution.py:402
  120.9 8.0 %collective-permute-start.16 = (bf16[64,1024]{1,0:T(8,128)(2,1)S(1)}, bf16[64,1024]{1,0:T(8,128)(2,1)S(1)}, u32[]{:S(2)}, u32[]{:S(2)}) collective-permute-start(bf16[64,1024]{1,0:T(8,128)(2,1)S(1)} %get-tuple-element.28), channel_id=1, source_target_pairs={{0,8},{1,9},{2,10},{3,11},{4,12},{5,13},{6,14},{7,15},{8,0},{9,1},... | collective-permute-start | bytes 393224 | tf_op jit(solution)/shard_map/ppermute | solution.py:413
  122.8 6.2 %collective-permute-start.17 = (bf16[64,1024]{1,0:T(8,128)(2,1)S(1)}, bf16[64,1024]{1,0:T(8,128)(2,1)S(1)}, u32[]{:S(2)}, u32[]{:S(2)}) collective-permute-start(bf16[64,1024]{1,0:T(8,128)(2,1)S(1)} %get-tuple-element.29), channel_id=1, source_target_pairs={{0,12},{1,13},{2,14},{3,15},{4,0},{5,1},{6,2},{7,3},{8,4},{9,5},{1... | collective-permute-start | bytes 393224 | tf_op jit(solution)/shard_map/ppermute | solution.py:414
  124.3 6.5 %collective-permute-start.18 = (bf16[64,1024]{1,0:T(8,128)(2,1)S(1)}, bf16[64,1024]{1,0:T(8,128)(2,1)S(1)}, u32[]{:S(2)}, u32[]{:S(2)}) collective-permute-start(bf16[64,1024]{1,0:T(8,128)(2,1)S(1)} %get-tuple-element.30), channel_id=1, source_target_pairs={{0,4},{1,5},{2,6},{3,7},{4,8},{5,9},{6,10},{7,11},{8,12},{9,13},{1... | collective-permute-start | bytes 393224 | tf_op jit(solution)/shard_map/ppermute | solution.py:415
  132.0 14.7 %all-to-all-start.1 = ((f32[16,64,100]{2,1,0:T(8,128)}), f32[16,64,100]{2,1,0:T(8,128)S(1)}, u32[]{:S(2)}, u32[]{:S(2)}) async-start(f32[16,64,100]{2,1,0:T(8,128)} %shard_map.146), calls=%async_computation.1 | async-start | bytes 1048576 | tf_op jit(solution)/shard_map/all_to_all | solution.py:283
  146.7 15.8 %collective-permute-start.19 = (f32[8,100]{1,0:T(8,128)S(1)}, f32[8,100]{1,0:T(8,128)S(1)}, u32[]{:S(2)}, u32[]{:S(2)}) collective-permute-start(f32[8,100]{1,0:T(8,128)S(1)} %get-tuple-element.39), channel_id=1, source_target_pairs={{0,16},{16,32},{32,48},{48,64},{64,80},{80,96},{96,112},{112,128},... | collective-permute-start | bytes 9608 | tf_op jit(solution)/shard_map/ppermute | solution.py:438
  150.3 12.3 %collective-permute-start.20 = (f32[8,100]{1,0:T(8,128)S(1)}, f32[8,100]{1,0:T(8,128)S(1)}, u32[]{:S(2)}, u32[]{:S(2)}) collective-permute-start(f32[8,100]{1,0:T(8,128)S(1)} %get-tuple-element.38), channel_id=1, source_target_pairs={{16,0},{32,16},{48,32},{64,48},{80,64},{96,80},{112,96},{128,112},... | collective-permute-start | bytes 9608 | tf_op jit(solution)/shard_map/ppermute | solution.py:439
  165.1 15.1 %all-to-all-start.2 = ((bf16[16,72,192]{2,1,0:T(8,128)(2,1)}), bf16[16,72,192]{2,1,0:T(8,128)(2,1)S(1)}, u32[]{:S(2)}, u32[]{:S(2)}) async-start(bf16[16,72,192]{2,1,0:T(8,128)(2,1)} %shard_map.148), calls=%async_computation.2 | async-start | bytes 1179648 | tf_op jit(solution)/shard_map/all_to_all | solution.py:283
  173.4 6.8 %copy-start.14 = (f32[2,768]{1,0:T(2,128)S(1)}, f32[2,768]{1,0:T(2,128)}, u32[]{:S(2)}) copy-start(f32[2,768]{1,0:T(2,128)} %alpha_ref.1) | copy-start | bytes 18436
  (10 other events, 16.2 us)
Sparse Core Ops, SparseCore 0:
  13.2 87.6 all-gather.2

commit v5 on v4

--- a/solution.py
+++ b/solution.py
@@ -16,8 +16,6 @@
 epsilon = 1e-06
 bf16 = jnp.bfloat16
 f32 = jnp.float32
-
-J_GROUPS = [[4 * x + j for j in range(4)] for x in range(4)]
 
 
 def norm_rows(rows, offset_row, scale_row):
@@ -57,17 +55,27 @@
     return pl.CostEstimate(flops=flops, bytes_accessed=nbytes, transcendentals=trans)
 
 
-def first_weights_kernel(w_ref, o_ref, pre_ref, dil_ref, plain_ref, a_ref, b_ref, voc_ref):
-    a_ref[0:64, :] = w_ref[0]
-    a_ref[64:128, :] = w_ref[1]
-    b_ref[0:64, :] = w_ref[2]
-    b_ref[64:128, :] = o_ref[...]
+def first_weights_kernel(
+    w_ref, o_ref, pre_ref, dil_ref, plain_ref, a_ref, b_ref, voc_ref, pre_scratch, sems
+):
+    moves = (
+        (w_ref.at[0], a_ref.at[pl.ds(0, 64), :]),
+        (w_ref.at[1], a_ref.at[pl.ds(64, 64), :]),
+        (w_ref.at[2], b_ref.at[pl.ds(0, 64), :]),
+        (o_ref, b_ref.at[pl.ds(64, 64), :]),
+        (dil_ref, voc_ref.at[pl.ds(96, 144), :]),
+        (plain_ref, voc_ref.at[pl.ds(240, 144), :]),
+        (pre_ref, pre_scratch),
+    )
+    copies = [pltpu.make_async_copy(src, dst, sems.at[n]) for n, (src, dst) in enumerate(moves)]
+    for copy in copies:
+        copy.start()
     voc_ref[0:96, :] = jnp.zeros((96, 768), bf16)
+    copies[6].wait()
     for k in range(7):
-        voc_ref[0:96, 100 * k : 100 * k + 100] = pre_ref[k]
-    for k in range(3):
-        voc_ref[96 + 48 * k : 144 + 48 * k, :] = dil_ref[k]
-        voc_ref[240 + 48 * k : 288 + 48 * k, :] = plain_ref[k]
+        voc_ref[0:96, 100 * k : 100 * k + 100] = pre_scratch[k]
+    for copy in copies[:6]:
+        copy.wait()
 
 
 def mlp_weights_kernel(up_ref, down_ref, out_ref):
@@ -85,20 +93,34 @@
             out_ref[s, :, 48 * t : 48 * t + 48] = w_ref[tap, :, 48 * s : 48 * s + 48]
 
 
-def attention_kernel(
-    flag_ref, own_ref, back_ref, mod_ref, a0, b0, a1, b1, a2, b2, a3, b3, o0, o1, o2, o3, heads, w_out, total_out
-):
+def attention_kernel(flag_ref, mod_ref, *refs):
+    row_refs, weight_refs = refs[:8], refs[8:16]
+    o0, o1, o2, o3, rows, w_a, w_v, w_out, heads, sems = refs[16:]
+    copies = []
+    for n, ref in enumerate(row_refs):
+        copies.append((ref, rows.at[pl.ds(64 * n, 64), :]))
+    for h in range(4):
+        first_half, second_half = weight_refs[2 * h], weight_refs[2 * h + 1]
+        copies.append((first_half, w_a.at[h]))
+        copies.append((second_half.at[pl.ds(0, 64), :], w_v.at[h]))
+        copies.append((second_half.at[pl.ds(64, 64), :], w_out.at[pl.ds(64 * h, 64), :]))
+    copies = [pltpu.make_async_copy(src, dst, sems.at[n]) for n, (src, dst) in enumerate(copies)]
+    for copy in copies:
+        copy.start()
     first = flag_ref[0] > 0
     scale = 1.0 / math.sqrt(HEAD_DIM)
-    shift, gain = mod_ref[0:1, :], mod_ref[1:2, :]
-    own = norm_rows(own_ref[...], shift, gain).astype(bf16)
-    back = norm_rows(back_ref[...], shift, gain).astype(bf16)
-    for h, (wa, wb) in enumerate(((a0, b0), (a1, b1), (a2, b2), (a3, b3))):
-        qk = mm_t(own, wa[0:128, :]).astype(bf16)
+    for copy in copies[:8]:
+        copy.wait()
+    normed = norm_rows(rows[...], mod_ref[0:1, :], mod_ref[1:2, :]).astype(bf16)
+    own, back = normed[:BLK], normed[BLK:]
+    for copy in copies[8:]:
+        copy.wait()
+    for h in range(4):
+        qk = mm_t(own, w_a[h]).astype(bf16)
         q, k = qk[:, 0:64], qk[:, 64:128]
-        v = mm_t(own, wb[0:64, :]).astype(bf16)
-        kb = mm_t(back, wa[64:128, :]).astype(bf16)
-        vb = mm_t(back, wb[0:64, :]).astype(bf16)
+        v = mm_t(own, w_v[h]).astype(bf16)
+        kb = mm_t(back, w_a[h, 64:128, :]).astype(bf16)
+        vb = mm_t(back, w_v[h]).astype(bf16)
         s_own = mm_t(q, k) * scale
         s_back = mm_t(q, kb) * scale
         s_back = jnp.where(first, -1e30, s_back)
@@ -112,11 +134,9 @@
         p_own = (e_own * inv).astype(bf16)
         p_back = (e_back * inv).astype(bf16)
         heads[:, 64 * h : 64 * h + 64] = (mm(p_own, v) + mm(p_back, vb)).astype(bf16)
-        w_out[64 * h : 64 * h + 64, :] = wb[64:128, :]
-    total_out[...] = mm(heads[...], w_out[...]).astype(bf16)
+    total = mm(heads[...], w_out[...]).astype(bf16)
     for k, out in enumerate((o0, o1, o2, o3)):
-        start = pl.multiple_of(64 * (flag_ref[1] ^ k), 64)
-        out[...] = total_out[pl.ds(start, 64), :]
+        out[...] = total[64 * k : 64 * k + 64]
 
 
 def sum_of(p0, p1, p2, p3):
@@ -273,10 +293,6 @@
         after = y[2][p + 1] if p <= 2 else shifted(y[2][0], -1)
         total = ups[p] + (before + y[1][p] + after)
         out_ref[:, 768 * p : 768 * p + 768] = shifted(total, -1)[0:64].astype(bf16)
-
-
-def gather(value, groups):
-    return lax.all_gather(value, "sub", axis=0, tiled=True, axis_index_groups=groups)
 
 
 def exchange(value, groups=None, axis="sub"):
@@ -329,11 +345,21 @@
 
     to_right = [(i, (i + 4) % 16) for i in range(16)]
     to_left = [(i, (i - 4) % 16) for i in range(16)]
-    own_a, own_b, w_voc = whole(
+    own_a, own_b, w_voc = pl.pallas_call(
         first_weights_kernel,
-        (shape((128, 1024), bf16), shape((128, 1024), bf16), shape((384, 768), bf16)),
-        (jnp.swapaxes(w_project, 1, 2), w_heads_out, w_prelude, w_dilated, w_plain),
-        cost=cost_of(0, 3 << 20),
+        out_shape=(shape((128, 1024), bf16), shape((128, 1024), bf16), shape((384, 768), bf16)),
+        in_specs=[pl.BlockSpec(memory_space=pl.ANY)] * 5,
+        out_specs=vmem_specs(3),
+        scratch_shapes=[pltpu.VMEM((7, 96, 100), bf16), pltpu.SemaphoreType.DMA((7,))],
+        compiler_params=pltpu.CompilerParams(vmem_limit_bytes=60 << 20),
+        cost_estimate=cost_of(0, 3 << 20),
+        name="first_weights",
+    )(
+        jnp.swapaxes(w_project, 1, 2),
+        w_heads_out,
+        w_prelude,
+        w_dilated.reshape(144, 768),
+        w_plain.reshape(144, 768),
     )
     back_frames = lax.ppermute(frames, both, [(i, i + 4) for i in range(n_all - 4)])
     left_a = lax.ppermute(own_a, "sub", to_right)
@@ -345,8 +371,9 @@
 
     w_voc = lax.all_gather(w_voc, "sub", axis=0, tiled=False)
 
-    block = gather(frames, J_GROUPS)
-    back = gather(back_frames, J_GROUPS)
+    beside = [[(i, i ^ k) for i in range(16)] for k in (1, 2, 3)]
+    block = [frames] + [lax.ppermute(frames, "sub", beside[k - 1]) for k in (1, 2, 3)]
+    back = [back_frames] + [lax.ppermute(back_frames, "sub", beside[k - 1]) for k in (1, 2, 3)]
 
     own_mlp = whole(
         mlp_weights_kernel, shape((2048, 256), bf16), (w_up, w_down), cost=cost_of(0, 2 << 20)
@@ -361,31 +388,40 @@
 
     is_first = (time_index == 0) & (sub_index < 4)
     quarter = shape((own_rows, 1024), bf16)
-    partial = whole(
+    partial = pl.pallas_call(
         attention_kernel,
-        (quarter,) * 4,
-        (
-            jnp.stack([is_first.astype(jnp.int32), lax.rem(sub_index, 4)]),
-            block,
-            back,
-            modulation,
-            own_a,
-            own_b,
-            left_a,
-            left_b,
-            right_a,
-            right_b,
-            far_a,
-            far_b,
-        ),
-        scratch=[pltpu.VMEM((BLK, 256), bf16)] + [pltpu.VMEM((256, 1024), bf16)] * 2,
-        cost=cost_of(10**9, 4 << 20, 1 << 19),
-        smem=1,
+        out_shape=(quarter,) * 4,
+        in_specs=[pl.BlockSpec(memory_space=pltpu.SMEM)]
+        + vmem_specs(1)
+        + [pl.BlockSpec(memory_space=pl.ANY)] * 16,
+        out_specs=vmem_specs(4),
+        scratch_shapes=[
+            pltpu.VMEM((2 * BLK, 1024), bf16),
+            pltpu.VMEM((4, 128, 1024), bf16),
+            pltpu.VMEM((4, 64, 1024), bf16),
+            pltpu.VMEM((256, 1024), bf16),
+            pltpu.VMEM((BLK, 256), bf16),
+            pltpu.SemaphoreType.DMA((20,)),
+        ],
+        compiler_params=pltpu.CompilerParams(vmem_limit_bytes=60 << 20),
+        cost_estimate=cost_of(10**9, 4 << 20, 1 << 19),
+        name="attention",
+    )(
+        is_first.astype(jnp.int32).reshape(1),
+        modulation,
+        *block,
+        *back,
+        own_a,
+        own_b,
+        left_a,
+        left_b,
+        right_a,
+        right_b,
+        far_a,
+        far_b,
     )
     ups = exchange(ups, OTHER_GROUPS, both)
-    parts = [partial[0]] + [
-        lax.ppermute(partial[k], "sub", [(i, i ^ k) for i in range(16)]) for k in (1, 2, 3)
-    ]
+    parts = [partial[0]] + [lax.ppermute(partial[k], "sub", beside[k - 1]) for k in (1, 2, 3)]
     mixed_rows, own_norm = whole(
         after_attention_kernel,
         (quarter, quarter),

time: 196 us -> 207 us (1.056)
  blocking collectives: 23.8 us -> 0 us
  waiting for transfers between devices: 66.3 us -> 86.4 us
  starting transfers between devices: 47.7 us -> 61.5 us
  Pallas kernels: 21.9 us -> 26 us
  local copies, waits for them, and re-layouts: 17.9 us -> 14.1 us
    all_gather x2 -> x0, blocking collectives: 23.8 us -> none  [gather(): lax.all_gather(value, 'sub', axis=0, tiled=True, axis_index_groups=groups)]
    pallas_call x0 -> x2, Pallas kernels: none -> 11.1 us  [the longest x1 8.46 us: program(): pl.pallas_call(attention_kernel, out_shape=(quarter,) * 4, in_specs=[pl.B...]
    ppermute x3 -> x9, waiting for transfers between devices: 6.57 us -> 16 us  [the longest x3 9.49 us: program(): lax.ppermute(back_frames, 'sub', beside[k - 1])]
    ppermute x1, waiting for transfers between devices: 0.01 us -> 7.31 us  [program(): right_a = lax.ppermute(own_a, 'sub', to_left)]
    pallas_call x10 -> x8, Pallas kernels: 21.4 us -> 14.4 us  [whole(): pl.pallas_call(kernel, out_shape=out_shapes, in_specs=[pl.BlockSpec(memor...]
    ppermute x3 -> x9, starting transfers between devices: 2.67 us -> 8.7 us  [the longest x3 3.56 us: program(): lax.ppermute(frames, 'sub', beside[k - 1])]
    ppermute x1, waiting for transfers between devices: 2.38 us -> 7.42 us  [program(): far_b = lax.ppermute(right_b, 'sub', to_left)]
    unnamed x37 -> x53, local copies, waits for them, and re-layouts: 16.9 us -> 13.1 us
  transfers between devices with their start and end apart: 25 -> 31, of which waited for: 11 -> 16; matrix products, arithmetic and copies ran while one was open for 3% -> 2% of each run, Pallas kernels for 7% -> 8%
where the time goes in v5:
time: 207 us; the launch traced here: 206 us
  waiting for transfers between devices  86.4 us (42%)
  starting transfers between devices  61.5 us (30%)
  Pallas kernels  26 us (13%)
  between operations  14.4 us (7%)
  local copies, waits for them, and re-layouts  14.1 us (7%)
  matrix products  3.39 us (2%)
    ppermute x1, waiting for transfers between devices, program(): other_y = lax.ppermute(own_mlp, both, OTHER_Y)  22.4 us
    pallas_call x8, Pallas kernels, whole(): pl.pallas_call(kernel, out_shape=out_shapes, in_specs=[pl.BlockSpec(memor...  14.4 us
    all_to_all x3, waiting for transfers between devices, exchange(): lax.all_to_all(value, axis, 0, 0, tiled=True, axis_index_groups=groups)  14.2 us
    unnamed x53, local copies, waits for them, and re-layouts  13.1 us
    all_to_all x3, starting transfers between devices, exchange(): lax.all_to_all(value, axis, 0, 0, tiled=True, axis_index_groups=groups)  12.3 us
    ppermute x3, waiting for transfers between devices, program(): lax.ppermute(back_frames, 'sub', beside[k - 1])  9.49 us
    pallas_call x1, Pallas kernels, program(): pl.pallas_call(attention_kernel, out_shape=(quarter,) * 4, in_specs=[pl.B...  8.46 us
    ppermute x1, starting transfers between devices, program(): lax.ppermute(mel_all[0, :8], 'tm', [(i + 1, i) for i in range(n_tm - 1)])  7.56 us
  transfers between devices with their start and end apart: 31, of which 16 were waited for; matrix products, arithmetic and copies ran while one was open for 2% of the time, Pallas kernels for 8%

profile of v5, /device:TPU:16, one launch (start us, length us, event | category | flops | bytes accessed | tf_op | source)
XLA Modules:
  0.0 206.0 jit_solution(4065333553196831352)
XLA Ops:
  7.2 2.6 %first_weights.1 = (bf16[128,1024]{1,0:T(8,128)(2,1)}, bf16[128,1024]{1,0:T(8,128)(2,1)}, bf16[384,768]{1,0:T(8,128)(2,1)}) custom-call(bf16[3,64,1024]{2,1,0:T(8,128)(2,1)} %bitcast.20, bf16[64,1024]{1,0:T(8,128)(2,1)} %o_ref.1, bf16[7,96,100]{2,1,0:T(8,128)(2,1)} %pre_ref.1, bf16[144,768]{1,0:T(8,128)(2,1)} %bitcast.21, bf16[144,768]{1,0:T(8,128)(2,1)} %bitcast.22), custom_call_target="tpu_custom_call" | custom-call | bytes 3145728 | tf_op jit(solution)/shard_map/first_weights/pallas_call | solution.py:348
  13.7 4.9 %all-to-all-start = ((bf16[16,96,384]{2,1,0:T(8,128)(2,1)}), bf16[16,96,384]{2,1,0:T(8,128)(2,1)}, u32[]{:S(2)}, u32[]{:S(2)}) async-start(bf16[16,96,384]{2,1,0:T(8,128)(2,1)} %shard_map.141), calls=%async_computation | async-start | bytes 2359296 | tf_op jit(solution)/shard_map/all_to_all | solution.py:299
  19.1 3.5 %collective-permute-start.3 = (bf16[64,1024]{1,0:T(8,128)(2,1)S(1)}, bf16[64,1024]{1,0:T(8,128)(2,1)S(1)}, u32[]{:S(2)}, u32[]{:S(2)}) collective-permute-start(bf16[64,1024]{1,0:T(8,128)(2,1)S(1)} %copy-done.7), channel_id=1, source_target_pairs={{0,4},{1,5},{2,6},{3,7},{4,8},{5,9},{6,10},{7,11},{8,12},{9,13},{1... | collective-permute-start | bytes 393224 | tf_op jit(solution)/shard_map/ppermute | solution.py:364
  22.7 3.1 %collective-permute-start.1 = (bf16[64,1024]{1,0:T(8,128)(2,1)S(1)}, bf16[64,1024]{1,0:T(8,128)(2,1)S(1)}, u32[]{:S(2)}, u32[]{:S(2)}) collective-permute-start(bf16[64,1024]{1,0:T(8,128)(2,1)S(1)} %copy-done.7), channel_id=1, source_target_pairs={{0,2},{1,3},{2,0},{3,1},{4,6},{5,7},{6,4},{7,5},{8,10},{9,11},{10,... | collective-permute-start | bytes 393224 | tf_op jit(solution)/shard_map/ppermute | solution.py:375
  26.0 22.4 %collective-permute-done.20.w2 = bf16[2048,256]{1,0:T(8,128)(2,1)S(1)} collective-permute-done((bf16[2048,256]{1,0:T(8,128)(2,1)S(1)}, bf16[2048,256]{1,0:T(8,128)(2,1)S(1)}, u32[]{:S(2)}, u32[]{:S(2)}) %collective-permute-start.20) | collective-permute-done | bytes 1048608 | tf_op jit(solution)/shard_map/ppermute | solution.py:382
  48.9 2.6 %collective-permute-start.5 = (bf16[64,1024]{1,0:T(8,128)(2,1)S(1)}, bf16[64,1024]{1,0:T(8,128)(2,1)S(1)}, u32[]{:S(2)}, u32[]{:S(2)}) collective-permute-start(bf16[64,1024]{1,0:T(8,128)(2,1)S(1)} %collective-permute-done.3.refs_4_), channel_id=1, source_target_pairs={{0,2},{1,3},{2,0},{3,1},{4,6},{5,7},{6,4},{7,5},{8,10},{9,11},{10,... | collective-permute-start | bytes 393224 | tf_op jit(solution)/shard_map/ppermute | solution.py:376
  51.6 2.6 %collective-permute-start.7 = (bf16[128,1024]{1,0:T(8,128)(2,1)S(1)}, bf16[128,1024]{1,0:T(8,128)(2,1)S(1)}, u32[]{:S(2)}, u32[]{:S(2)}) collective-permute-start(bf16[128,1024]{1,0:T(8,128)(2,1)S(1)} %copy-done.13), channel_id=1, source_target_pairs={{0,4},{1,5},{2,6},{3,7},{4,8},{5,9},{6,10},{7,11},{8,12},{9,13},{1... | collective-permute-start | bytes 786440 | tf_op jit(solution)/shard_map/ppermute | solution.py:365
  54.2 4.2 %collective-permute-done.5.refs_6_ = bf16[64,1024]{1,0:T(8,128)(2,1)S(1)} collective-permute-done((bf16[64,1024]{1,0:T(8,128)(2,1)S(1)}, bf16[64,1024]{1,0:T(8,128)(2,1)S(1)}, u32[]{:S(2)}, u32[]{:S(2)}) %collective-permute-start.5) | collective-permute-done | bytes 131104 | tf_op jit(solution)/shard_map/ppermute | solution.py:376
  58.5 5.3 %collective-permute-done.6.refs_7_ = bf16[64,1024]{1,0:T(8,128)(2,1)S(1)} collective-permute-done((bf16[64,1024]{1,0:T(8,128)(2,1)S(1)}, bf16[64,1024]{1,0:T(8,128)(2,1)S(1)}, u32[]{:S(2)}, u32[]{:S(2)}) %collective-permute-start.6) | collective-permute-done | bytes 131104 | tf_op jit(solution)/shard_map/ppermute | solution.py:376
  63.8 3.6 %collective-permute-start.10 = (bf16[128,1024]{1,0:T(8,128)(2,1)S(1)}, bf16[128,1024]{1,0:T(8,128)(2,1)}, u32[]{:S(2)}, u32[]{:S(2)}) collective-permute-start(bf16[128,1024]{1,0:T(8,128)(2,1)S(1)} %copy-done.14), channel_id=1, source_target_pairs={{0,12},{1,13},{2,14},{3,15},{4,0},{5,1},{6,2},{7,3},{8,4},{9,5},{1... | collective-permute-start | bytes 786440 | tf_op jit(solution)/shard_map/ppermute | solution.py:366
  67.4 3.1 %collective-permute-start.9 = (bf16[128,1024]{1,0:T(8,128)(2,1)S(1)}, bf16[128,1024]{1,0:T(8,128)(2,1)}, u32[]{:S(2)}, u32[]{:S(2)}) collective-permute-start(bf16[128,1024]{1,0:T(8,128)(2,1)S(1)} %copy-done.13), channel_id=1, source_target_pairs={{0,12},{1,13},{2,14},{3,15},{4,0},{5,1},{6,2},{7,3},{8,4},{9,5},{1... | collective-permute-start | bytes 786440 | tf_op jit(solution)/shard_map/ppermute | solution.py:368
  70.5 7.0 %collective-permute-done.8.refs_11_ = bf16[128,1024]{1,0:T(8,128)(2,1)S(1)} collective-permute-done((bf16[128,1024]{1,0:T(8,128)(2,1)S(1)}, bf16[128,1024]{1,0:T(8,128)(2,1)S(1)}, u32[]{:S(2)}, u32[]{:S(2)}) %collective-permute-start.8) | collective-permute-done | bytes 262176 | tf_op jit(solution)/shard_map/ppermute | solution.py:367
  82.2 7.3 %collective-permute-done.9.refs_12_ = bf16[128,1024]{1,0:T(8,128)(2,1)} collective-permute-done((bf16[128,1024]{1,0:T(8,128)(2,1)S(1)}, bf16[128,1024]{1,0:T(8,128)(2,1)}, u32[]{:S(2)}, u32[]{:S(2)}) %collective-permute-start.9) | collective-permute-done | bytes 262176 | tf_op jit(solution)/shard_map/ppermute | solution.py:368
  91.8 7.4 %collective-permute-done.12.refs_15_ = bf16[128,1024]{1,0:T(8,128)(2,1)S(1)} collective-permute-done((bf16[128,1024]{1,0:T(8,128)(2,1)}, bf16[128,1024]{1,0:T(8,128)(2,1)S(1)}, u32[]{:S(2)}, u32[]{:S(2)}) %collective-permute-start.12) | collective-permute-done | bytes 262176 | tf_op jit(solution)/shard_map/ppermute | solution.py:370
  100.0 8.5 %attention.1 = (bf16[64,1024]{1,0:T(8,128)(2,1)}, bf16[64,1024]{1,0:T(8,128)(2,1)}, bf16[64,1024]{1,0:T(8,128)(2,1)}, bf16[64,1024]{1,0:T(8,128)(2,1)}) custom-call(s32[1]{0:T(128)} %bitcast.flag_ref, f32[8,1024]{1,0:T(8,128)} %mod_ref.5, bf16[64,1024]{1,0:T(8,128)(2,1)} %frames_ref.1, bf16[64,1024]{1,0:T(8,128)(2,1)} %copy-done.18, ...), custom_call_target="tpu_custom_call" | custom-call | flops 1000000000 | bytes 4194304 | tf_op jit(solution)/shard_map/attention/pallas_call | solution.py:391
  110.4 4.8 %collective-permute-done.14.p2 = bf16[64,1024]{1,0:T(8,128)(2,1)S(1)} collective-permute-done((bf16[64,1024]{1,0:T(8,128)(2,1)}, bf16[64,1024]{1,0:T(8,128)(2,1)S(1)}, u32[]{:S(2)}, u32[]{:S(2)}) %collective-permute-start.14) | collective-permute-done | bytes 131104 | tf_op jit(solution)/shard_map/ppermute | solution.py:424
  118.1 3.3 %collective-permute-start.16 = (bf16[64,1024]{1,0:T(8,128)(2,1)S(1)}, bf16[64,1024]{1,0:T(8,128)(2,1)S(1)}, u32[]{:S(2)}, u32[]{:S(2)}) collective-permute-start(bf16[64,1024]{1,0:T(8,128)(2,1)S(1)} %get-tuple-element.26.h0), channel_id=1, source_target_pairs={{0,8},{1,9},{2,10},{3,11},{4,12},{5,13},{6,14},{7,15},{8,0},{9,1},... | collective-permute-start | bytes 393224 | tf_op jit(solution)/shard_map/ppermute | solution.py:436
  121.4 3.2 %collective-permute-start.18 = (bf16[64,1024]{1,0:T(8,128)(2,1)S(1)}, bf16[64,1024]{1,0:T(8,128)(2,1)S(1)}, u32[]{:S(2)}, u32[]{:S(2)}) collective-permute-start(bf16[64,1024]{1,0:T(8,128)(2,1)S(1)} %get-tuple-element.26.h0), channel_id=1, source_target_pairs={{0,12},{1,13},{2,14},{3,15},{4,0},{5,1},{6,2},{7,3},{8,4},{9,5},{1... | collective-permute-start | bytes 393224 | tf_op jit(solution)/shard_map/ppermute | solution.py:438
  128.5 3.1 %shard_map.143 = (bf16[64,1024]{1,0:T(8,128)(2,1)S(1)}, bf16[64,1024]{1,0:T(8,128)(2,1)S(1)}, bf16[64,1024]{1,0:T(8,128)(2,1)S(1)}, bf16[64,1024]{1,0:T(8,128)(2,1)S(1)}) custom-call(bf16[64,1024]{1,0:T(8,128)(2,1)S(1)} %get-tuple-element.26.h0, bf16[64,1024]{1,0:T(8,128)(2,1)S(1)} %collective-permute-done.16.h1, ...), custom_call_target="tpu_custom_call" | custom-call | flops 1100000000 | bytes 5242880 | tf_op jit(solution)/shard_map/pallas_call | solution.py:43
  133.3 2.6 %collective-permute-start.23 = (bf16[64,1024]{1,0:T(8,128)(2,1)S(1)}, bf16[64,1024]{1,0:T(8,128)(2,1)S(1)}, u32[]{:S(2)}, u32[]{:S(2)}) collective-permute-start(bf16[64,1024]{1,0:T(8,128)(2,1)S(1)} %get-tuple-element.29), channel_id=1, source_target_pairs={{0,12},{1,13},{2,14},{3,15},{4,0},{5,1},{6,2},{7,3},{8,4},{9,5},{1... | collective-permute-start | bytes 393224 | tf_op jit(solution)/shard_map/ppermute | solution.py:450
  136.3 2.9 %collective-permute-done.22.p1 = bf16[64,1024]{1,0:T(8,128)(2,1)S(1)} collective-permute-done((bf16[64,1024]{1,0:T(8,128)(2,1)S(1)}, bf16[64,1024]{1,0:T(8,128)(2,1)S(1)}, u32[]{:S(2)}, u32[]{:S(2)}) %collective-permute-start.22) | collective-permute-done | bytes 131104 | tf_op jit(solution)/shard_map/ppermute | solution.py:449
  143.3 3.8 %all-to-all-start.1 = ((f32[16,64,100]{2,1,0:T(8,128)}), f32[16,64,100]{2,1,0:T(8,128)S(1)}, u32[]{:S(2)}, u32[]{:S(2)}) async-start(f32[16,64,100]{2,1,0:T(8,128)} %shard_map.144), calls=%async_computation.1 | async-start | bytes 1048576 | tf_op jit(solution)/shard_map/all_to_all | solution.py:299
  147.2 10.7 %all-to-all-done.1.mel_ref = f32[16,64,100]{2,1,0:T(8,128)S(1)} async-done(((f32[16,64,100]{2,1,0:T(8,128)}), f32[16,64,100]{2,1,0:T(8,128)S(1)}, u32[]{:S(2)}, u32[]{:S(2)}) %all-to-all-start.1) | async-done | bytes 409632 | tf_op jit(solution)/shard_map/all_to_all | solution.py:299
  157.9 3.7 %collective-permute-start.25 = (f32[8,100]{1,0:T(8,128)S(1)}, f32[8,100]{1,0:T(8,128)S(1)}, u32[]{:S(2)}, u32[]{:S(2)}) collective-permute-start(f32[8,100]{1,0:T(8,128)S(1)} %get-tuple-element.39), channel_id=1, source_target_pairs={{0,16},{16,32},{32,48},{48,64},{64,80},{80,96},{96,112},{112,128},... | collective-permute-start | bytes 9608 | tf_op jit(solution)/shard_map/ppermute | solution.py:474
  161.7 7.6 %collective-permute-start.26 = (f32[8,100]{1,0:T(8,128)S(1)}, f32[8,100]{1,0:T(8,128)S(1)}, u32[]{:S(2)}, u32[]{:S(2)}) collective-permute-start(f32[8,100]{1,0:T(8,128)S(1)} %get-tuple-element.38), channel_id=1, source_target_pairs={{16,0},{32,16},{48,32},{64,48},{80,64},{96,80},{112,96},{128,112},... | collective-permute-start | bytes 9608 | tf_op jit(solution)/shard_map/ppermute | solution.py:475
  169.3 3.4 %fusion.2.comp_ref = f32[768,384]{1,0:T(8,128)S(1)} fusion(bf16[16,96,384]{2,1,0:T(8,128)(2,1)} %all-to-all-done, bf16[16,384,768]{2,1,0:T(8,128)(2,1)} %bitcast.17), kind=kOutput, calls=%fused_computation.2 | convolution fusion | flops 905969664 | bytes 4718592 | tf_op jit(solution)/shard_map/dot_general | solution.py:464
  175.5 3.6 %all-to-all-start.2 = ((bf16[16,72,192]{2,1,0:T(8,128)(2,1)}), bf16[16,72,192]{2,1,0:T(8,128)(2,1)S(1)}, u32[]{:S(2)}, u32[]{:S(2)}) async-start(bf16[16,72,192]{2,1,0:T(8,128)(2,1)} %shard_map.146), calls=%async_computation.2 | async-start | bytes 1179648 | tf_op jit(solution)/shard_map/all_to_all | solution.py:299
  180.2 3.7 %copy-done.3 = bf16[6144,768]{1,0:T(8,128)(2,1)S(1)} copy-done((bf16[6144,768]{1,0:T(8,128)(2,1)S(1)}, bf16[6144,768]{1,0:T(8,128)(2,1)}, u32[]{:S(2)}) %copy-start.3) | copy-done | bytes 9437208
  184.4 2.8 %copy-done.1 = bf16[16,288,768]{2,1,0:T(8,128)(2,1)} copy-done((bf16[16,288,768]{2,1,0:T(8,128)(2,1)}, bf16[16,288,768]{2,1,0:T(8,128)(2,1)S(1)}, u32[]{:S(2)}) %copy-start.1) | copy-done | bytes 7077912
  187.2 3.5 %all-to-all-done.2.up_ref = bf16[16,72,192]{2,1,0:T(8,128)(2,1)S(1)} async-done(((bf16[16,72,192]{2,1,0:T(8,128)(2,1)}), bf16[16,72,192]{2,1,0:T(8,128)(2,1)S(1)}, u32[]{:S(2)}, u32[]{:S(2)}) %all-to-all-start.2) | async-done | bytes 442400 | tf_op jit(solution)/shard_map/all_to_all | solution.py:299
  190.6 3.0 %copy-done.2 = bf16[16,288,768]{2,1,0:T(8,128)(2,1)S(1)} copy-done((bf16[16,288,768]{2,1,0:T(8,128)(2,1)S(1)}, bf16[16,288,768]{2,1,0:T(8,128)(2,1)}, u32[]{:S(2)}) %copy-start.2) | copy-done | bytes 7077912
  193.6 4.5 %shard_map.147 = bf16[64,3072]{1,0:T(8,128)(2,1)S(1)} custom-call(s32[2]{0:T(128)S(1)} %add_convert_fusion.flag_ref, bf16[16,72,192]{2,1,0:T(8,128)(2,1)S(1)} %all-to-all-done.2.up_ref, f32[2,768]{1,0:T(2,128)S(1)} %copy-done.11, bf16[16,288,768]{2,1,0:T(8,128)(2,1)S(1)} %copy-done.2), custom_call_target="tpu_custom_call" | custom-call | flops 2000000000 | bytes 8388608 | tf_op jit(solution)/shard_map/pallas_call | solution.py:43
  (101 shorter events, 33.3 us)
Async XLA Ops:
  7.2 129.0 %copy-start = (f32[1024,100]{0,1:T(8,128)S(1)}, f32[1024,100]{0,1:T(8,128)}, u32[]{:S(2)}) copy-start(f32[1024,100]{0,1:T(8,128)} %param.20) | copy-start | bytes 1228804
  7.2 162.1 %all-gather.3.cloned.1.call-start = ((), (), s32[]{:S(2)}) async-start(), calls=%async_computation.3 | async-start | bytes 10027008 | tf_op jit(solution)/shard_map/all_gather | solution.py:372
  10.0 38.4 %collective-permute-start.20 = (bf16[2048,256]{1,0:T(8,128)(2,1)S(1)}, bf16[2048,256]{1,0:T(8,128)(2,1)S(1)}, u32[]{:S(2)}, u32[]{:S(2)}) collective-permute-start(bf16[2048,256]{1,0:T(8,128)(2,1)S(1)} %shard_map.142.w0), channel_id=1, source_target_pairs={{0,130},{1,131},{2,128},{3,129},{4,134},{5,135},{6,132},{7,133},{8... | collective-permute-start | bytes 3145736 | tf_op jit(solution)/shard_map/ppermute | solution.py:382
  13.7 104.4 %all-to-all-start = ((bf16[16,96,384]{2,1,0:T(8,128)(2,1)}), bf16[16,96,384]{2,1,0:T(8,128)(2,1)}, u32[]{:S(2)}, u32[]{:S(2)}) async-start(bf16[16,96,384]{2,1,0:T(8,128)(2,1)} %shard_map.141), calls=%async_computation | async-start | bytes 2359296 | tf_op jit(solution)/shard_map/all_to_all | solution.py:299
  18.7 7.1 %collective-permute-start = (bf16[64,1024]{1,0:T(8,128)(2,1)S(1)}, bf16[64,1024]{1,0:T(8,128)(2,1)S(1)}, u32[]{:S(2)}, u32[]{:S(2)}) collective-permute-start(bf16[64,1024]{1,0:T(8,128)(2,1)S(1)} %copy-done.7), channel_id=1, source_target_pairs={{0,1},{1,0},{2,3},{3,2},{4,5},{5,4},{6,7},{7,6},{8,9},{9,8},{10,11... | collective-permute-start | bytes 393224 | tf_op jit(solution)/shard_map/ppermute | solution.py:375
  19.1 29.3 %collective-permute-start.3 = (bf16[64,1024]{1,0:T(8,128)(2,1)S(1)}, bf16[64,1024]{1,0:T(8,128)(2,1)S(1)}, u32[]{:S(2)}, u32[]{:S(2)}) collective-permute-start(bf16[64,1024]{1,0:T(8,128)(2,1)S(1)} %copy-done.7), channel_id=1, source_target_pairs={{0,4},{1,5},{2,6},{3,7},{4,8},{5,9},{6,10},{7,11},{8,12},{9,13},{1... | collective-permute-start | bytes 393224 | tf_op jit(solution)/shard_map/ppermute | solution.py:364
  22.7 26.3 %collective-permute-start.1 = (bf16[64,1024]{1,0:T(8,128)(2,1)S(1)}, bf16[64,1024]{1,0:T(8,128)(2,1)S(1)}, u32[]{:S(2)}, u32[]{:S(2)}) collective-permute-start(bf16[64,1024]{1,0:T(8,128)(2,1)S(1)} %copy-done.7), channel_id=1, source_target_pairs={{0,2},{1,3},{2,0},{3,1},{4,6},{5,7},{6,4},{7,5},{8,10},{9,11},{10,... | collective-permute-start | bytes 393224 | tf_op jit(solution)/shard_map/ppermute | solution.py:375
  25.8 25.7 %collective-permute-start.2 = (bf16[64,1024]{1,0:T(8,128)(2,1)S(1)}, bf16[64,1024]{1,0:T(8,128)(2,1)S(1)}, u32[]{:S(2)}, u32[]{:S(2)}) collective-permute-start(bf16[64,1024]{1,0:T(8,128)(2,1)S(1)} %copy-done.7), channel_id=1, source_target_pairs={{0,3},{1,2},{2,1},{3,0},{4,7},{5,6},{6,5},{7,4},{8,11},{9,10},{10,... | collective-permute-start | bytes 393224 | tf_op jit(solution)/shard_map/ppermute | solution.py:375
  25.8 98.9 %collective-permute-start.19 = (bf16[2048,256]{1,0:T(8,128)(2,1)S(1)}, bf16[2048,256]{1,0:T(8,128)(2,1)}, u32[]{:S(2)}, u32[]{:S(2)}) collective-permute-start(bf16[2048,256]{1,0:T(8,128)(2,1)S(1)} %shard_map.142.w0), channel_id=1, source_target_pairs={{0,1},{1,0},{2,3},{3,2},{4,5},{5,4},{6,7},{7,6},{8,9},{9,8},{10,11... | collective-permute-start | bytes 3145736 | tf_op jit(solution)/shard_map/ppermute | solution.py:381
  48.4 80.1 %collective-permute-start.21 = (bf16[2048,256]{1,0:T(8,128)(2,1)S(1)}, bf16[2048,256]{1,0:T(8,128)(2,1)}, u32[]{:S(2)}, u32[]{:S(2)}) collective-permute-start(bf16[2048,256]{1,0:T(8,128)(2,1)S(1)} %collective-permute-done.20.w2), channel_id=1, source_target_pairs={{0,1},{1,0},{2,3},{3,2},{4,5},{5,4},{6,7},{7,6},{8,9},{9,8},{10,11... | collective-permute-start | bytes 3145736 | tf_op jit(solution)/shard_map/ppermute | solution.py:383
  48.4 3.2 %collective-permute-start.4 = (bf16[64,1024]{1,0:T(8,128)(2,1)S(1)}, bf16[64,1024]{1,0:T(8,128)(2,1)S(1)}, u32[]{:S(2)}, u32[]{:S(2)}) collective-permute-start(bf16[64,1024]{1,0:T(8,128)(2,1)S(1)} %collective-permute-done.3.refs_4_), channel_id=1, source_target_pairs={{0,1},{1,0},{2,3},{3,2},{4,5},{5,4},{6,7},{7,6},{8,9},{9,8},{10,11... | collective-permute-start | bytes 393224 | tf_op jit(solution)/shard_map/ppermute | solution.py:376
  48.9 9.4 %collective-permute-start.5 = (bf16[64,1024]{1,0:T(8,128)(2,1)S(1)}, bf16[64,1024]{1,0:T(8,128)(2,1)S(1)}, u32[]{:S(2)}, u32[]{:S(2)}) collective-permute-start(bf16[64,1024]{1,0:T(8,128)(2,1)S(1)} %collective-permute-done.3.refs_4_), channel_id=1, source_target_pairs={{0,2},{1,3},{2,0},{3,1},{4,6},{5,7},{6,4},{7,5},{8,10},{9,11},{10,... | collective-permute-start | bytes 393224 | tf_op jit(solution)/shard_map/ppermute | solution.py:376
  51.5 12.3 %collective-permute-start.6 = (bf16[64,1024]{1,0:T(8,128)(2,1)S(1)}, bf16[64,1024]{1,0:T(8,128)(2,1)S(1)}, u32[]{:S(2)}, u32[]{:S(2)}) collective-permute-start(bf16[64,1024]{1,0:T(8,128)(2,1)S(1)} %collective-permute-done.3.refs_4_), channel_id=1, source_target_pairs={{0,3},{1,2},{2,1},{3,0},{4,7},{5,6},{6,5},{7,4},{8,11},{9,10},{10,... | collective-permute-start | bytes 393224 | tf_op jit(solution)/shard_map/ppermute | solution.py:376
  51.6 15.7 %collective-permute-start.7 = (bf16[128,1024]{1,0:T(8,128)(2,1)S(1)}, bf16[128,1024]{1,0:T(8,128)(2,1)S(1)}, u32[]{:S(2)}, u32[]{:S(2)}) collective-permute-start(bf16[128,1024]{1,0:T(8,128)(2,1)S(1)} %copy-done.13), channel_id=1, source_target_pairs={{0,4},{1,5},{2,6},{3,7},{4,8},{5,9},{6,10},{7,11},{8,12},{9,13},{1... | collective-permute-start | bytes 786440 | tf_op jit(solution)/shard_map/ppermute | solution.py:365
  58.4 19.1 %collective-permute-start.8 = (bf16[128,1024]{1,0:T(8,128)(2,1)S(1)}, bf16[128,1024]{1,0:T(8,128)(2,1)S(1)}, u32[]{:S(2)}, u32[]{:S(2)}) collective-permute-start(bf16[128,1024]{1,0:T(8,128)(2,1)S(1)} %copy-done.14), channel_id=1, source_target_pairs={{0,4},{1,5},{2,6},{3,7},{4,8},{5,9},{6,10},{7,11},{8,12},{9,13},{1... | collective-permute-start | bytes 786440 | tf_op jit(solution)/shard_map/ppermute | solution.py:367
  63.8 16.2 %collective-permute-start.10 = (bf16[128,1024]{1,0:T(8,128)(2,1)S(1)}, bf16[128,1024]{1,0:T(8,128)(2,1)}, u32[]{:S(2)}, u32[]{:S(2)}) collective-permute-start(bf16[128,1024]{1,0:T(8,128)(2,1)S(1)} %copy-done.14), channel_id=1, source_target_pairs={{0,12},{1,13},{2,14},{3,15},{4,0},{5,1},{6,2},{7,3},{8,4},{9,5},{1... | collective-permute-start | bytes 786440 | tf_op jit(solution)/shard_map/ppermute | solution.py:366
  67.4 22.1 %collective-permute-start.9 = (bf16[128,1024]{1,0:T(8,128)(2,1)S(1)}, bf16[128,1024]{1,0:T(8,128)(2,1)}, u32[]{:S(2)}, u32[]{:S(2)}) collective-permute-start(bf16[128,1024]{1,0:T(8,128)(2,1)S(1)} %copy-done.13), channel_id=1, source_target_pairs={{0,12},{1,13},{2,14},{3,15},{4,0},{5,1},{6,2},{7,3},{8,4},{9,5},{1... | collective-permute-start | bytes 786440 | tf_op jit(solution)/shard_map/ppermute | solution.py:368
  77.5 14.3 %collective-permute-start.11 = (bf16[128,1024]{1,0:T(8,128)(2,1)S(1)}, bf16[128,1024]{1,0:T(8,128)(2,1)}, u32[]{:S(2)}, u32[]{:S(2)}) collective-permute-start(bf16[128,1024]{1,0:T(8,128)(2,1)S(1)} %collective-permute-done.7.refs_10_), channel_id=1, source_target_pairs={{0,4},{1,5},{2,6},{3,7},{4,8},{5,9},{6,10},{7,11},{8,12},{9,13},{1... | collective-permute-start | bytes 786440 | tf_op jit(solution)/shard_map/ppermute | solution.py:369
  80.0 19.3 %collective-permute-start.12 = (bf16[128,1024]{1,0:T(8,128)(2,1)}, bf16[128,1024]{1,0:T(8,128)(2,1)S(1)}, u32[]{:S(2)}, u32[]{:S(2)}) collective-permute-start(bf16[128,1024]{1,0:T(8,128)(2,1)} %collective-permute-done.10.refs_13_), channel_id=1, source_target_pairs={{0,12},{1,13},{2,14},{3,15},{4,0},{5,1},{6,2},{7,3},{8,4},{9,5},{1... | collective-permute-start | bytes 786440 | tf_op jit(solution)/shard_map/ppermute | solution.py:370
  108.5 2.0 collective-permute-start.13
  108.6 6.7 %collective-permute-start.14 = (bf16[64,1024]{1,0:T(8,128)(2,1)}, bf16[64,1024]{1,0:T(8,128)(2,1)S(1)}, u32[]{:S(2)}, u32[]{:S(2)}) collective-permute-start(bf16[64,1024]{1,0:T(8,128)(2,1)} %get-tuple-element.23), channel_id=1, source_target_pairs={{0,2},{1,3},{2,0},{3,1},{4,6},{5,7},{6,4},{7,5},{8,10},{9,11},{10,... | collective-permute-start | bytes 393224 | tf_op jit(solution)/shard_map/ppermute | solution.py:424
  109.9 7.0 %collective-permute-start.15 = (bf16[64,1024]{1,0:T(8,128)(2,1)}, bf16[64,1024]{1,0:T(8,128)(2,1)S(1)}, u32[]{:S(2)}, u32[]{:S(2)}) collective-permute-start(bf16[64,1024]{1,0:T(8,128)(2,1)} %get-tuple-element.24), channel_id=1, source_target_pairs={{0,3},{1,2},{2,1},{3,0},{4,7},{5,6},{6,5},{7,4},{8,11},{9,10},{10,... | collective-permute-start | bytes 393224 | tf_op jit(solution)/shard_map/ppermute | solution.py:424
  118.1 8.0 %collective-permute-start.16 = (bf16[64,1024]{1,0:T(8,128)(2,1)S(1)}, bf16[64,1024]{1,0:T(8,128)(2,1)S(1)}, u32[]{:S(2)}, u32[]{:S(2)}) collective-permute-start(bf16[64,1024]{1,0:T(8,128)(2,1)S(1)} %get-tuple-element.26.h0), channel_id=1, source_target_pairs={{0,8},{1,9},{2,10},{3,11},{4,12},{5,13},{6,14},{7,15},{8,0},{9,1},... | collective-permute-start | bytes 393224 | tf_op jit(solution)/shard_map/ppermute | solution.py:436
  121.4 7.1 %collective-permute-start.17 = (bf16[64,1024]{1,0:T(8,128)(2,1)S(1)}, bf16[64,1024]{1,0:T(8,128)(2,1)S(1)}, u32[]{:S(2)}, u32[]{:S(2)}) collective-permute-start(bf16[64,1024]{1,0:T(8,128)(2,1)S(1)} %get-tuple-element.26.h0), channel_id=1, source_target_pairs={{0,4},{1,5},{2,6},{3,7},{4,8},{5,9},{6,10},{7,11},{8,12},{9,13},{1... | collective-permute-start | bytes 393224 | tf_op jit(solution)/shard_map/ppermute | solution.py:437
  121.4 7.1 %collective-permute-start.18 = (bf16[64,1024]{1,0:T(8,128)(2,1)S(1)}, bf16[64,1024]{1,0:T(8,128)(2,1)S(1)}, u32[]{:S(2)}, u32[]{:S(2)}) collective-permute-start(bf16[64,1024]{1,0:T(8,128)(2,1)S(1)} %get-tuple-element.26.h0), channel_id=1, source_target_pairs={{0,12},{1,13},{2,14},{3,15},{4,0},{5,1},{6,2},{7,3},{8,4},{9,5},{1... | collective-permute-start | bytes 393224 | tf_op jit(solution)/shard_map/ppermute | solution.py:438
  131.6 7.6 %collective-permute-start.22 = (bf16[64,1024]{1,0:T(8,128)(2,1)S(1)}, bf16[64,1024]{1,0:T(8,128)(2,1)S(1)}, u32[]{:S(2)}, u32[]{:S(2)}) collective-permute-start(bf16[64,1024]{1,0:T(8,128)(2,1)S(1)} %get-tuple-element.28), channel_id=1, source_target_pairs={{0,8},{1,9},{2,10},{3,11},{4,12},{5,13},{6,14},{7,15},{8,0},{9,1},... | collective-permute-start | bytes 393224 | tf_op jit(solution)/shard_map/ppermute | solution.py:449
  133.3 7.0 %collective-permute-start.23 = (bf16[64,1024]{1,0:T(8,128)(2,1)S(1)}, bf16[64,1024]{1,0:T(8,128)(2,1)S(1)}, u32[]{:S(2)}, u32[]{:S(2)}) collective-permute-start(bf16[64,1024]{1,0:T(8,128)(2,1)S(1)} %get-tuple-element.29), channel_id=1, source_target_pairs={{0,12},{1,13},{2,14},{3,15},{4,0},{5,1},{6,2},{7,3},{8,4},{9,5},{1... | collective-permute-start | bytes 393224 | tf_op jit(solution)/shard_map/ppermute | solution.py:450
  136.0 6.2 %collective-permute-start.24 = (bf16[64,1024]{1,0:T(8,128)(2,1)S(1)}, bf16[64,1024]{1,0:T(8,128)(2,1)S(1)}, u32[]{:S(2)}, u32[]{:S(2)}) collective-permute-start(bf16[64,1024]{1,0:T(8,128)(2,1)S(1)} %get-tuple-element.30), channel_id=1, source_target_pairs={{0,4},{1,5},{2,6},{3,7},{4,8},{5,9},{6,10},{7,11},{8,12},{9,13},{1... | collective-permute-start | bytes 393224 | tf_op jit(solution)/shard_map/ppermute | solution.py:451
  143.3 14.6 %all-to-all-start.1 = ((f32[16,64,100]{2,1,0:T(8,128)}), f32[16,64,100]{2,1,0:T(8,128)S(1)}, u32[]{:S(2)}, u32[]{:S(2)}) async-start(f32[16,64,100]{2,1,0:T(8,128)} %shard_map.144), calls=%async_computation.1 | async-start | bytes 1048576 | tf_op jit(solution)/shard_map/all_to_all | solution.py:299
  157.9 15.1 %collective-permute-start.25 = (f32[8,100]{1,0:T(8,128)S(1)}, f32[8,100]{1,0:T(8,128)S(1)}, u32[]{:S(2)}, u32[]{:S(2)}) collective-permute-start(f32[8,100]{1,0:T(8,128)S(1)} %get-tuple-element.39), channel_id=1, source_target_pairs={{0,16},{16,32},{32,48},{48,64},{64,80},{80,96},{96,112},{112,128},... | collective-permute-start | bytes 9608 | tf_op jit(solution)/shard_map/ppermute | solution.py:474
  161.7 11.3 %collective-permute-start.26 = (f32[8,100]{1,0:T(8,128)S(1)}, f32[8,100]{1,0:T(8,128)S(1)}, u32[]{:S(2)}, u32[]{:S(2)}) collective-permute-start(f32[8,100]{1,0:T(8,128)S(1)} %get-tuple-element.38), channel_id=1, source_target_pairs={{16,0},{32,16},{48,32},{64,48},{80,64},{96,80},{112,96},{128,112},... | collective-permute-start | bytes 9608 | tf_op jit(solution)/shard_map/ppermute | solution.py:475
  175.5 15.1 %all-to-all-start.2 = ((bf16[16,72,192]{2,1,0:T(8,128)(2,1)}), bf16[16,72,192]{2,1,0:T(8,128)(2,1)S(1)}, u32[]{:S(2)}, u32[]{:S(2)}) async-start(bf16[16,72,192]{2,1,0:T(8,128)(2,1)} %shard_map.146), calls=%async_computation.2 | async-start | bytes 1179648 | tf_op jit(solution)/shard_map/all_to_all | solution.py:299
  (24 other events, 364.1 us)
Sparse Core Ops, SparseCore 0:
  10.0 90.2 all-gather.2
